TPU v7x, 32 devices: a whole 2x2x4 slice. The times are simulated.
32 devices in a mesh: ma: 16 (over z, y, x), ch: 2 (over core).
Axes of the slice: x: 2, y: 2, z: 4, core: 2. Of those that a mesh axis runs over, the one named last changes fastest.
Arguments:
- visibilities: bfloat16 [512, 512, 2, 128], P('ma', 'ch'), may hold values from -6 to 6
- kl_basis: bfloat16 [512, 256, 2, 512], P('ma', 'ch'), may hold values from -0.1875 to 0.1875
- time_flags: int32 [512], P('ma'), may hold values 0 or 1
Outputs:
- kl_modes: bfloat16 [512, 256, 2, 128], P('ma', 'ch')
All inputs are finite; a program needn't handle non-finite values. No bound on the sum of `time_flags` on one device may be relied on, other than what follows from the above.
Results may differ from a plain program's by a relative error of at most 0.006.
Values may be sent and summed in bfloat16 or wider, within the bound.
No kernel may reach another device: no remote copies, remote signals or barrier semaphores. Data moves between devices by JAX's collectives and lax.ppermute only.
A program may use at most 128 MiB of HBM per device.

v0:
```python
import functools
import math

import jax
import jax.numpy as jnp
from jax import lax
from jax.experimental import pallas as pl
from jax.experimental.pallas import tpu as pltpu
from jax.sharding import PartitionSpec as P


H = 128
UNITS = 8
PARTS = (4, 2, 1, 1)
VMEM_BYTES = 24 << 20


def regroup(visibilities, picks, width, group):
    rows, _, two, svd = visibilities.shape
    shapes = [(size, rows, two, svd) for _, _, size in picks]

    def kernel(src, *refs):
        place = lax.rem(lax.axis_index("ma"), group)
        outs, bufs = refs[: len(picks)], refs[len(picks) : 2 * len(picks)]
        load_sem, store_sem = refs[2 * len(picks) :]
        for n, (partner, offset, size) in enumerate(picks):
            start = lax.bitwise_xor(place, partner) * width + offset

            @pl.loop(0, rows)
            def load(m):
                pltpu.make_async_copy(src.at[m, pl.ds(start, size)], bufs[n].at[:, m], load_sem.at[n]).start()

        stores = []
        for n in range(len(picks)):
            pltpu.make_async_copy(bufs[n], bufs[n], load_sem.at[n]).wait()
            stores.append(pltpu.make_async_copy(bufs[n], outs[n], store_sem.at[n]))
            stores[-1].start()
        for copy in stores:
            copy.wait()

    nbytes = 4 * sum(math.prod(shape) for shape in shapes)
    outs = pl.pallas_call(
        kernel,
        out_shape=[jax.ShapeDtypeStruct(shape, visibilities.dtype) for shape in shapes],
        in_specs=[pl.BlockSpec(memory_space=pltpu.HBM)],
        out_specs=[pl.BlockSpec(memory_space=pl.ANY)] * len(picks),
        scratch_shapes=[pltpu.VMEM(shape, visibilities.dtype) for shape in shapes]
        + [pltpu.SemaphoreType.DMA((len(picks),)), pltpu.SemaphoreType.DMA((len(picks),))],
        cost_estimate=pl.CostEstimate(flops=0, bytes_accessed=nbytes, transcendentals=0),
        name="regroup",
    )(visibilities)
    return [out.reshape(out.shape[0], rows * two, svd) for out in outs]


def mixing_matrix(flags, place, rows, group, total):
    def waves(count):
        at = lax.broadcasted_iota(jnp.int32, (count, total), 0)
        t = lax.broadcasted_iota(jnp.int32, (count, total), 1)
        phases = jnp.mod(row_of(at, place, rows, group) * t + (total // 4) * (at % 2), total)
        phases = phases.astype(jnp.float32) * (2.0 * math.pi / total)
        return jnp.cos(phases), jnp.sin(phases)

    outs, ins = 2 * rows * group, 6 * rows * group
    co, so, ci, si = lax.optimization_barrier(waves(outs) + waves(ins))
    kept = flags.astype(jnp.float32)
    dot = functools.partial(
        lax.dot_general, dimension_numbers=(((1,), (1,)), ((), ())), precision=lax.Precision.HIGHEST
    )
    taps = (dot(co * kept, ci) + dot(so * kept, si)) / total
    out_row = row_of(lax.broadcasted_iota(jnp.int32, taps.shape, 0), place, rows, group)
    in_row = row_of(lax.broadcasted_iota(jnp.int32, taps.shape, 1), place, rows, group)
    return jnp.where(jnp.abs(out_row - in_row) <= H, taps, 0.0).astype(jnp.bfloat16)


def row_of(at, place, rows, group):
    row = (at // 2) % rows
    block = lax.bitwise_xor((at // (2 * rows)) % group, place)
    side = at // (2 * rows * group)
    return block * rows + row + jnp.where(side == 1, -H, jnp.where(side == 2, H, 0))


def mix(matrix, firsts, others, offset, unit, size):
    pair_rows, svd = firsts[0].shape[1:]
    group = matrix.shape[0] // pair_rows
    rows = pair_rows // 2
    start = offset // unit

    def kernel(t_ref, *refs):
        ins, outs = refs[:6], refs[6:]
        table = t_ref[...]
        for c in range(0, unit, 2):
            stack = []
            for first, other in zip(ins[:3], ins[3:]):
                stack.append(jnp.concatenate([first[c], first[c + 1]], axis=1))
                for p in range(group - 1):
                    stack.append(jnp.concatenate([other[p, c], other[p, c + 1]], axis=1))
            data = jnp.concatenate(stack, axis=0)
            mixed = jnp.dot(table, data, preferred_element_type=jnp.float32).astype(jnp.bfloat16)
            for r in range(group):
                part = mixed[r * pair_rows : (r + 1) * pair_rows]
                outs[r][:, c] = part[:, :svd].reshape(rows, 2, svd)
                outs[r][:, c + 1] = part[:, svd:].reshape(rows, 2, svd)

    flops = 2 * matrix.size * size * svd
    nbytes = 2 * (matrix.size + 4 * group * size * pair_rows * svd)
    return pl.pallas_call(
        kernel,
        grid=(size // unit,),
        out_shape=[jax.ShapeDtypeStruct((rows, size, 2, svd), jnp.bfloat16)] * group,
        in_specs=[pl.BlockSpec(matrix.shape, lambda i: (0, 0))]
        + [pl.BlockSpec((unit, pair_rows, svd), lambda i: (start + i, 0, 0))] * 3
        + [pl.BlockSpec((group - 1, unit, pair_rows, svd), lambda i: (0, i, 0, 0))] * 3,
        out_specs=[pl.BlockSpec((rows, unit, 2, svd), lambda i: (0, i, 0, 0))] * group,
        compiler_params=pltpu.CompilerParams(vmem_limit_bytes=VMEM_BYTES),
        cost_estimate=pl.CostEstimate(flops=flops, bytes_accessed=nbytes, transcendentals=0),
        name="mix",
    )(matrix, *firsts, *others)


def arrange_basis(kl_basis, chunks, width, group, copies):
    rows, modes, two, chans = kl_basis.shape
    pieces = copies * group
    widths = [2 * pieces * size for _, size in chunks]

    def kernel(kl_ref, *refs):
        outs, picked = refs[: len(chunks)], refs[len(chunks) :]

        @pl.when(pl.program_id(0) == 0)
        def _():
            place = lax.rem(lax.axis_index("ma"), group)
            core = lax.axis_index("ch")
            for n, (offset, size) in enumerate(chunks):
                at = lax.broadcasted_iota(jnp.int32, (1, widths[n]), 1)
                begin = jnp.zeros_like(at)
                for piece in range(pieces):
                    source = lax.rem(core + piece // group, copies)
                    quarter = lax.bitwise_xor(place, piece % group)
                    first = source * group * width + quarter * width + offset - piece * size
                    begin = jnp.where(at >= 2 * piece * size, first, begin)
                hit = begin + (at >> 1) == lax.broadcasted_iota(jnp.int32, (chans, widths[n]), 0)
                for plane in range(2):
                    keep = hit & ((at & 1) == plane)
                    picked[2 * n + plane][...] = jnp.where(keep, 1.0, 0.0).astype(jnp.bfloat16)

        plain = kl_ref[0].reshape(2 * modes, chans)
        r = lax.broadcasted_iota(jnp.int32, (2 * modes, 2 * modes), 0)
        c = lax.broadcasted_iota(jnp.int32, (2 * modes, 2 * modes), 1)
        odd = (r & 1) == 1
        turn = jnp.where(c == jnp.where(odd, r - 1, r + 1), jnp.where(odd, 1.0, -1.0), 0.0).astype(jnp.bfloat16)
        turned = jnp.dot(turn, plain, preferred_element_type=jnp.float32).astype(jnp.bfloat16)
        for n in range(len(widths)):
            value = jnp.dot(plain, picked[2 * n][...], preferred_element_type=jnp.float32)
            value += jnp.dot(turned, picked[2 * n + 1][...], preferred_element_type=jnp.float32)
            outs[n][0] = value.astype(jnp.bfloat16)

    flops = 4 * rows * 2 * modes * chans * sum(widths)
    nbytes = 2 * (kl_basis.size + rows * 2 * modes * sum(widths))
    return pl.pallas_call(
        kernel,
        grid=(rows,),
        out_shape=[jax.ShapeDtypeStruct((rows, 2 * modes, w), jnp.bfloat16) for w in widths],
        in_specs=[pl.BlockSpec((1, modes, two, chans), lambda i: (i, 0, 0, 0))],
        out_specs=[pl.BlockSpec((1, 2 * modes, w), lambda i: (i, 0, 0)) for w in widths],
        scratch_shapes=[pltpu.VMEM((chans, w), jnp.bfloat16) for w in widths for _ in range(2)],
        compiler_params=pltpu.CompilerParams(vmem_limit_bytes=VMEM_BYTES),
        cost_estimate=pl.CostEstimate(flops=flops, bytes_accessed=nbytes, transcendentals=0),
        name="arrange",
    )(kl_basis)


def project(basis, pieces, total, last):
    rows, out_rows, _ = basis.shape
    svd = pieces[0].shape[2]
    step = math.gcd(rows, 4)
    args = [basis] + list(pieces) + ([] if total is None else [total])

    def kernel(*refs):
        out = refs[-1]
        for m in range(step):
            data = jnp.concatenate([ref[m] for ref in refs[1 : 1 + len(pieces)]], axis=0)
            value = jnp.dot(refs[0][m], data, preferred_element_type=jnp.float32)
            if total is not None:
                value += refs[1 + len(pieces)][m]
            out[m] = value.astype(out.dtype)

    def spec(shape):
        return pl.BlockSpec((step,) + shape, lambda i: (i, 0, 0))

    out_shape = jax.ShapeDtypeStruct((rows, out_rows, svd), jnp.bfloat16 if last else jnp.float32)
    nbytes = sum(a.size * a.dtype.itemsize for a in args) + out_shape.size * out_shape.dtype.itemsize
    return pl.pallas_call(
        kernel,
        grid=(rows // step,),
        out_shape=out_shape,
        in_specs=[spec(a.shape[1:]) for a in args],
        out_specs=spec((out_rows, svd)),
        compiler_params=pltpu.CompilerParams(vmem_limit_bytes=VMEM_BYTES),
        cost_estimate=pl.CostEstimate(flops=2 * basis.size * svd, bytes_accessed=nbytes, transcendentals=0),
        name="project",
    )(*args)


def stages(visibilities, kl_basis, time_flags):
    rows, chans, _, svd = visibilities.shape
    modes = kl_basis.shape[1]
    count = lax.axis_size("ma")
    copies = lax.axis_size("ch")
    total = rows * count
    group = H // rows
    width = chans // group
    unit = width // UNITS
    chunks = [(sum(PARTS[:n]) * unit, part * unit) for n, part in enumerate(PARTS)]
    me = lax.axis_index("ma")
    place = lax.rem(me, group).astype(jnp.int32)

    def swap(x, bits):
        return lax.ppermute(x, "ma", [(i, i ^ bits) for i in range(count)])

    def shift(x, by):
        return lax.ppermute(x, "ma", [(i, (i + by * group) % count) for i in range(count)])

    def sides(x):
        up = shift(x, 1)
        down = shift(x, -1)
        return x, up, down

    (own,) = regroup(visibilities, ((0, 0, width),), width, group)
    firsts = sides(own)
    picks = [(p, offset, size) for offset, size in chunks for p in range(1, group)]
    away = regroup(visibilities, picks, width, group)
    others = []
    for n in range(len(chunks)):
        near = []
        for p in range(1, group):
            near.append(swap(away[n * (group - 1) + p - 1], p))
        near = jnp.stack(near, 0)
        others.append(sides(near))

    mine = lax.dynamic_update_slice(jnp.zeros((total,), jnp.int32), time_flags, (me * rows,))
    flags = mine
    for by in range(1, count // group):
        flags = flags + shift(mine, by)
    bits = group // 2
    while bits:
        flags = flags + swap(flags, bits)
        bits //= 2
    matrix = mixing_matrix(flags, place, rows, group, total)
    bases = arrange_basis(kl_basis, chunks, width, group, copies)

    result = None
    for n, (offset, size) in enumerate(chunks):
        mixed = mix(matrix, firsts, others[n], offset, unit, size)
        back = [mixed[0]]
        for p in range(1, group):
            back.append(swap(mixed[p], p))
        joined = jnp.concatenate([piece.reshape(rows, 2 * size, svd) for piece in back], axis=1)
        pieces = [joined]
        for o in range(1, copies):
            pieces.append(lax.ppermute(joined, "ch", [(i, (i - o) % copies) for i in range(copies)]))
        result = project(bases[n], pieces, result, n == len(chunks) - 1)
    return result.reshape(rows, modes, 2, svd)


def solution(mesh):
    return jax.shard_map(
        stages,
        mesh=mesh,
        in_specs=(P("ma", "ch", None, None), P("ma", "ch", None, None), P("ma")),
        out_specs=P("ma", "ch", None, None),
        check_vma=False,
    )
```

profile of v0, /device:TPU:0, one launch (start us, length us, event | category | flops | bytes accessed | tf_op | source)
XLA Modules:
  0.0 310.0 jit_solution(2347835199507459002)
XLA Ops:
  0.8 5.1 %collective-permute-start.2 = (s32[512]{0:T(512)S(1)}, s32[512]{0:T(512)S(1)}, u32[]{:S(2)}, u32[]{:S(2)}) collective-permute-start(s32[512]{0:T(512)S(1)} %dynamic_update_slice.5), channel_id=1, source_target_pairs={{0,24},{2,26},{4,28},{6,30},{8,0},{10,2},{12,4},{14,6},{16,8},{18,... | collective-permute-start | bytes 6152 | tf_op jit(solution)/shard_map/ppermute | solution.py:220
  6.9 5.1 %regroup.3 = (bf16[32,32,2,128]{3,2,1,0:T(2,128)(2,1)}, bf16[32,32,2,128]{3,2,1,0:T(2,128)(2,1)}, bf16[32,32,2,128]{3,2,1,0:T(2,128)(2,1)}, bf16[16,32,2,128]{3,...) custom-call(bf16[32,256,2,128]{3,2,1,0:T(2,128)(2,1)} %src.3), custom_call_target="tpu_custom_call" | custom-call | bytes 6291456 | tf_op jit(solution)/shard_map/regroup/pallas_call | solution.py:42
  15.9 9.5 %fusion.29 = (f32[768,512]{1,0:T(8,128)}, f32[768,512]{1,0:T(8,128)}) fusion(s32[768]{0:T(1024)S(1)} %get-tuple-element.95, s32[768]{0:T(1024)S(1)} %get-tuple-element.96, pred[768]{0:T(1024)(128)(4,1)S(1)} %fusion.52, s32[768]{0:T(1024)S(1)} %get-tuple-element.92, s32[768]{0:T(1024)S(1)} %get-tuple-element.94, pred[768]{0:T(1024)(128)(4,1)S(1)} %get-tuple-element.98, ...), kind=kLoop, calls=%fused_computation.86 | loop fusion | flops 19660800 | bytes 3173380 | tf_op jit(solution)/shard_map/sin | solution.py:61
  29.3 12.2 %collective-permute-done.3 = s32[512]{0:T(512)S(1)} collective-permute-done((s32[512]{0:T(512)S(1)}, s32[512]{0:T(512)S(1)}, u32[]{:S(2)}, u32[]{:S(2)}) %collective-permute-start.3) | collective-permute-done | bytes 2080 | tf_op jit(solution)/shard_map/ppermute | solution.py:217
  46.3 5.9 %collective-permute-done.4 = s32[512]{0:T(512)S(1)} collective-permute-done((s32[512]{0:T(512)S(1)}, s32[512]{0:T(512)S(1)}, u32[]{:S(2)}, u32[]{:S(2)}) %collective-permute-start.4) | collective-permute-done | bytes 2080 | tf_op jit(solution)/shard_map/ppermute | solution.py:217
  52.2 3.1 collective-permute-start.38
  64.9 4.1 %collective-permute-start.6 = (bf16[64,64,128]{2,1,0:T(8,128)(2,1)}, bf16[64,64,128]{2,1,0:T(8,128)(2,1)S(1)}, u32[]{:S(2)}, u32[]{:S(2)}) collective-permute-start(bf16[64,64,128]{2,1,0:T(8,128)(2,1)} %bitcast.44), channel_id=1, source_target_pairs={{0,24},{2,26},{4,28},{6,30},{8,0},{10,2},{12,4},{14,6},{16,8},{18,... | collective-permute-start | bytes 3145736 | tf_op jit(solution)/shard_map/ppermute | solution.py:220
  69.4 3.2 %fusion.47 = (f32[256,512]{1,0:T(8,128)S(1)}, f32[256,512]{1,0:T(8,128)S(1)}) fusion(s32[256]{0:T(256)} %get-tuple-element.87, s32[256]{0:T(256)} %get-tuple-element.88, pred[256]{0:T(512)(128)(4,1)} %compare_and_fusion, s32[256]{0:T(256)S(1)} %get-tuple-element.82, s32[256]{0:T(256)} %get-tuple-element.86, pred[256]{0:T(512)(128)(4,1)} %get-tuple-element.83, ...), kind=kLoop, calls=%fused_computation.110 | loop fusion | flops 6553600 | bytes 1057796 | tf_op jit(solution)/shard_map/sin | solution.py:61
  72.7 5.8 %collective-permute-done.26 = bf16[16,64,128]{2,1,0:T(8,128)(2,1)S(1)} collective-permute-done((bf16[16,64,128]{2,1,0:T(8,128)(2,1)}, bf16[16,64,128]{2,1,0:T(8,128)(2,1)S(1)}, u32[]{:S(2)}, u32[]{:S(2)}) %collective-permute-start.26) | collective-permute-done | bytes 262176 | tf_op jit(solution)/shard_map/ppermute | solution.py:217
  81.7 4.3 %collective-permute-done.27 = bf16[16,64,128]{2,1,0:T(8,128)(2,1)S(1)} collective-permute-done((bf16[16,64,128]{2,1,0:T(8,128)(2,1)}, bf16[16,64,128]{2,1,0:T(8,128)(2,1)S(1)}, u32[]{:S(2)}, u32[]{:S(2)}) %collective-permute-start.27) | collective-permute-done | bytes 262176 | tf_op jit(solution)/shard_map/ppermute | solution.py:217
  85.9 3.8 %collective-permute-start.20 = (bf16[3,8,64,128]{3,2,1,0:T(8,128)(2,1)S(1)}, bf16[3,8,64,128]{3,2,1,0:T(8,128)(2,1)S(1)}, u32[]{:S(2)}, u32[]{:S(2)}) collective-permute-start(bf16[3,8,64,128]{3,2,1,0:T(8,128)(2,1)S(1)} %pad_maximum_fusion.7.refs_3_), channel_id=1, source_target_pairs={{0,24},{2,26},{4,28},{6,30},{8,0},{10,2},{12,4},{14,6},{16,8},{18,... | collective-permute-start | bytes 1179656 | tf_op jit(solution)/shard_map/ppermute | solution.py:220
  92.5 82.8 %collective-permute-done.20.refs_5_ = bf16[3,8,64,128]{3,2,1,0:T(8,128)(2,1)S(1)} collective-permute-done((bf16[3,8,64,128]{3,2,1,0:T(8,128)(2,1)S(1)}, bf16[3,8,64,128]{3,2,1,0:T(8,128)(2,1)S(1)}, u32[]{:S(2)}, u32[]{:S(2)}) %collective-permute-start.20) | collective-permute-done | bytes 393248 | tf_op jit(solution)/shard_map/ppermute | solution.py:220
  176.8 2.8 collective-permute-start.11
  179.6 3.8 %collective-permute-start.29 = (bf16[3,16,64,128]{3,2,1,0:T(8,128)(2,1)S(1)}, bf16[3,16,64,128]{3,2,1,0:T(8,128)(2,1)S(1)}, u32[]{:S(2)}, u32[]{:S(2)}) collective-permute-start(bf16[3,16,64,128]{3,2,1,0:T(8,128)(2,1)S(1)} %pad_maximum_fusion.3.refs_3_), channel_id=1, source_target_pairs={{0,24},{2,26},{4,28},{6,30},{8,0},{10,2},{12,4},{14,6},{16,8},{18,... | collective-permute-start | bytes 2359304 | tf_op jit(solution)/shard_map/ppermute | solution.py:220
  185.2 4.5 %mix.7 = (bf16[32,32,2,128]{3,2,1,0:T(2,128)(2,1)S(1)}, bf16[32,32,2,128]{3,2,1,0:T(2,128)(2,1)S(1)}, bf16[32,32,2,128]{3,2,1,0:T(2,128)(2,1)S(1)}, bf16[32,32,2,128]{3,2,1,0:T(2,128)(2,1)S(1)}) custom-call(bf16[256,768]{1,0:T(8,128)(2,1)S(1)} %fusion.13.t_ref, bf16[64,64,128]{2,1,0:T(8,128)(2,1)S(1)} %bitcast.46, ...), custom_call_target="tpu_custom_call" | custom-call | flops 1610612736 | bytes 8781824 | tf_op jit(solution)/shard_map/mix/pallas_call | solution.py:106
  191.6 6.4 %collective-permute-done.11.refs_5_ = bf16[3,8,64,128]{3,2,1,0:T(8,128)(2,1)S(1)} collective-permute-done((bf16[3,8,64,128]{3,2,1,0:T(8,128)(2,1)S(1)}, bf16[3,8,64,128]{3,2,1,0:T(8,128)(2,1)S(1)}, u32[]{:S(2)}, u32[]{:S(2)}) %collective-permute-start.11) | collective-permute-done | bytes 393248 | tf_op jit(solution)/shard_map/ppermute | solution.py:220
  199.8 6.7 %collective-permute-done.10.refs_4_ = bf16[3,8,64,128]{3,2,1,0:T(8,128)(2,1)S(1)} collective-permute-done((bf16[3,8,64,128]{3,2,1,0:T(8,128)(2,1)S(1)}, bf16[3,8,64,128]{3,2,1,0:T(8,128)(2,1)S(1)}, u32[]{:S(2)}, u32[]{:S(2)}) %collective-permute-start.10) | collective-permute-done | bytes 393248 | tf_op jit(solution)/shard_map/ppermute | solution.py:220
  209.6 11.4 %collective-permute-done.29.refs_5_ = bf16[3,16,64,128]{3,2,1,0:T(8,128)(2,1)S(1)} collective-permute-done((bf16[3,16,64,128]{3,2,1,0:T(8,128)(2,1)S(1)}, bf16[3,16,64,128]{3,2,1,0:T(8,128)(2,1)S(1)}, u32[]{:S(2)}, u32[]{:S(2)}) %collective-permute-start.29) | collective-permute-done | bytes 786464 | tf_op jit(solution)/shard_map/ppermute | solution.py:220
  222.7 14.4 %collective-permute-done.28.refs_4_ = bf16[3,16,64,128]{3,2,1,0:T(8,128)(2,1)S(1)} collective-permute-done((bf16[3,16,64,128]{3,2,1,0:T(8,128)(2,1)S(1)}, bf16[3,16,64,128]{3,2,1,0:T(8,128)(2,1)S(1)}, u32[]{:S(2)}, u32[]{:S(2)}) %collective-permute-start.28) | collective-permute-done | bytes 786464 | tf_op jit(solution)/shard_map/ppermute | solution.py:220
  250.1 11.9 %collective-permute-done.23 = bf16[32,8,2,128]{3,2,1,0:T(2,128)(2,1)S(1)} collective-permute-done((bf16[32,8,2,128]{3,2,1,0:T(2,128)(2,1)S(1)}, bf16[32,8,2,128]{3,2,1,0:T(2,128)(2,1)S(1)}, u32[]{:S(2)}, u32[]{:S(2)}) %collective-permute-start.23) | collective-permute-done | bytes 131104 | tf_op jit(solution)/shard_map/ppermute | solution.py:217
  262.9 3.4 %copy-done.1 = bf16[32,128,2,512]{3,2,1,0:T(2,128)(2,1)S(1)} copy-done((bf16[32,128,2,512]{3,2,1,0:T(2,128)(2,1)S(1)}, bf16[32,128,2,512]{3,2,1,0:T(2,128)(2,1)}, u32[]{:S(2)}) %copy-start.1) | copy-done | bytes 8388632
  266.3 32.1 %arrange.1 = (bf16[32,256,512]{2,1,0:T(8,128)(2,1)S(1)}, bf16[32,256,256]{2,1,0:T(8,128)(2,1)S(1)}, bf16[32,256,128]{2,1,0:T(8,128)(2,1)S(1)}, bf16[32,256,128]{2,1,0:T(8,128)(2,1)S(1)}) custom-call(bf16[32,128,2,512]{3,2,1,0:T(2,128)(2,1)S(1)} %copy-done.1), custom_call_target="tpu_custom_call" | custom-call | flops 17179869184 | bytes 25165824 | tf_op jit(solution)/shard_map/arrange/pallas_call | solution.py:158
  298.4 3.4 %project.4.refs_3_ = f32[32,256,128]{2,1,0:T(8,128)S(1)} custom-call(bf16[32,256,512]{2,1,0:T(8,128)(2,1)S(1)} %get-tuple-element.69.refs_0_, bf16[32,256,128]{2,1,0:T(8,128)(2,1)S(1)} %pad_maximum_fusion.refs_1_, bf16[32,256,128]{2,1,0:T(8,128)(2,1)S(1)} %collective-permute-done.42.refs_2_), custom_call_target="tpu_custom_call" | custom-call | flops 1073741824 | bytes 16777216 | tf_op jit(solution)/shard_map/project/pallas_call | solution.py:191
  306.1 3.9 %project.7 = bf16[32,256,128]{2,1,0:T(8,128)(2,1)} custom-call(bf16[32,256,128]{2,1,0:T(8,128)(2,1)S(1)} %get-tuple-element.41.refs_0_, bf16[32,64,128]{2,1,0:T(8,128)(2,1)S(1)} %pad_maximum_fusion.4.refs_1_, bf16[32,64,128]{2,1,0:T(8,128)(2,1)S(1)} %collective-permute-done.15.refs_2_, f32[32,256,128]{2,1,0:T(8,128)S(1)} %project.6.refs_3_), custom_call_target="tpu_custom_call" | custom-call | flops 268435456 | bytes 9437184 | tf_op jit(solution)/shard_map/project/pallas_call | solution.py:191
  (167 shorter events, 59.8 us)
Async XLA Ops:
  0.8 25.8 %collective-permute-start.2 = (s32[512]{0:T(512)S(1)}, s32[512]{0:T(512)S(1)}, u32[]{:S(2)}, u32[]{:S(2)}) collective-permute-start(s32[512]{0:T(512)S(1)} %dynamic_update_slice.5), channel_id=1, source_target_pairs={{0,24},{2,26},{4,28},{6,30},{8,0},{10,2},{12,4},{14,6},{16,8},{18,... | collective-permute-start | bytes 6152 | tf_op jit(solution)/shard_map/ppermute | solution.py:220
  5.9 22.3 %collective-permute-start.1 = (s32[512]{0:T(512)S(1)}, s32[512]{0:T(512)S(1)}, u32[]{:S(2)}, u32[]{:S(2)}) collective-permute-start(s32[512]{0:T(512)S(1)} %dynamic_update_slice.5), channel_id=1, source_target_pairs={{0,16},{2,18},{4,20},{6,22},{8,24},{10,26},{12,28},{14,30},{16,0},... | collective-permute-start | bytes 6152 | tf_op jit(solution)/shard_map/ppermute | solution.py:220
  5.9 20.1 %collective-permute-start = (s32[512]{0:T(512)S(1)}, s32[512]{0:T(512)S(1)}, u32[]{:S(2)}, u32[]{:S(2)}) collective-permute-start(s32[512]{0:T(512)S(1)} %dynamic_update_slice.5), channel_id=1, source_target_pairs={{0,8},{2,10},{4,12},{6,14},{8,16},{10,18},{12,20},{14,22},{16,24},... | collective-permute-start | bytes 6152 | tf_op jit(solution)/shard_map/ppermute | solution.py:220
  12.1 30.5 %collective-permute-start.34 = (bf16[32,64,128]{2,1,0:T(8,128)(2,1)}, bf16[32,64,128]{2,1,0:T(8,128)(2,1)S(1)}, u32[]{:S(2)}, u32[]{:S(2)}) collective-permute-start(bf16[32,64,128]{2,1,0:T(8,128)(2,1)} %bitcast.76), channel_id=1, source_target_pairs={{0,2},{2,0},{4,6},{6,4},{8,10},{10,8},{12,14},{14,12},{16,18},{18,... | collective-permute-start | bytes 1572872 | tf_op jit(solution)/shard_map/ppermute | solution.py:217
  13.6 30.4 %collective-permute-start.35 = (bf16[32,64,128]{2,1,0:T(8,128)(2,1)}, bf16[32,64,128]{2,1,0:T(8,128)(2,1)S(1)}, u32[]{:S(2)}, u32[]{:S(2)}) collective-permute-start(bf16[32,64,128]{2,1,0:T(8,128)(2,1)} %bitcast.75), channel_id=1, source_target_pairs={{0,4},{2,6},{4,0},{6,2},{8,12},{10,14},{12,8},{14,10},{16,20},{18,... | collective-permute-start | bytes 1572872 | tf_op jit(solution)/shard_map/ppermute | solution.py:217
  26.0 18.6 %collective-permute-start.36 = (bf16[32,64,128]{2,1,0:T(8,128)(2,1)S(1)}, bf16[32,64,128]{2,1,0:T(8,128)(2,1)S(1)}, u32[]{:S(2)}, u32[]{:S(2)}) collective-permute-start(bf16[32,64,128]{2,1,0:T(8,128)(2,1)S(1)} %bitcast.74), channel_id=1, source_target_pairs={{0,6},{2,4},{4,2},{6,0},{8,14},{10,12},{12,10},{14,8},{16,22},{18,... | collective-permute-start | bytes 1572872 | tf_op jit(solution)/shard_map/ppermute | solution.py:217
  26.6 28.7 %collective-permute-start.8 = (bf16[8,64,128]{2,1,0:T(8,128)(2,1)S(1)}, bf16[8,64,128]{2,1,0:T(8,128)(2,1)S(1)}, u32[]{:S(2)}, u32[]{:S(2)}) collective-permute-start(bf16[8,64,128]{2,1,0:T(8,128)(2,1)S(1)} %bitcast.82), channel_id=1, source_target_pairs={{0,4},{2,6},{4,0},{6,2},{8,12},{10,14},{12,8},{14,10},{16,20},{18,... | collective-permute-start | bytes 393224 | tf_op jit(solution)/shard_map/ppermute | solution.py:217
  52.2 127.3 %collective-permute-start.38 = (bf16[3,32,64,128]{3,2,1,0:T(8,128)(2,1)S(1)}, bf16[3,32,64,128]{3,2,1,0:T(8,128)(2,1)S(1)}, u32[]{:S(2)}, u32[]{:S(2)}) collective-permute-start(bf16[3,32,64,128]{3,2,1,0:T(8,128)(2,1)S(1)} %pad_maximum_fusion.1.refs_3_), channel_id=1, source_target_pairs={{0,24},{2,26},{4,28},{6,30},{8,0},{10,2},{12,4},{14,6},{16,8},{18,... | collective-permute-start | bytes 4718600 | tf_op jit(solution)/shard_map/ppermute | solution.py:220
  55.3 128.1 %collective-permute-start.37 = (bf16[3,32,64,128]{3,2,1,0:T(8,128)(2,1)S(1)}, bf16[3,32,64,128]{3,2,1,0:T(8,128)(2,1)}, u32[]{:S(2)}, u32[]{:S(2)}) collective-permute-start(bf16[3,32,64,128]{3,2,1,0:T(8,128)(2,1)S(1)} %pad_maximum_fusion.1.refs_3_), channel_id=1, source_target_pairs={{0,8},{2,10},{4,12},{6,14},{8,16},{10,18},{12,20},{14,22},{16,24},... | collective-permute-start | bytes 4718600 | tf_op jit(solution)/shard_map/ppermute | solution.py:220
  64.9 111.9 %collective-permute-start.6 = (bf16[64,64,128]{2,1,0:T(8,128)(2,1)}, bf16[64,64,128]{2,1,0:T(8,128)(2,1)S(1)}, u32[]{:S(2)}, u32[]{:S(2)}) collective-permute-start(bf16[64,64,128]{2,1,0:T(8,128)(2,1)} %bitcast.44), channel_id=1, source_target_pairs={{0,24},{2,26},{4,28},{6,30},{8,0},{10,2},{12,4},{14,6},{16,8},{18,... | collective-permute-start | bytes 3145736 | tf_op jit(solution)/shard_map/ppermute | solution.py:220
  69.0 110.6 %collective-permute-start.5 = (bf16[64,64,128]{2,1,0:T(8,128)(2,1)}, bf16[64,64,128]{2,1,0:T(8,128)(2,1)S(1)}, u32[]{:S(2)}, u32[]{:S(2)}) collective-permute-start(bf16[64,64,128]{2,1,0:T(8,128)(2,1)} %bitcast.45), channel_id=1, source_target_pairs={{0,8},{2,10},{4,12},{6,14},{8,16},{10,18},{12,20},{14,22},{16,24},... | collective-permute-start | bytes 3145736 | tf_op jit(solution)/shard_map/ppermute | solution.py:220
  85.9 89.4 %collective-permute-start.20 = (bf16[3,8,64,128]{3,2,1,0:T(8,128)(2,1)S(1)}, bf16[3,8,64,128]{3,2,1,0:T(8,128)(2,1)S(1)}, u32[]{:S(2)}, u32[]{:S(2)}) collective-permute-start(bf16[3,8,64,128]{3,2,1,0:T(8,128)(2,1)S(1)} %pad_maximum_fusion.7.refs_3_), channel_id=1, source_target_pairs={{0,24},{2,26},{4,28},{6,30},{8,0},{10,2},{12,4},{14,6},{16,8},{18,... | collective-permute-start | bytes 1179656 | tf_op jit(solution)/shard_map/ppermute | solution.py:220
  176.8 21.2 %collective-permute-start.11 = (bf16[3,8,64,128]{3,2,1,0:T(8,128)(2,1)S(1)}, bf16[3,8,64,128]{3,2,1,0:T(8,128)(2,1)S(1)}, u32[]{:S(2)}, u32[]{:S(2)}) collective-permute-start(bf16[3,8,64,128]{3,2,1,0:T(8,128)(2,1)S(1)} %pad_maximum_fusion.6.refs_3_), channel_id=1, source_target_pairs={{0,24},{2,26},{4,28},{6,30},{8,0},{10,2},{12,4},{14,6},{16,8},{18,... | collective-permute-start | bytes 1179656 | tf_op jit(solution)/shard_map/ppermute | solution.py:220
  179.6 26.9 %collective-permute-start.10 = (bf16[3,8,64,128]{3,2,1,0:T(8,128)(2,1)S(1)}, bf16[3,8,64,128]{3,2,1,0:T(8,128)(2,1)S(1)}, u32[]{:S(2)}, u32[]{:S(2)}) collective-permute-start(bf16[3,8,64,128]{3,2,1,0:T(8,128)(2,1)S(1)} %pad_maximum_fusion.6.refs_3_), channel_id=1, source_target_pairs={{0,8},{2,10},{4,12},{6,14},{8,16},{10,18},{12,20},{14,22},{16,24},... | collective-permute-start | bytes 1179656 | tf_op jit(solution)/shard_map/ppermute | solution.py:220
  179.6 41.3 %collective-permute-start.29 = (bf16[3,16,64,128]{3,2,1,0:T(8,128)(2,1)S(1)}, bf16[3,16,64,128]{3,2,1,0:T(8,128)(2,1)S(1)}, u32[]{:S(2)}, u32[]{:S(2)}) collective-permute-start(bf16[3,16,64,128]{3,2,1,0:T(8,128)(2,1)S(1)} %pad_maximum_fusion.3.refs_3_), channel_id=1, source_target_pairs={{0,24},{2,26},{4,28},{6,30},{8,0},{10,2},{12,4},{14,6},{16,8},{18,... | collective-permute-start | bytes 2359304 | tf_op jit(solution)/shard_map/ppermute | solution.py:220
  183.4 53.7 %collective-permute-start.28 = (bf16[3,16,64,128]{3,2,1,0:T(8,128)(2,1)S(1)}, bf16[3,16,64,128]{3,2,1,0:T(8,128)(2,1)S(1)}, u32[]{:S(2)}, u32[]{:S(2)}) collective-permute-start(bf16[3,16,64,128]{3,2,1,0:T(8,128)(2,1)S(1)} %pad_maximum_fusion.3.refs_3_), channel_id=1, source_target_pairs={{0,8},{2,10},{4,12},{6,14},{8,16},{10,18},{12,20},{14,22},{16,24},... | collective-permute-start | bytes 2359304 | tf_op jit(solution)/shard_map/ppermute | solution.py:220
  189.7 49.8 %collective-permute-start.39 = (bf16[32,32,2,128]{3,2,1,0:T(2,128)(2,1)S(1)}, bf16[32,32,2,128]{3,2,1,0:T(2,128)(2,1)S(1)}, u32[]{:S(2)}, u32[]{:S(2)}) collective-permute-start(bf16[32,32,2,128]{3,2,1,0:T(2,128)(2,1)S(1)} %get-tuple-element.74), channel_id=1, source_target_pairs={{0,2},{2,0},{4,6},{6,4},{8,10},{10,8},{12,14},{14,12},{16,18},{18,... | collective-permute-start | bytes 1572872 | tf_op jit(solution)/shard_map/ppermute | solution.py:217
  198.0 42.1 %collective-permute-start.40 = (bf16[32,32,2,128]{3,2,1,0:T(2,128)(2,1)S(1)}, bf16[32,32,2,128]{3,2,1,0:T(2,128)(2,1)S(1)}, u32[]{:S(2)}, u32[]{:S(2)}) collective-permute-start(bf16[32,32,2,128]{3,2,1,0:T(2,128)(2,1)S(1)} %get-tuple-element.75), channel_id=1, source_target_pairs={{0,4},{2,6},{4,0},{6,2},{8,12},{10,14},{12,8},{14,10},{16,20},{18,... | collective-permute-start | bytes 1572872 | tf_op jit(solution)/shard_map/ppermute | solution.py:217
  206.4 35.2 %collective-permute-start.41 = (bf16[32,32,2,128]{3,2,1,0:T(2,128)(2,1)S(1)}, bf16[32,32,2,128]{3,2,1,0:T(2,128)(2,1)S(1)}, u32[]{:S(2)}, u32[]{:S(2)}) collective-permute-start(bf16[32,32,2,128]{3,2,1,0:T(2,128)(2,1)S(1)} %get-tuple-element.76), channel_id=1, source_target_pairs={{0,6},{2,4},{4,2},{6,0},{8,14},{10,12},{12,10},{14,8},{16,22},{18,... | collective-permute-start | bytes 1572872 | tf_op jit(solution)/shard_map/ppermute | solution.py:217
  220.9 22.3 %collective-permute-start.21 = (bf16[32,8,2,128]{3,2,1,0:T(2,128)(2,1)S(1)}, bf16[32,8,2,128]{3,2,1,0:T(2,128)(2,1)S(1)}, u32[]{:S(2)}, u32[]{:S(2)}) collective-permute-start(bf16[32,8,2,128]{3,2,1,0:T(2,128)(2,1)S(1)} %get-tuple-element.58), channel_id=1, source_target_pairs={{0,2},{2,0},{4,6},{6,4},{8,10},{10,8},{12,14},{14,12},{16,18},{18,... | collective-permute-start | bytes 393224 | tf_op jit(solution)/shard_map/ppermute | solution.py:217
  243.2 55.2 %collective-permute-start.42 = (bf16[32,256,128]{2,1,0:T(8,128)(2,1)S(1)}, bf16[32,256,128]{2,1,0:T(8,128)(2,1)S(1)}, u32[]{:S(2)}, u32[]{:S(2)}) collective-permute-start(bf16[32,256,128]{2,1,0:T(8,128)(2,1)S(1)} %pad_maximum_fusion.refs_1_), channel_id=1, source_target_pairs={{0,1},{1,0},{2,3},{3,2},{4,5},{5,4},{6,7},{7,6},{8,9},{9,8},{10,11... | collective-permute-start | bytes 6291464 | tf_op jit(solution)/shard_map/ppermute | solution.py:259
  262.1 44.0 %collective-permute-start.15 = (bf16[32,64,128]{2,1,0:T(8,128)(2,1)S(1)}, bf16[32,64,128]{2,1,0:T(8,128)(2,1)S(1)}, u32[]{:S(2)}, u32[]{:S(2)}) collective-permute-start(bf16[32,64,128]{2,1,0:T(8,128)(2,1)S(1)} %pad_maximum_fusion.4.refs_1_), channel_id=1, source_target_pairs={{0,1},{1,0},{2,3},{3,2},{4,5},{5,4},{6,7},{7,6},{8,9},{9,8},{10,11... | collective-permute-start | bytes 1572872 | tf_op jit(solution)/shard_map/ppermute | solution.py:259
  262.1 42.1 %collective-permute-start.24 = (bf16[32,64,128]{2,1,0:T(8,128)(2,1)S(1)}, bf16[32,64,128]{2,1,0:T(8,128)(2,1)S(1)}, u32[]{:S(2)}, u32[]{:S(2)}) collective-permute-start(bf16[32,64,128]{2,1,0:T(8,128)(2,1)S(1)} %pad_maximum_fusion.5.refs_1_), channel_id=1, source_target_pairs={{0,1},{1,0},{2,3},{3,2},{4,5},{5,4},{6,7},{7,6},{8,9},{9,8},{10,11... | collective-permute-start | bytes 1572872 | tf_op jit(solution)/shard_map/ppermute | solution.py:259
  262.8 39.0 %collective-permute-start.33 = (bf16[32,128,128]{2,1,0:T(8,128)(2,1)S(1)}, bf16[32,128,128]{2,1,0:T(8,128)(2,1)S(1)}, u32[]{:S(2)}, u32[]{:S(2)}) collective-permute-start(bf16[32,128,128]{2,1,0:T(8,128)(2,1)S(1)} %pad_maximum_fusion.2.refs_1_), channel_id=1, source_target_pairs={{0,1},{1,0},{2,3},{3,2},{4,5},{5,4},{6,7},{7,6},{8,9},{9,8},{10,11... | collective-permute-start | bytes 3145736 | tf_op jit(solution)/shard_map/ppermute | solution.py:259
  (50 other events, 1717.6 us)
where the time goes:
time: 310 us
  waiting for transfers between devices  163 us (53%)
  starting transfers between devices  59.5 us (19%)
  Pallas kernels  58.6 us (19%)
  other arithmetic  19.8 us (6%)
  local copies, waits for them, and re-layouts  4.98 us (2%)
  matrix products  3.16 us (1%)
    ppermute x13, waiting for transfers between devices, shift(): lax.ppermute(x, 'ma', [(i, (i + by * group) % count) for i in range(count)])  122 us
    ppermute x26, waiting for transfers between devices, swap(): return lax.ppermute(x, 'ma', [(i, i ^ bits) for i in range(count)])  41.7 us
    ppermute x26, starting transfers between devices, swap(): return lax.ppermute(x, 'ma', [(i, i ^ bits) for i in range(count)])  33.6 us
    pallas_call x1, Pallas kernels, arrange_basis(): pl.pallas_call(kernel, grid=(rows,), out_shape=[jax.ShapeDtypeStruct((row...  32.1 us
    ppermute x13, starting transfers between devices, shift(): lax.ppermute(x, 'ma', [(i, (i + by * group) % count) for i in range(count)])  25.2 us
    sin x2, other arithmetic, waves(): return (jnp.cos(phases), jnp.sin(phases))  12.7 us
    pallas_call x4, Pallas kernels, project(): pl.pallas_call(kernel, grid=(rows // step,), out_shape=out_shape, in_spec...  11.5 us
    pallas_call x4, Pallas kernels, mix(): pl.pallas_call(kernel, grid=(size // unit,), out_shape=[jax.ShapeDtypeStr...  7.63 us
  transfers between devices with their start and end apart: 43, of which 11 were waited for; matrix products, arithmetic and copies ran while one was open for 7% of the time, Pallas kernels for 18%

commit v1 on v0

--- a/solution.py
+++ b/solution.py
@@ -115,6 +115,38 @@
         cost_estimate=pl.CostEstimate(flops=flops, bytes_accessed=nbytes, transcendentals=0),
         name="mix",
     )(matrix, *firsts, *others)
+
+
+def mix_apart(matrix, first, others):
+    size, pair_rows, svd = first.shape
+    depth = matrix.shape[0]
+    group = depth // pair_rows
+    rows = pair_rows // 2
+    sides = matrix.shape[1] // depth
+
+    def kernel(t_ref, f_ref, o_ref, *outs):
+        for c in range(0, size, 2):
+            stack = [jnp.concatenate([f_ref[c], f_ref[c + 1]], axis=1)]
+            for p in range(group - 1):
+                stack.append(jnp.concatenate([o_ref[p, c], o_ref[p, c + 1]], axis=1))
+            data = jnp.concatenate(stack, axis=0)
+            for side in range(sides):
+                table = t_ref[:, side * depth : (side + 1) * depth]
+                mixed = jnp.dot(table, data, preferred_element_type=jnp.float32).astype(jnp.bfloat16)
+                for r in range(group):
+                    part = mixed[r * pair_rows : (r + 1) * pair_rows]
+                    outs[r][side, :, c] = part[:, :svd].reshape(rows, 2, svd)
+                    outs[r][side, :, c + 1] = part[:, svd:].reshape(rows, 2, svd)
+
+    flops = 2 * matrix.size * size * svd
+    nbytes = 2 * (matrix.size + (1 + sides) * group * size * pair_rows * svd)
+    return pl.pallas_call(
+        kernel,
+        out_shape=[jax.ShapeDtypeStruct((sides, rows, size, 2, svd), jnp.bfloat16)] * group,
+        compiler_params=pltpu.CompilerParams(vmem_limit_bytes=VMEM_BYTES),
+        cost_estimate=pl.CostEstimate(flops=flops, bytes_accessed=nbytes, transcendentals=0),
+        name="mix_apart",
+    )(matrix, first, others)
 
 
 def arrange_basis(kl_basis, chunks, width, group, copies):
@@ -224,9 +256,11 @@
         down = shift(x, -1)
         return x, up, down
 
-    (own,) = regroup(visibilities, ((0, 0, width),), width, group)
+    last = len(chunks) - 1
+    begin, tail = chunks[last]
+    (own,) = regroup(visibilities, ((0, 0, begin),), width, group)
     firsts = sides(own)
-    picks = [(p, offset, size) for offset, size in chunks for p in range(1, group)]
+    picks = [(p, offset, size) for offset, size in chunks for p in range(1, group)] + [(0, begin, tail)]
     away = regroup(visibilities, picks, width, group)
     others = []
     for n in range(len(chunks)):
@@ -234,7 +268,7 @@
         for p in range(1, group):
             near.append(swap(away[n * (group - 1) + p - 1], p))
         near = jnp.stack(near, 0)
-        others.append(sides(near))
+        others.append(sides(near) if n < last else near)
 
     mine = lax.dynamic_update_slice(jnp.zeros((total,), jnp.int32), time_flags, (me * rows,))
     flags = mine
@@ -247,17 +281,31 @@
     matrix = mixing_matrix(flags, place, rows, group, total)
     bases = arrange_basis(kl_basis, chunks, width, group, copies)
 
+    def returned(pieces):
+        back = [pieces[0]]
+        for p in range(1, group):
+            back.append(swap(pieces[p], p))
+        return [piece.reshape(piece.shape[:-3] + (2 * piece.shape[-3], svd)) for piece in back]
+
+    shares = mix_apart(matrix, away[-1], others[last])
+    shares = returned(shares)
+    kept, rise, fall = [jnp.concatenate([share[side] for share in shares], axis=1) for side in range(3)]
+    rise = shift(rise, 1)
+    fall = shift(fall, -1)
+
     result = None
     for n, (offset, size) in enumerate(chunks):
-        mixed = mix(matrix, firsts, others[n], offset, unit, size)
-        back = [mixed[0]]
-        for p in range(1, group):
-            back.append(swap(mixed[p], p))
-        joined = jnp.concatenate([piece.reshape(rows, 2 * size, svd) for piece in back], axis=1)
+        if n < last:
+            mixed = mix(matrix, firsts, others[n], offset, unit, size)
+            back = returned(mixed)
+            joined = jnp.concatenate(back, axis=1)
+        else:
+            wide = [share.astype(jnp.float32) for share in (kept, rise, fall)]
+            joined = (wide[0] + wide[1] + wide[2]).astype(jnp.bfloat16)
         pieces = [joined]
         for o in range(1, copies):
             pieces.append(lax.ppermute(joined, "ch", [(i, (i - o) % copies) for i in range(copies)]))
-        result = project(bases[n], pieces, result, n == len(chunks) - 1)
+        result = project(bases[n], pieces, result, n == last)
     return result.reshape(rows, modes, 2, svd)
 
 

time: 310 us -> 334 us (1.077)
  waiting for transfers between devices: 163 us -> 186 us
  starting transfers between devices: 59.5 us -> 66.4 us
  other arithmetic: 19.8 us -> 13.5 us
    ppermute x26, waiting for transfers between devices: 41.7 us -> 63.2 us  [swap(): return lax.ppermute(x, 'ma', [(i, i ^ bits) for i in range(count)])]
    ppermute x13, starting transfers between devices: 25.2 us -> 34.7 us  [shift(): lax.ppermute(x, 'ma', [(i, (i + by * group) % count) for i in range(count)])]
    pallas_call x4 -> x3, Pallas kernels: 7.63 us -> 5.85 us  [mix(): pl.pallas_call(kernel, grid=(size // unit,), out_shape=[jax.ShapeDtypeStr...]
  transfers between devices with their start and end apart: 43 -> 43, of which waited for: 11 -> 13; matrix products, arithmetic and copies ran while one was open for 7% -> 5% of each run, Pallas kernels for 18% -> 16%
where the time goes in v1:
time: 334 us; the launch traced here: 333 us
  waiting for transfers between devices  186 us (56%)
  starting transfers between devices  66.4 us (20%)
  Pallas kernels  58.3 us (17%)
  other arithmetic  13.5 us (4%)
  local copies, waits for them, and re-layouts  5.33 us (2%)
    ppermute x13, waiting for transfers between devices, shift(): lax.ppermute(x, 'ma', [(i, (i + by * group) % count) for i in range(count)])  123 us
    ppermute x26, waiting for transfers between devices, swap(): return lax.ppermute(x, 'ma', [(i, i ^ bits) for i in range(count)])  63.2 us
    ppermute x13, starting transfers between devices, shift(): lax.ppermute(x, 'ma', [(i, (i + by * group) % count) for i in range(count)])  34.7 us
    pallas_call x1, Pallas kernels, arrange_basis(): pl.pallas_call(kernel, grid=(rows,), out_shape=[jax.ShapeDtypeStruct((row...  32.1 us
    ppermute x26, starting transfers between devices, swap(): return lax.ppermute(x, 'ma', [(i, i ^ bits) for i in range(count)])  31 us
    pallas_call x4, Pallas kernels, project(): pl.pallas_call(kernel, grid=(rows // step,), out_shape=out_shape, in_spec...  11.5 us
    sin x2, other arithmetic, waves(): return (jnp.cos(phases), jnp.sin(phases))  11 us
    pallas_call x2, Pallas kernels, regroup(): pl.pallas_call(kernel, out_shape=[jax.ShapeDtypeStruct(shape, visibilitie...  7.66 us
  transfers between devices with their start and end apart: 43, of which 13 were waited for; matrix products, arithmetic and copies ran while one was open for 5% of the time, Pallas kernels for 16%

profile of v1, /device:TPU:0, one launch (start us, length us, event | category | flops | bytes accessed | tf_op | source)
XLA Modules:
  0.0 333.3 jit_solution(11248443157394307888)
XLA Ops:
  0.8 5.1 %collective-permute-start.2 = (s32[512]{0:T(512)S(1)}, s32[512]{0:T(512)S(1)}, u32[]{:S(2)}, u32[]{:S(2)}) collective-permute-start(s32[512]{0:T(512)S(1)} %dynamic_update_slice.5), channel_id=1, source_target_pairs={{0,24},{2,26},{4,28},{6,30},{8,0},{10,2},{12,4},{14,6},{16,8},{18,... | collective-permute-start | bytes 6152 | tf_op jit(solution)/shard_map/ppermute | solution.py:252
  6.9 5.4 %regroup.2 = (bf16[32,32,2,128]{3,2,1,0:T(2,128)(2,1)}, bf16[32,32,2,128]{3,2,1,0:T(2,128)(2,1)}, bf16[32,32,2,128]{3,2,1,0:T(2,128)(2,1)}, bf16[16,32,2,128]{3,...) custom-call(bf16[32,256,2,128]{3,2,1,0:T(2,128)(2,1)} %src.3), custom_call_target="tpu_custom_call" | custom-call | bytes 6553600 | tf_op jit(solution)/shard_map/regroup/pallas_call | solution.py:42
  14.6 8.6 %fusion.29 = (f32[768,512]{1,0:T(8,128)S(1)}, f32[768,512]{1,0:T(8,128)}) fusion(s32[768]{0:T(1024)S(1)} %get-tuple-element.109, s32[768]{0:T(1024)S(1)} %get-tuple-element.110, pred[768]{0:T(1024)(128)(4,1)S(1)} %fusion.52, s32[768]{0:T(1024)S(1)} %get-tuple-element.106, s32[768]{0:T(1024)S(1)} %get-tuple-element.108, ...), kind=kLoop, calls=%fused_computation.87 | loop fusion | flops 19660800 | bytes 3173380 | tf_op jit(solution)/shard_map/sin | solution.py:61
  27.9 19.2 %collective-permute-done.3 = s32[512]{0:T(512)S(1)} collective-permute-done((s32[512]{0:T(512)S(1)}, s32[512]{0:T(512)S(1)}, u32[]{:S(2)}, u32[]{:S(2)}) %collective-permute-start.3) | collective-permute-done | bytes 2080 | tf_op jit(solution)/shard_map/ppermute | solution.py:249
  55.4 3.5 %collective-permute-done.17 = bf16[8,64,128]{2,1,0:T(8,128)(2,1)S(1)} collective-permute-done((bf16[8,64,128]{2,1,0:T(8,128)(2,1)}, bf16[8,64,128]{2,1,0:T(8,128)(2,1)S(1)}, u32[]{:S(2)}, u32[]{:S(2)}) %collective-permute-start.17) | collective-permute-done | bytes 131104 | tf_op jit(solution)/shard_map/ppermute | solution.py:249
  65.3 3.1 collective-permute-start.20
  71.0 4.7 %collective-permute-start.27 = (bf16[16,64,128]{2,1,0:T(8,128)(2,1)S(1)}, bf16[16,64,128]{2,1,0:T(8,128)(2,1)S(1)}, u32[]{:S(2)}, u32[]{:S(2)}) collective-permute-start(bf16[16,64,128]{2,1,0:T(8,128)(2,1)S(1)} %bitcast.94), channel_id=1, source_target_pairs={{0,6},{2,4},{4,2},{6,0},{8,14},{10,12},{12,10},{14,8},{16,22},{18,... | collective-permute-start | bytes 786440 | tf_op jit(solution)/shard_map/ppermute | solution.py:249
  75.6 3.5 %collective-permute-start.38 = (bf16[3,32,64,128]{3,2,1,0:T(8,128)(2,1)S(1)}, bf16[3,32,64,128]{3,2,1,0:T(8,128)(2,1)S(1)}, u32[]{:S(2)}, u32[]{:S(2)}) collective-permute-start(bf16[3,32,64,128]{3,2,1,0:T(8,128)(2,1)S(1)} %pad_maximum_fusion.1.refs_3_), channel_id=1, source_target_pairs={{0,24},{2,26},{4,28},{6,30},{8,0},{10,2},{12,4},{14,6},{16,8},{18,... | collective-permute-start | bytes 4718600 | tf_op jit(solution)/shard_map/ppermute | solution.py:252
  87.8 102.3 %collective-permute-done.19.refs_4_ = bf16[3,8,64,128]{3,2,1,0:T(8,128)(2,1)S(1)} collective-permute-done((bf16[3,8,64,128]{3,2,1,0:T(8,128)(2,1)S(1)}, bf16[3,8,64,128]{3,2,1,0:T(8,128)(2,1)S(1)}, u32[]{:S(2)}, u32[]{:S(2)}) %collective-permute-start.19) | collective-permute-done | bytes 393248 | tf_op jit(solution)/shard_map/ppermute | solution.py:252
  190.9 10.4 %collective-permute-done.8 = bf16[3,32,8,2,128]{4,3,2,1,0:T(2,128)(2,1)S(1)} collective-permute-done((bf16[3,32,8,2,128]{4,3,2,1,0:T(2,128)(2,1)S(1)}, bf16[3,32,8,2,128]{4,3,2,1,0:T(2,128)(2,1)S(1)}, u32[]{:S(2)}, u32[]{:S(2)}) %collective-permute-start.8) | collective-permute-done | bytes 393248 | tf_op jit(solution)/shard_map/ppermute | solution.py:249
  206.5 3.5 %mix.5 = (bf16[32,32,2,128]{3,2,1,0:T(2,128)(2,1)S(1)}, bf16[32,32,2,128]{3,2,1,0:T(2,128)(2,1)S(1)}, bf16[32,32,2,128]{3,2,1,0:T(2,128)(2,1)S(1)}, bf16[32,32,2,128]{3,2,1,0:T(2,128)(2,1)S(1)}) custom-call(bf16[256,768]{1,0:T(8,128)(2,1)S(1)} %fusion.13.t_ref, bf16[56,64,128]{2,1,0:T(8,128)(2,1)S(1)} %bitcast.56, ...), custom_call_target="tpu_custom_call" | custom-call | flops 1610612736 | bytes 8781824 | tf_op jit(solution)/shard_map/mix/pallas_call | solution.py:106
  210.1 6.5 %collective-permute-done.9 = bf16[3,32,8,2,128]{4,3,2,1,0:T(2,128)(2,1)S(1)} collective-permute-done((bf16[3,32,8,2,128]{4,3,2,1,0:T(2,128)(2,1)S(1)}, bf16[3,32,8,2,128]{4,3,2,1,0:T(2,128)(2,1)S(1)}, u32[]{:S(2)}, u32[]{:S(2)}) %collective-permute-start.9) | collective-permute-done | bytes 393248 | tf_op jit(solution)/shard_map/ppermute | solution.py:249
  218.4 7.5 %collective-permute-start.29 = (bf16[3,16,64,128]{3,2,1,0:T(8,128)(2,1)S(1)}, bf16[3,16,64,128]{3,2,1,0:T(8,128)(2,1)S(1)}, u32[]{:S(2)}, u32[]{:S(2)}) collective-permute-start(bf16[3,16,64,128]{3,2,1,0:T(8,128)(2,1)S(1)} %pad_maximum_fusion.3.refs_3_), channel_id=1, source_target_pairs={{0,24},{2,26},{4,28},{6,30},{8,0},{10,2},{12,4},{14,6},{16,8},{18,... | collective-permute-start | bytes 2359304 | tf_op jit(solution)/shard_map/ppermute | solution.py:252
  227.5 9.5 %collective-permute-done.40 = bf16[32,32,2,128]{3,2,1,0:T(2,128)(2,1)S(1)} collective-permute-done((bf16[32,32,2,128]{3,2,1,0:T(2,128)(2,1)S(1)}, bf16[32,32,2,128]{3,2,1,0:T(2,128)(2,1)S(1)}, u32[]{:S(2)}, u32[]{:S(2)}) %collective-permute-start.40) | collective-permute-done | bytes 524320 | tf_op jit(solution)/shard_map/ppermute | solution.py:249
  237.0 11.0 %collective-permute-start.12 = (bf16[32,64,128]{2,1,0:T(8,128)(2,1)S(1)}, bf16[32,64,128]{2,1,0:T(8,128)(2,1)S(1)}, u32[]{:S(2)}, u32[]{:S(2)}) collective-permute-start(bf16[32,64,128]{2,1,0:T(8,128)(2,1)S(1)} %pad_maximum_fusion.5), channel_id=1, source_target_pairs={{0,24},{2,26},{4,28},{6,30},{8,0},{10,2},{12,4},{14,6},{16,8},{18,... | collective-permute-start | bytes 1572872 | tf_op jit(solution)/shard_map/ppermute | solution.py:252
  249.2 4.7 %collective-permute-done.23 = bf16[32,8,2,128]{3,2,1,0:T(2,128)(2,1)S(1)} collective-permute-done((bf16[32,8,2,128]{3,2,1,0:T(2,128)(2,1)S(1)}, bf16[32,8,2,128]{3,2,1,0:T(2,128)(2,1)S(1)}, u32[]{:S(2)}, u32[]{:S(2)}) %collective-permute-start.23) | collective-permute-done | bytes 131104 | tf_op jit(solution)/shard_map/ppermute | solution.py:249
  254.5 7.3 %collective-permute-done.28.refs_4_ = bf16[3,16,64,128]{3,2,1,0:T(8,128)(2,1)S(1)} collective-permute-done((bf16[3,16,64,128]{3,2,1,0:T(8,128)(2,1)S(1)}, bf16[3,16,64,128]{3,2,1,0:T(8,128)(2,1)S(1)}, u32[]{:S(2)}, u32[]{:S(2)}) %collective-permute-start.28) | collective-permute-done | bytes 786464 | tf_op jit(solution)/shard_map/ppermute | solution.py:252
  264.1 8.9 %collective-permute-done.11 = bf16[32,64,128]{2,1,0:T(8,128)(2,1)S(1)} collective-permute-done((bf16[32,64,128]{2,1,0:T(8,128)(2,1)S(1)}, bf16[32,64,128]{2,1,0:T(8,128)(2,1)S(1)}, u32[]{:S(2)}, u32[]{:S(2)}) %collective-permute-start.11) | collective-permute-done | bytes 524320 | tf_op jit(solution)/shard_map/ppermute | solution.py:252
  274.0 4.5 %collective-permute-done.12 = bf16[32,64,128]{2,1,0:T(8,128)(2,1)S(1)} collective-permute-done((bf16[32,64,128]{2,1,0:T(8,128)(2,1)S(1)}, bf16[32,64,128]{2,1,0:T(8,128)(2,1)S(1)}, u32[]{:S(2)}, u32[]{:S(2)}) %collective-permute-start.12) | collective-permute-done | bytes 524320 | tf_op jit(solution)/shard_map/ppermute | solution.py:252
  279.8 6.2 %collective-permute-done.32 = bf16[32,16,2,128]{3,2,1,0:T(2,128)(2,1)S(1)} collective-permute-done((bf16[32,16,2,128]{3,2,1,0:T(2,128)(2,1)S(1)}, bf16[32,16,2,128]{3,2,1,0:T(2,128)(2,1)S(1)}, u32[]{:S(2)}, u32[]{:S(2)}) %collective-permute-start.32) | collective-permute-done | bytes 262176 | tf_op jit(solution)/shard_map/ppermute | solution.py:249
  286.2 3.4 %copy-done.1 = bf16[32,128,2,512]{3,2,1,0:T(2,128)(2,1)S(1)} copy-done((bf16[32,128,2,512]{3,2,1,0:T(2,128)(2,1)S(1)}, bf16[32,128,2,512]{3,2,1,0:T(2,128)(2,1)}, u32[]{:S(2)}) %copy-start.1) | copy-done | bytes 8388632
  289.6 32.1 %arrange.1 = (bf16[32,256,512]{2,1,0:T(8,128)(2,1)S(1)}, bf16[32,256,256]{2,1,0:T(8,128)(2,1)S(1)}, bf16[32,256,128]{2,1,0:T(8,128)(2,1)S(1)}, bf16[32,256,128]{2,1,0:T(8,128)(2,1)S(1)}) custom-call(bf16[32,128,2,512]{3,2,1,0:T(2,128)(2,1)S(1)} %copy-done.1), custom_call_target="tpu_custom_call" | custom-call | flops 17179869184 | bytes 25165824 | tf_op jit(solution)/shard_map/arrange/pallas_call | solution.py:190
  321.7 3.4 %project.4.refs_3_ = f32[32,256,128]{2,1,0:T(8,128)S(1)} custom-call(bf16[32,256,512]{2,1,0:T(8,128)(2,1)S(1)} %get-tuple-element.71.refs_0_, bf16[32,256,128]{2,1,0:T(8,128)(2,1)S(1)} %pad_maximum_fusion.refs_1_, bf16[32,256,128]{2,1,0:T(8,128)(2,1)S(1)} %collective-permute-done.42.refs_2_), custom_call_target="tpu_custom_call" | custom-call | flops 1073741824 | bytes 16777216 | tf_op jit(solution)/shard_map/project/pallas_call | solution.py:223
  329.3 3.9 %project.7 = bf16[32,256,128]{2,1,0:T(8,128)(2,1)} custom-call(bf16[32,256,128]{2,1,0:T(8,128)(2,1)S(1)} %get-tuple-element.42.refs_0_, bf16[32,64,128]{2,1,0:T(8,128)(2,1)S(1)} %add_convert_fusion.refs_1_, bf16[32,64,128]{2,1,0:T(8,128)(2,1)S(1)} %collective-permute-done.13.refs_2_, f32[32,256,128]{2,1,0:T(8,128)S(1)} %project.6.refs_3_), custom_call_target="tpu_custom_call" | custom-call | flops 268435456 | bytes 9437184 | tf_op jit(solution)/shard_map/project/pallas_call | solution.py:223
  (127 shorter events, 54.7 us)
Async XLA Ops:
  0.8 24.1 %collective-permute-start.2 = (s32[512]{0:T(512)S(1)}, s32[512]{0:T(512)S(1)}, u32[]{:S(2)}, u32[]{:S(2)}) collective-permute-start(s32[512]{0:T(512)S(1)} %dynamic_update_slice.5), channel_id=1, source_target_pairs={{0,24},{2,26},{4,28},{6,30},{8,0},{10,2},{12,4},{14,6},{16,8},{18,... | collective-permute-start | bytes 6152 | tf_op jit(solution)/shard_map/ppermute | solution.py:252
  5.9 20.5 %collective-permute-start.1 = (s32[512]{0:T(512)S(1)}, s32[512]{0:T(512)S(1)}, u32[]{:S(2)}, u32[]{:S(2)}) collective-permute-start(s32[512]{0:T(512)S(1)} %dynamic_update_slice.5), channel_id=1, source_target_pairs={{0,16},{2,18},{4,20},{6,22},{8,24},{10,26},{12,28},{14,30},{16,0},... | collective-permute-start | bytes 6152 | tf_op jit(solution)/shard_map/ppermute | solution.py:252
  12.4 42.5 %collective-permute-start.16 = (bf16[8,64,128]{2,1,0:T(8,128)(2,1)}, bf16[8,64,128]{2,1,0:T(8,128)(2,1)S(1)}, u32[]{:S(2)}, u32[]{:S(2)}) collective-permute-start(bf16[8,64,128]{2,1,0:T(8,128)(2,1)} %bitcast.102), channel_id=1, source_target_pairs={{0,2},{2,0},{4,6},{6,4},{8,10},{10,8},{12,14},{14,12},{16,18},{18,... | collective-permute-start | bytes 393224 | tf_op jit(solution)/shard_map/ppermute | solution.py:249
  13.9 48.3 %collective-permute-start.34 = (bf16[32,64,128]{2,1,0:T(8,128)(2,1)}, bf16[32,64,128]{2,1,0:T(8,128)(2,1)S(1)}, u32[]{:S(2)}, u32[]{:S(2)}) collective-permute-start(bf16[32,64,128]{2,1,0:T(8,128)(2,1)} %bitcast.93), channel_id=1, source_target_pairs={{0,2},{2,0},{4,6},{6,4},{8,10},{10,8},{12,14},{14,12},{16,18},{18,... | collective-permute-start | bytes 1572872 | tf_op jit(solution)/shard_map/ppermute | solution.py:249
  23.2 40.1 %collective-permute-start.35 = (bf16[32,64,128]{2,1,0:T(8,128)(2,1)}, bf16[32,64,128]{2,1,0:T(8,128)(2,1)}, u32[]{:S(2)}, u32[]{:S(2)}) collective-permute-start(bf16[32,64,128]{2,1,0:T(8,128)(2,1)} %bitcast.42), channel_id=1, source_target_pairs={{0,4},{2,6},{4,0},{6,2},{8,12},{10,14},{12,8},{14,10},{16,20},{18,... | collective-permute-start | bytes 1572872 | tf_op jit(solution)/shard_map/ppermute | solution.py:249
  25.0 40.3 %collective-permute-start.36 = (bf16[32,64,128]{2,1,0:T(8,128)(2,1)}, bf16[32,64,128]{2,1,0:T(8,128)(2,1)}, u32[]{:S(2)}, u32[]{:S(2)}) collective-permute-start(bf16[32,64,128]{2,1,0:T(8,128)(2,1)} %bitcast.44), channel_id=1, source_target_pairs={{0,6},{2,4},{4,2},{6,0},{8,14},{10,12},{12,10},{14,8},{16,22},{18,... | collective-permute-start | bytes 1572872 | tf_op jit(solution)/shard_map/ppermute | solution.py:249
  26.4 20.7 %collective-permute-start.3 = (s32[512]{0:T(512)S(1)}, s32[512]{0:T(512)S(1)}, u32[]{:S(2)}, u32[]{:S(2)}) collective-permute-start(s32[512]{0:T(512)S(1)} %add_add_fusion), channel_id=1, source_target_pairs={{0,4},{2,6},{4,0},{6,2},{8,12},{10,14},{12,8},{14,10},{16,20},{18,... | collective-permute-start | bytes 6152 | tf_op jit(solution)/shard_map/ppermute | solution.py:249
  75.6 130.4 %collective-permute-start.38 = (bf16[3,32,64,128]{3,2,1,0:T(8,128)(2,1)S(1)}, bf16[3,32,64,128]{3,2,1,0:T(8,128)(2,1)S(1)}, u32[]{:S(2)}, u32[]{:S(2)}) collective-permute-start(bf16[3,32,64,128]{3,2,1,0:T(8,128)(2,1)S(1)} %pad_maximum_fusion.1.refs_3_), channel_id=1, source_target_pairs={{0,24},{2,26},{4,28},{6,30},{8,0},{10,2},{12,4},{14,6},{16,8},{18,... | collective-permute-start | bytes 4718600 | tf_op jit(solution)/shard_map/ppermute | solution.py:252
  79.2 127.3 %collective-permute-start.37 = (bf16[3,32,64,128]{3,2,1,0:T(8,128)(2,1)S(1)}, bf16[3,32,64,128]{3,2,1,0:T(8,128)(2,1)S(1)}, u32[]{:S(2)}, u32[]{:S(2)}) collective-permute-start(bf16[3,32,64,128]{3,2,1,0:T(8,128)(2,1)S(1)} %pad_maximum_fusion.1.refs_3_), channel_id=1, source_target_pairs={{0,8},{2,10},{4,12},{6,14},{8,16},{10,18},{12,20},{14,22},{16,24},... | collective-permute-start | bytes 4718600 | tf_op jit(solution)/shard_map/ppermute | solution.py:252
  81.5 120.6 %collective-permute-start.15 = (bf16[56,64,128]{2,1,0:T(8,128)(2,1)S(1)}, bf16[56,64,128]{2,1,0:T(8,128)(2,1)S(1)}, u32[]{:S(2)}, u32[]{:S(2)}) collective-permute-start(bf16[56,64,128]{2,1,0:T(8,128)(2,1)S(1)} %bitcast.53), channel_id=1, source_target_pairs={{0,24},{2,26},{4,28},{6,30},{8,0},{10,2},{12,4},{14,6},{16,8},{18,... | collective-permute-start | bytes 2752520 | tf_op jit(solution)/shard_map/ppermute | solution.py:252
  84.6 118.6 %collective-permute-start.14 = (bf16[56,64,128]{2,1,0:T(8,128)(2,1)S(1)}, bf16[56,64,128]{2,1,0:T(8,128)(2,1)S(1)}, u32[]{:S(2)}, u32[]{:S(2)}) collective-permute-start(bf16[56,64,128]{2,1,0:T(8,128)(2,1)S(1)} %bitcast.54), channel_id=1, source_target_pairs={{0,8},{2,10},{4,12},{6,14},{8,16},{10,18},{12,20},{14,22},{16,24},... | collective-permute-start | bytes 2752520 | tf_op jit(solution)/shard_map/ppermute | solution.py:252
  84.6 105.4 %collective-permute-start.19 = (bf16[3,8,64,128]{3,2,1,0:T(8,128)(2,1)S(1)}, bf16[3,8,64,128]{3,2,1,0:T(8,128)(2,1)S(1)}, u32[]{:S(2)}, u32[]{:S(2)}) collective-permute-start(bf16[3,8,64,128]{3,2,1,0:T(8,128)(2,1)S(1)} %pad_maximum_fusion.8.refs_3_), channel_id=1, source_target_pairs={{0,8},{2,10},{4,12},{6,14},{8,16},{10,18},{12,20},{14,22},{16,24},... | collective-permute-start | bytes 1179656 | tf_op jit(solution)/shard_map/ppermute | solution.py:252
  203.9 22.1 %collective-permute-start.21 = (bf16[32,8,2,128]{3,2,1,0:T(2,128)(2,1)S(1)}, bf16[32,8,2,128]{3,2,1,0:T(2,128)(2,1)S(1)}, u32[]{:S(2)}, u32[]{:S(2)}) collective-permute-start(bf16[32,8,2,128]{3,2,1,0:T(2,128)(2,1)S(1)} %get-tuple-element.60), channel_id=1, source_target_pairs={{0,2},{2,0},{4,6},{6,4},{8,10},{10,8},{12,14},{14,12},{16,18},{18,... | collective-permute-start | bytes 393224 | tf_op jit(solution)/shard_map/ppermute | solution.py:249
  206.0 19.9 %collective-permute-start.22 = (bf16[32,8,2,128]{3,2,1,0:T(2,128)(2,1)S(1)}, bf16[32,8,2,128]{3,2,1,0:T(2,128)(2,1)S(1)}, u32[]{:S(2)}, u32[]{:S(2)}) collective-permute-start(bf16[32,8,2,128]{3,2,1,0:T(2,128)(2,1)S(1)} %get-tuple-element.61), channel_id=1, source_target_pairs={{0,4},{2,6},{4,0},{6,2},{8,12},{10,14},{12,8},{14,10},{16,20},{18,... | collective-permute-start | bytes 393224 | tf_op jit(solution)/shard_map/ppermute | solution.py:249
  216.6 20.4 %collective-permute-start.40 = (bf16[32,32,2,128]{3,2,1,0:T(2,128)(2,1)S(1)}, bf16[32,32,2,128]{3,2,1,0:T(2,128)(2,1)S(1)}, u32[]{:S(2)}, u32[]{:S(2)}) collective-permute-start(bf16[32,32,2,128]{3,2,1,0:T(2,128)(2,1)S(1)} %get-tuple-element.77), channel_id=1, source_target_pairs={{0,4},{2,6},{4,0},{6,2},{8,12},{10,14},{12,8},{14,10},{16,20},{18,... | collective-permute-start | bytes 1572872 | tf_op jit(solution)/shard_map/ppermute | solution.py:249
  218.4 35.6 %collective-permute-start.29 = (bf16[3,16,64,128]{3,2,1,0:T(8,128)(2,1)S(1)}, bf16[3,16,64,128]{3,2,1,0:T(8,128)(2,1)S(1)}, u32[]{:S(2)}, u32[]{:S(2)}) collective-permute-start(bf16[3,16,64,128]{3,2,1,0:T(8,128)(2,1)S(1)} %pad_maximum_fusion.3.refs_3_), channel_id=1, source_target_pairs={{0,24},{2,26},{4,28},{6,30},{8,0},{10,2},{12,4},{14,6},{16,8},{18,... | collective-permute-start | bytes 2359304 | tf_op jit(solution)/shard_map/ppermute | solution.py:252
  225.9 35.9 %collective-permute-start.28 = (bf16[3,16,64,128]{3,2,1,0:T(8,128)(2,1)S(1)}, bf16[3,16,64,128]{3,2,1,0:T(8,128)(2,1)S(1)}, u32[]{:S(2)}, u32[]{:S(2)}) collective-permute-start(bf16[3,16,64,128]{3,2,1,0:T(8,128)(2,1)S(1)} %pad_maximum_fusion.3.refs_3_), channel_id=1, source_target_pairs={{0,8},{2,10},{4,12},{6,14},{8,16},{10,18},{12,20},{14,22},{16,24},... | collective-permute-start | bytes 2359304 | tf_op jit(solution)/shard_map/ppermute | solution.py:252
  225.9 22.1 %collective-permute-start.41 = (bf16[32,32,2,128]{3,2,1,0:T(2,128)(2,1)S(1)}, bf16[32,32,2,128]{3,2,1,0:T(2,128)(2,1)S(1)}, u32[]{:S(2)}, u32[]{:S(2)}) collective-permute-start(bf16[32,32,2,128]{3,2,1,0:T(2,128)(2,1)S(1)} %get-tuple-element.78), channel_id=1, source_target_pairs={{0,6},{2,4},{4,2},{6,0},{8,14},{10,12},{12,10},{14,8},{16,22},{18,... | collective-permute-start | bytes 1572872 | tf_op jit(solution)/shard_map/ppermute | solution.py:249
  227.3 45.7 %collective-permute-start.11 = (bf16[32,64,128]{2,1,0:T(8,128)(2,1)S(1)}, bf16[32,64,128]{2,1,0:T(8,128)(2,1)S(1)}, u32[]{:S(2)}, u32[]{:S(2)}) collective-permute-start(bf16[32,64,128]{2,1,0:T(8,128)(2,1)S(1)} %pad_maximum_fusion.4), channel_id=1, source_target_pairs={{0,8},{2,10},{4,12},{6,14},{8,16},{10,18},{12,20},{14,22},{16,24},... | collective-permute-start | bytes 1572872 | tf_op jit(solution)/shard_map/ppermute | solution.py:252
  237.0 41.5 %collective-permute-start.12 = (bf16[32,64,128]{2,1,0:T(8,128)(2,1)S(1)}, bf16[32,64,128]{2,1,0:T(8,128)(2,1)S(1)}, u32[]{:S(2)}, u32[]{:S(2)}) collective-permute-start(bf16[32,64,128]{2,1,0:T(8,128)(2,1)S(1)} %pad_maximum_fusion.5), channel_id=1, source_target_pairs={{0,24},{2,26},{4,28},{6,30},{8,0},{10,2},{12,4},{14,6},{16,8},{18,... | collective-permute-start | bytes 1572872 | tf_op jit(solution)/shard_map/ppermute | solution.py:252
  253.9 67.8 %collective-permute-start.42 = (bf16[32,256,128]{2,1,0:T(8,128)(2,1)S(1)}, bf16[32,256,128]{2,1,0:T(8,128)(2,1)S(1)}, u32[]{:S(2)}, u32[]{:S(2)}) collective-permute-start(bf16[32,256,128]{2,1,0:T(8,128)(2,1)S(1)} %pad_maximum_fusion.refs_1_), channel_id=1, source_target_pairs={{0,1},{1,0},{2,3},{3,2},{4,5},{5,4},{6,7},{7,6},{8,9},{9,8},{10,11... | collective-permute-start | bytes 6291464 | tf_op jit(solution)/shard_map/ppermute | solution.py:307
  254.0 73.5 %collective-permute-start.24 = (bf16[32,64,128]{2,1,0:T(8,128)(2,1)S(1)}, bf16[32,64,128]{2,1,0:T(8,128)(2,1)S(1)}, u32[]{:S(2)}, u32[]{:S(2)}) collective-permute-start(bf16[32,64,128]{2,1,0:T(8,128)(2,1)S(1)} %pad_maximum_fusion.6.refs_1_), channel_id=1, source_target_pairs={{0,1},{1,0},{2,3},{3,2},{4,5},{5,4},{6,7},{7,6},{8,9},{9,8},{10,11... | collective-permute-start | bytes 1572872 | tf_op jit(solution)/shard_map/ppermute | solution.py:307
  279.7 49.7 %collective-permute-start.13 = (bf16[32,64,128]{2,1,0:T(8,128)(2,1)S(1)}, bf16[32,64,128]{2,1,0:T(8,128)(2,1)S(1)}, u32[]{:S(2)}, u32[]{:S(2)}) collective-permute-start(bf16[32,64,128]{2,1,0:T(8,128)(2,1)S(1)} %add_convert_fusion.refs_1_), channel_id=1, source_target_pairs={{0,1},{1,0},{2,3},{3,2},{4,5},{5,4},{6,7},{7,6},{8,9},{9,8},{10,11... | collective-permute-start | bytes 1572872 | tf_op jit(solution)/shard_map/ppermute | solution.py:307
  286.1 39.0 %collective-permute-start.33 = (bf16[32,128,128]{2,1,0:T(8,128)(2,1)S(1)}, bf16[32,128,128]{2,1,0:T(8,128)(2,1)S(1)}, u32[]{:S(2)}, u32[]{:S(2)}) collective-permute-start(bf16[32,128,128]{2,1,0:T(8,128)(2,1)S(1)} %pad_maximum_fusion.2.refs_1_), channel_id=1, source_target_pairs={{0,1},{1,0},{2,3},{3,2},{4,5},{5,4},{6,7},{7,6},{8,9},{9,8},{10,11... | collective-permute-start | bytes 3145736 | tf_op jit(solution)/shard_map/ppermute | solution.py:307
  (27 other events, 288.0 us)

commit v2 on v1

--- a/solution.py
+++ b/solution.py
@@ -50,6 +50,30 @@
         name="regroup",
     )(visibilities)
     return [out.reshape(out.shape[0], rows * two, svd) for out in outs]
+
+
+def regroup_own(visibilities, width, size, group):
+    rows, _, two, svd = visibilities.shape
+    shape = (size, rows, two, svd)
+
+    def kernel(src, out, sem):
+        start = lax.rem(lax.axis_index("ma"), group) * width
+
+        @pl.loop(0, rows)
+        def load(m):
+            pltpu.make_async_copy(src.at[m, pl.ds(start, size)], out.at[:, m], sem).start()
+
+        pltpu.make_async_copy(out, out, sem).wait()
+
+    out = pl.pallas_call(
+        kernel,
+        out_shape=jax.ShapeDtypeStruct(shape, visibilities.dtype),
+        in_specs=[pl.BlockSpec(memory_space=pltpu.HBM)],
+        scratch_shapes=[pltpu.SemaphoreType.DMA],
+        cost_estimate=pl.CostEstimate(flops=0, bytes_accessed=4 * math.prod(shape), transcendentals=0),
+        name="regroup_own",
+    )(visibilities)
+    return out.reshape(size, rows * two, svd)
 
 
 def mixing_matrix(flags, place, rows, group, total):
@@ -200,7 +224,7 @@
     )(kl_basis)
 
 
-def project(basis, pieces, total, last):
+def project(basis, pieces, total):
     rows, out_rows, _ = basis.shape
     svd = pieces[0].shape[2]
     step = math.gcd(rows, 4)
@@ -218,7 +242,7 @@
     def spec(shape):
         return pl.BlockSpec((step,) + shape, lambda i: (i, 0, 0))
 
-    out_shape = jax.ShapeDtypeStruct((rows, out_rows, svd), jnp.bfloat16 if last else jnp.float32)
+    out_shape = jax.ShapeDtypeStruct((rows, out_rows, svd), jnp.float32)
     nbytes = sum(a.size * a.dtype.itemsize for a in args) + out_shape.size * out_shape.dtype.itemsize
     return pl.pallas_call(
         kernel,
@@ -229,6 +253,47 @@
         compiler_params=pltpu.CompilerParams(vmem_limit_bytes=VMEM_BYTES),
         cost_estimate=pl.CostEstimate(flops=2 * basis.size * svd, bytes_accessed=nbytes, transcendentals=0),
         name="project",
+    )(*args)
+
+
+def project_last(basis, pieces, total):
+    rows, out_rows, width = basis.shape
+    svd = pieces[0].shape[2]
+    block = math.gcd(rows, 4)
+
+    def kernel(a_ref, *refs):
+        data_refs, t_ref, out, buf, sem = refs[: len(pieces)], *refs[len(pieces) :]
+        empty = jnp.zeros((width, svd), jnp.bfloat16)
+
+        @pl.loop(0, rows // block)
+        def step(n):
+            for m in range(0, block, 2):
+                at = n * block + m
+                left = jnp.concatenate([a_ref[at], a_ref[at + 1]], axis=1)
+                one = jnp.concatenate([ref[at] for ref in data_refs], axis=0)
+                two = jnp.concatenate([ref[at + 1] for ref in data_refs], axis=0)
+                right = jnp.concatenate(
+                    [jnp.concatenate([one, empty], axis=1), jnp.concatenate([empty, two], axis=1)], axis=0
+                )
+                value = jnp.dot(left, right, preferred_element_type=jnp.float32)
+                buf[at] = (value[:, :svd] + t_ref[at]).astype(buf.dtype)
+                buf[at + 1] = (value[:, svd:] + t_ref[at + 1]).astype(buf.dtype)
+            span = pl.ds(n * block, block)
+            pltpu.make_async_copy(buf.at[span], out.at[span], sem).start()
+
+        pltpu.make_async_copy(buf, out, sem).wait()
+
+    args = [basis, *pieces, total]
+    out_shape = jax.ShapeDtypeStruct((rows, out_rows, svd), jnp.bfloat16)
+    nbytes = sum(a.size * a.dtype.itemsize for a in args) + out_shape.size * 2
+    return pl.pallas_call(
+        kernel,
+        out_shape=out_shape,
+        out_specs=pl.BlockSpec(memory_space=pl.ANY),
+        scratch_shapes=[pltpu.VMEM(out_shape.shape, out_shape.dtype), pltpu.SemaphoreType.DMA],
+        compiler_params=pltpu.CompilerParams(vmem_limit_bytes=VMEM_BYTES),
+        cost_estimate=pl.CostEstimate(flops=2 * basis.size * svd, bytes_accessed=nbytes, transcendentals=0),
+        name="project_last",
     )(*args)
 
 
@@ -258,7 +323,7 @@
 
     last = len(chunks) - 1
     begin, tail = chunks[last]
-    (own,) = regroup(visibilities, ((0, 0, begin),), width, group)
+    own = regroup_own(visibilities, width, begin, group)
     firsts = sides(own)
     picks = [(p, offset, size) for offset, size in chunks for p in range(1, group)] + [(0, begin, tail)]
     away = regroup(visibilities, picks, width, group)
@@ -305,7 +370,7 @@
         pieces = [joined]
         for o in range(1, copies):
             pieces.append(lax.ppermute(joined, "ch", [(i, (i - o) % copies) for i in range(copies)]))
-        result = project(bases[n], pieces, result, n == last)
+        result = (project_last if n == last else project)(bases[n], pieces, result)
     return result.reshape(rows, modes, 2, svd)
 
 

time: 334 us -> 333 us (level)
    pallas_call x0 -> x2, Pallas kernels: none -> 4.78 us  [the longest x1 2.57 us: project_last(): pl.pallas_call(kernel, out_shape=out_shape, out_specs=pl.BlockSpec(memory...]
    pallas_call x4 -> x3, Pallas kernels: 11.5 us -> 7.61 us  [project(): pl.pallas_call(kernel, grid=(rows // step,), out_shape=out_shape, in_spec...]
    pallas_call x2 -> x1, Pallas kernels: 7.66 us -> 5.44 us  [regroup(): pl.pallas_call(kernel, out_shape=[jax.ShapeDtypeStruct(shape, visibilitie...]
where the time goes in v2:
time: 333 us; the launch traced here: 332 us
  waiting for transfers between devices  186 us (56%)
  starting transfers between devices  66.4 us (20%)
  Pallas kernels  56.9 us (17%)
  other arithmetic  13.5 us (4%)
  local copies, waits for them, and re-layouts  5.33 us (2%)
    ppermute x13, waiting for transfers between devices, shift(): lax.ppermute(x, 'ma', [(i, (i + by * group) % count) for i in range(count)])  123 us
    ppermute x26, waiting for transfers between devices, swap(): return lax.ppermute(x, 'ma', [(i, i ^ bits) for i in range(count)])  63.2 us
    ppermute x13, starting transfers between devices, shift(): lax.ppermute(x, 'ma', [(i, (i + by * group) % count) for i in range(count)])  34.7 us
    pallas_call x1, Pallas kernels, arrange_basis(): pl.pallas_call(kernel, grid=(rows,), out_shape=[jax.ShapeDtypeStruct((row...  32.1 us
    ppermute x26, starting transfers between devices, swap(): return lax.ppermute(x, 'ma', [(i, i ^ bits) for i in range(count)])  31 us
    sin x2, other arithmetic, waves(): return (jnp.cos(phases), jnp.sin(phases))  11 us
    pallas_call x3, Pallas kernels, project(): pl.pallas_call(kernel, grid=(rows // step,), out_shape=out_shape, in_spec...  7.61 us
  transfers between devices with their start and end apart: 43, of which 13 were waited for; matrix products, arithmetic and copies ran while one was open for 5% of the time, Pallas kernels for 16%

profile of v2, /device:TPU:0, one launch (start us, length us, event | category | flops | bytes accessed | tf_op | source)
XLA Modules:
  0.0 332.1 jit_solution(8570678090336852862)
XLA Ops:
  0.8 5.1 %collective-permute-start.2 = (s32[512]{0:T(512)S(1)}, s32[512]{0:T(512)S(1)}, u32[]{:S(2)}, u32[]{:S(2)}) collective-permute-start(s32[512]{0:T(512)S(1)} %dynamic_update_slice.5), channel_id=1, source_target_pairs={{0,24},{2,26},{4,28},{6,30},{8,0},{10,2},{12,4},{14,6},{16,8},{18,... | collective-permute-start | bytes 6152 | tf_op jit(solution)/shard_map/ppermute | solution.py:317
  6.9 5.4 %regroup.1 = (bf16[32,32,2,128]{3,2,1,0:T(2,128)(2,1)}, bf16[32,32,2,128]{3,2,1,0:T(2,128)(2,1)}, bf16[32,32,2,128]{3,2,1,0:T(2,128)(2,1)}, bf16[16,32,2,128]{3,...) custom-call(bf16[32,256,2,128]{3,2,1,0:T(2,128)(2,1)} %src.3), custom_call_target="tpu_custom_call" | custom-call | bytes 6553600 | tf_op jit(solution)/shard_map/regroup/pallas_call | solution.py:42
  14.6 8.6 %fusion.29 = (f32[768,512]{1,0:T(8,128)S(1)}, f32[768,512]{1,0:T(8,128)}) fusion(s32[768]{0:T(1024)S(1)} %get-tuple-element.109, s32[768]{0:T(1024)S(1)} %get-tuple-element.110, pred[768]{0:T(1024)(128)(4,1)S(1)} %fusion.52, s32[768]{0:T(1024)S(1)} %get-tuple-element.106, s32[768]{0:T(1024)S(1)} %get-tuple-element.108, ...), kind=kLoop, calls=%fused_computation.87 | loop fusion | flops 19660800 | bytes 3173380 | tf_op jit(solution)/shard_map/sin | solution.py:85
  27.9 19.2 %collective-permute-done.3 = s32[512]{0:T(512)S(1)} collective-permute-done((s32[512]{0:T(512)S(1)}, s32[512]{0:T(512)S(1)}, u32[]{:S(2)}, u32[]{:S(2)}) %collective-permute-start.3) | collective-permute-done | bytes 2080 | tf_op jit(solution)/shard_map/ppermute | solution.py:314
  55.4 3.5 %collective-permute-done.17 = bf16[8,64,128]{2,1,0:T(8,128)(2,1)S(1)} collective-permute-done((bf16[8,64,128]{2,1,0:T(8,128)(2,1)}, bf16[8,64,128]{2,1,0:T(8,128)(2,1)S(1)}, u32[]{:S(2)}, u32[]{:S(2)}) %collective-permute-start.17) | collective-permute-done | bytes 131104 | tf_op jit(solution)/shard_map/ppermute | solution.py:314
  65.3 3.1 collective-permute-start.20
  70.9 4.7 %collective-permute-start.27 = (bf16[16,64,128]{2,1,0:T(8,128)(2,1)S(1)}, bf16[16,64,128]{2,1,0:T(8,128)(2,1)S(1)}, u32[]{:S(2)}, u32[]{:S(2)}) collective-permute-start(bf16[16,64,128]{2,1,0:T(8,128)(2,1)S(1)} %bitcast.94), channel_id=1, source_target_pairs={{0,6},{2,4},{4,2},{6,0},{8,14},{10,12},{12,10},{14,8},{16,22},{18,... | collective-permute-start | bytes 786440 | tf_op jit(solution)/shard_map/ppermute | solution.py:314
  75.6 3.5 %collective-permute-start.38 = (bf16[3,32,64,128]{3,2,1,0:T(8,128)(2,1)S(1)}, bf16[3,32,64,128]{3,2,1,0:T(8,128)(2,1)S(1)}, u32[]{:S(2)}, u32[]{:S(2)}) collective-permute-start(bf16[3,32,64,128]{3,2,1,0:T(8,128)(2,1)S(1)} %pad_maximum_fusion.1.refs_3_), channel_id=1, source_target_pairs={{0,24},{2,26},{4,28},{6,30},{8,0},{10,2},{12,4},{14,6},{16,8},{18,... | collective-permute-start | bytes 4718600 | tf_op jit(solution)/shard_map/ppermute | solution.py:317
  81.5 3.1 collective-permute-start.15
  87.8 102.3 %collective-permute-done.19.refs_4_ = bf16[3,8,64,128]{3,2,1,0:T(8,128)(2,1)S(1)} collective-permute-done((bf16[3,8,64,128]{3,2,1,0:T(8,128)(2,1)S(1)}, bf16[3,8,64,128]{3,2,1,0:T(8,128)(2,1)S(1)}, u32[]{:S(2)}, u32[]{:S(2)}) %collective-permute-start.19) | collective-permute-done | bytes 393248 | tf_op jit(solution)/shard_map/ppermute | solution.py:317
  190.9 10.4 %collective-permute-done.8 = bf16[3,32,8,2,128]{4,3,2,1,0:T(2,128)(2,1)S(1)} collective-permute-done((bf16[3,32,8,2,128]{4,3,2,1,0:T(2,128)(2,1)S(1)}, bf16[3,32,8,2,128]{4,3,2,1,0:T(2,128)(2,1)S(1)}, u32[]{:S(2)}, u32[]{:S(2)}) %collective-permute-start.8) | collective-permute-done | bytes 393248 | tf_op jit(solution)/shard_map/ppermute | solution.py:314
  206.5 3.5 %mix.5 = (bf16[32,32,2,128]{3,2,1,0:T(2,128)(2,1)S(1)}, bf16[32,32,2,128]{3,2,1,0:T(2,128)(2,1)S(1)}, bf16[32,32,2,128]{3,2,1,0:T(2,128)(2,1)S(1)}, bf16[32,32,2,128]{3,2,1,0:T(2,128)(2,1)S(1)}) custom-call(bf16[256,768]{1,0:T(8,128)(2,1)S(1)} %fusion.13.t_ref, bf16[56,64,128]{2,1,0:T(8,128)(2,1)S(1)} %bitcast.56, ...), custom_call_target="tpu_custom_call" | custom-call | flops 1610612736 | bytes 8781824 | tf_op jit(solution)/shard_map/mix/pallas_call | solution.py:130
  210.1 6.5 %collective-permute-done.9 = bf16[3,32,8,2,128]{4,3,2,1,0:T(2,128)(2,1)S(1)} collective-permute-done((bf16[3,32,8,2,128]{4,3,2,1,0:T(2,128)(2,1)S(1)}, bf16[3,32,8,2,128]{4,3,2,1,0:T(2,128)(2,1)S(1)}, u32[]{:S(2)}, u32[]{:S(2)}) %collective-permute-start.9) | collective-permute-done | bytes 393248 | tf_op jit(solution)/shard_map/ppermute | solution.py:314
  218.4 7.5 %collective-permute-start.29 = (bf16[3,16,64,128]{3,2,1,0:T(8,128)(2,1)S(1)}, bf16[3,16,64,128]{3,2,1,0:T(8,128)(2,1)S(1)}, u32[]{:S(2)}, u32[]{:S(2)}) collective-permute-start(bf16[3,16,64,128]{3,2,1,0:T(8,128)(2,1)S(1)} %pad_maximum_fusion.3.refs_3_), channel_id=1, source_target_pairs={{0,24},{2,26},{4,28},{6,30},{8,0},{10,2},{12,4},{14,6},{16,8},{18,... | collective-permute-start | bytes 2359304 | tf_op jit(solution)/shard_map/ppermute | solution.py:317
  227.5 9.5 %collective-permute-done.40 = bf16[32,32,2,128]{3,2,1,0:T(2,128)(2,1)S(1)} collective-permute-done((bf16[32,32,2,128]{3,2,1,0:T(2,128)(2,1)S(1)}, bf16[32,32,2,128]{3,2,1,0:T(2,128)(2,1)S(1)}, u32[]{:S(2)}, u32[]{:S(2)}) %collective-permute-start.40) | collective-permute-done | bytes 524320 | tf_op jit(solution)/shard_map/ppermute | solution.py:314
  237.0 11.0 %collective-permute-start.12 = (bf16[32,64,128]{2,1,0:T(8,128)(2,1)S(1)}, bf16[32,64,128]{2,1,0:T(8,128)(2,1)S(1)}, u32[]{:S(2)}, u32[]{:S(2)}) collective-permute-start(bf16[32,64,128]{2,1,0:T(8,128)(2,1)S(1)} %pad_maximum_fusion.5), channel_id=1, source_target_pairs={{0,24},{2,26},{4,28},{6,30},{8,0},{10,2},{12,4},{14,6},{16,8},{18,... | collective-permute-start | bytes 1572872 | tf_op jit(solution)/shard_map/ppermute | solution.py:317
  249.2 4.7 %collective-permute-done.23 = bf16[32,8,2,128]{3,2,1,0:T(2,128)(2,1)S(1)} collective-permute-done((bf16[32,8,2,128]{3,2,1,0:T(2,128)(2,1)S(1)}, bf16[32,8,2,128]{3,2,1,0:T(2,128)(2,1)S(1)}, u32[]{:S(2)}, u32[]{:S(2)}) %collective-permute-start.23) | collective-permute-done | bytes 131104 | tf_op jit(solution)/shard_map/ppermute | solution.py:314
  254.5 7.3 %collective-permute-done.28.refs_4_ = bf16[3,16,64,128]{3,2,1,0:T(8,128)(2,1)S(1)} collective-permute-done((bf16[3,16,64,128]{3,2,1,0:T(8,128)(2,1)S(1)}, bf16[3,16,64,128]{3,2,1,0:T(8,128)(2,1)S(1)}, u32[]{:S(2)}, u32[]{:S(2)}) %collective-permute-start.28) | collective-permute-done | bytes 786464 | tf_op jit(solution)/shard_map/ppermute | solution.py:317
  264.1 8.9 %collective-permute-done.11 = bf16[32,64,128]{2,1,0:T(8,128)(2,1)S(1)} collective-permute-done((bf16[32,64,128]{2,1,0:T(8,128)(2,1)S(1)}, bf16[32,64,128]{2,1,0:T(8,128)(2,1)S(1)}, u32[]{:S(2)}, u32[]{:S(2)}) %collective-permute-start.11) | collective-permute-done | bytes 524320 | tf_op jit(solution)/shard_map/ppermute | solution.py:317
  274.0 4.5 %collective-permute-done.12 = bf16[32,64,128]{2,1,0:T(8,128)(2,1)S(1)} collective-permute-done((bf16[32,64,128]{2,1,0:T(8,128)(2,1)S(1)}, bf16[32,64,128]{2,1,0:T(8,128)(2,1)S(1)}, u32[]{:S(2)}, u32[]{:S(2)}) %collective-permute-start.12) | collective-permute-done | bytes 524320 | tf_op jit(solution)/shard_map/ppermute | solution.py:317
  279.8 6.2 %collective-permute-done.32 = bf16[32,16,2,128]{3,2,1,0:T(2,128)(2,1)S(1)} collective-permute-done((bf16[32,16,2,128]{3,2,1,0:T(2,128)(2,1)S(1)}, bf16[32,16,2,128]{3,2,1,0:T(2,128)(2,1)S(1)}, u32[]{:S(2)}, u32[]{:S(2)}) %collective-permute-start.32) | collective-permute-done | bytes 262176 | tf_op jit(solution)/shard_map/ppermute | solution.py:314
  286.2 3.4 %copy-done.1 = bf16[32,128,2,512]{3,2,1,0:T(2,128)(2,1)S(1)} copy-done((bf16[32,128,2,512]{3,2,1,0:T(2,128)(2,1)S(1)}, bf16[32,128,2,512]{3,2,1,0:T(2,128)(2,1)}, u32[]{:S(2)}) %copy-start.1) | copy-done | bytes 8388632
  289.6 32.1 %arrange.1 = (bf16[32,256,512]{2,1,0:T(8,128)(2,1)S(1)}, bf16[32,256,256]{2,1,0:T(8,128)(2,1)S(1)}, bf16[32,256,128]{2,1,0:T(8,128)(2,1)S(1)}, bf16[32,256,128]{2,1,0:T(8,128)(2,1)S(1)}) custom-call(bf16[32,128,2,512]{3,2,1,0:T(2,128)(2,1)S(1)} %copy-done.1), custom_call_target="tpu_custom_call" | custom-call | flops 17179869184 | bytes 25165824 | tf_op jit(solution)/shard_map/arrange/pallas_call | solution.py:214
  321.7 3.4 %project.3.refs_3_ = f32[32,256,128]{2,1,0:T(8,128)S(1)} custom-call(bf16[32,256,512]{2,1,0:T(8,128)(2,1)S(1)} %get-tuple-element.71.refs_0_, bf16[32,256,128]{2,1,0:T(8,128)(2,1)S(1)} %pad_maximum_fusion.refs_1_, bf16[32,256,128]{2,1,0:T(8,128)(2,1)S(1)} %collective-permute-done.42.refs_2_), custom_call_target="tpu_custom_call" | custom-call | flops 1073741824 | bytes 16777216 | tf_op jit(solution)/shard_map/project/pallas_call | solution.py:247
  (127 shorter events, 54.2 us)
Async XLA Ops:
  0.8 24.1 %collective-permute-start.2 = (s32[512]{0:T(512)S(1)}, s32[512]{0:T(512)S(1)}, u32[]{:S(2)}, u32[]{:S(2)}) collective-permute-start(s32[512]{0:T(512)S(1)} %dynamic_update_slice.5), channel_id=1, source_target_pairs={{0,24},{2,26},{4,28},{6,30},{8,0},{10,2},{12,4},{14,6},{16,8},{18,... | collective-permute-start | bytes 6152 | tf_op jit(solution)/shard_map/ppermute | solution.py:317
  5.9 20.5 %collective-permute-start.1 = (s32[512]{0:T(512)S(1)}, s32[512]{0:T(512)S(1)}, u32[]{:S(2)}, u32[]{:S(2)}) collective-permute-start(s32[512]{0:T(512)S(1)} %dynamic_update_slice.5), channel_id=1, source_target_pairs={{0,16},{2,18},{4,20},{6,22},{8,24},{10,26},{12,28},{14,30},{16,0},... | collective-permute-start | bytes 6152 | tf_op jit(solution)/shard_map/ppermute | solution.py:317
  12.4 42.5 %collective-permute-start.16 = (bf16[8,64,128]{2,1,0:T(8,128)(2,1)}, bf16[8,64,128]{2,1,0:T(8,128)(2,1)S(1)}, u32[]{:S(2)}, u32[]{:S(2)}) collective-permute-start(bf16[8,64,128]{2,1,0:T(8,128)(2,1)} %bitcast.102), channel_id=1, source_target_pairs={{0,2},{2,0},{4,6},{6,4},{8,10},{10,8},{12,14},{14,12},{16,18},{18,... | collective-permute-start | bytes 393224 | tf_op jit(solution)/shard_map/ppermute | solution.py:314
  13.9 48.3 %collective-permute-start.34 = (bf16[32,64,128]{2,1,0:T(8,128)(2,1)}, bf16[32,64,128]{2,1,0:T(8,128)(2,1)S(1)}, u32[]{:S(2)}, u32[]{:S(2)}) collective-permute-start(bf16[32,64,128]{2,1,0:T(8,128)(2,1)} %bitcast.93), channel_id=1, source_target_pairs={{0,2},{2,0},{4,6},{6,4},{8,10},{10,8},{12,14},{14,12},{16,18},{18,... | collective-permute-start | bytes 1572872 | tf_op jit(solution)/shard_map/ppermute | solution.py:314
  23.2 40.1 %collective-permute-start.35 = (bf16[32,64,128]{2,1,0:T(8,128)(2,1)}, bf16[32,64,128]{2,1,0:T(8,128)(2,1)}, u32[]{:S(2)}, u32[]{:S(2)}) collective-permute-start(bf16[32,64,128]{2,1,0:T(8,128)(2,1)} %bitcast.42), channel_id=1, source_target_pairs={{0,4},{2,6},{4,0},{6,2},{8,12},{10,14},{12,8},{14,10},{16,20},{18,... | collective-permute-start | bytes 1572872 | tf_op jit(solution)/shard_map/ppermute | solution.py:314
  25.0 40.3 %collective-permute-start.36 = (bf16[32,64,128]{2,1,0:T(8,128)(2,1)}, bf16[32,64,128]{2,1,0:T(8,128)(2,1)}, u32[]{:S(2)}, u32[]{:S(2)}) collective-permute-start(bf16[32,64,128]{2,1,0:T(8,128)(2,1)} %bitcast.44), channel_id=1, source_target_pairs={{0,6},{2,4},{4,2},{6,0},{8,14},{10,12},{12,10},{14,8},{16,22},{18,... | collective-permute-start | bytes 1572872 | tf_op jit(solution)/shard_map/ppermute | solution.py:314
  26.4 20.7 %collective-permute-start.3 = (s32[512]{0:T(512)S(1)}, s32[512]{0:T(512)S(1)}, u32[]{:S(2)}, u32[]{:S(2)}) collective-permute-start(s32[512]{0:T(512)S(1)} %add_add_fusion), channel_id=1, source_target_pairs={{0,4},{2,6},{4,0},{6,2},{8,12},{10,14},{12,8},{14,10},{16,20},{18,... | collective-permute-start | bytes 6152 | tf_op jit(solution)/shard_map/ppermute | solution.py:314
  75.6 130.4 %collective-permute-start.38 = (bf16[3,32,64,128]{3,2,1,0:T(8,128)(2,1)S(1)}, bf16[3,32,64,128]{3,2,1,0:T(8,128)(2,1)S(1)}, u32[]{:S(2)}, u32[]{:S(2)}) collective-permute-start(bf16[3,32,64,128]{3,2,1,0:T(8,128)(2,1)S(1)} %pad_maximum_fusion.1.refs_3_), channel_id=1, source_target_pairs={{0,24},{2,26},{4,28},{6,30},{8,0},{10,2},{12,4},{14,6},{16,8},{18,... | collective-permute-start | bytes 4718600 | tf_op jit(solution)/shard_map/ppermute | solution.py:317
  79.2 127.3 %collective-permute-start.37 = (bf16[3,32,64,128]{3,2,1,0:T(8,128)(2,1)S(1)}, bf16[3,32,64,128]{3,2,1,0:T(8,128)(2,1)S(1)}, u32[]{:S(2)}, u32[]{:S(2)}) collective-permute-start(bf16[3,32,64,128]{3,2,1,0:T(8,128)(2,1)S(1)} %pad_maximum_fusion.1.refs_3_), channel_id=1, source_target_pairs={{0,8},{2,10},{4,12},{6,14},{8,16},{10,18},{12,20},{14,22},{16,24},... | collective-permute-start | bytes 4718600 | tf_op jit(solution)/shard_map/ppermute | solution.py:317
  81.5 120.6 %collective-permute-start.15 = (bf16[56,64,128]{2,1,0:T(8,128)(2,1)S(1)}, bf16[56,64,128]{2,1,0:T(8,128)(2,1)S(1)}, u32[]{:S(2)}, u32[]{:S(2)}) collective-permute-start(bf16[56,64,128]{2,1,0:T(8,128)(2,1)S(1)} %bitcast.53), channel_id=1, source_target_pairs={{0,24},{2,26},{4,28},{6,30},{8,0},{10,2},{12,4},{14,6},{16,8},{18,... | collective-permute-start | bytes 2752520 | tf_op jit(solution)/shard_map/ppermute | solution.py:317
  84.6 118.6 %collective-permute-start.14 = (bf16[56,64,128]{2,1,0:T(8,128)(2,1)S(1)}, bf16[56,64,128]{2,1,0:T(8,128)(2,1)S(1)}, u32[]{:S(2)}, u32[]{:S(2)}) collective-permute-start(bf16[56,64,128]{2,1,0:T(8,128)(2,1)S(1)} %bitcast.54), channel_id=1, source_target_pairs={{0,8},{2,10},{4,12},{6,14},{8,16},{10,18},{12,20},{14,22},{16,24},... | collective-permute-start | bytes 2752520 | tf_op jit(solution)/shard_map/ppermute | solution.py:317
  84.6 105.4 %collective-permute-start.19 = (bf16[3,8,64,128]{3,2,1,0:T(8,128)(2,1)S(1)}, bf16[3,8,64,128]{3,2,1,0:T(8,128)(2,1)S(1)}, u32[]{:S(2)}, u32[]{:S(2)}) collective-permute-start(bf16[3,8,64,128]{3,2,1,0:T(8,128)(2,1)S(1)} %pad_maximum_fusion.8.refs_3_), channel_id=1, source_target_pairs={{0,8},{2,10},{4,12},{6,14},{8,16},{10,18},{12,20},{14,22},{16,24},... | collective-permute-start | bytes 1179656 | tf_op jit(solution)/shard_map/ppermute | solution.py:317
  203.9 22.1 %collective-permute-start.21 = (bf16[32,8,2,128]{3,2,1,0:T(2,128)(2,1)S(1)}, bf16[32,8,2,128]{3,2,1,0:T(2,128)(2,1)S(1)}, u32[]{:S(2)}, u32[]{:S(2)}) collective-permute-start(bf16[32,8,2,128]{3,2,1,0:T(2,128)(2,1)S(1)} %get-tuple-element.60), channel_id=1, source_target_pairs={{0,2},{2,0},{4,6},{6,4},{8,10},{10,8},{12,14},{14,12},{16,18},{18,... | collective-permute-start | bytes 393224 | tf_op jit(solution)/shard_map/ppermute | solution.py:314
  206.0 19.9 %collective-permute-start.22 = (bf16[32,8,2,128]{3,2,1,0:T(2,128)(2,1)S(1)}, bf16[32,8,2,128]{3,2,1,0:T(2,128)(2,1)S(1)}, u32[]{:S(2)}, u32[]{:S(2)}) collective-permute-start(bf16[32,8,2,128]{3,2,1,0:T(2,128)(2,1)S(1)} %get-tuple-element.61), channel_id=1, source_target_pairs={{0,4},{2,6},{4,0},{6,2},{8,12},{10,14},{12,8},{14,10},{16,20},{18,... | collective-permute-start | bytes 393224 | tf_op jit(solution)/shard_map/ppermute | solution.py:314
  216.6 20.4 %collective-permute-start.40 = (bf16[32,32,2,128]{3,2,1,0:T(2,128)(2,1)S(1)}, bf16[32,32,2,128]{3,2,1,0:T(2,128)(2,1)S(1)}, u32[]{:S(2)}, u32[]{:S(2)}) collective-permute-start(bf16[32,32,2,128]{3,2,1,0:T(2,128)(2,1)S(1)} %get-tuple-element.77), channel_id=1, source_target_pairs={{0,4},{2,6},{4,0},{6,2},{8,12},{10,14},{12,8},{14,10},{16,20},{18,... | collective-permute-start | bytes 1572872 | tf_op jit(solution)/shard_map/ppermute | solution.py:314
  218.4 35.6 %collective-permute-start.29 = (bf16[3,16,64,128]{3,2,1,0:T(8,128)(2,1)S(1)}, bf16[3,16,64,128]{3,2,1,0:T(8,128)(2,1)S(1)}, u32[]{:S(2)}, u32[]{:S(2)}) collective-permute-start(bf16[3,16,64,128]{3,2,1,0:T(8,128)(2,1)S(1)} %pad_maximum_fusion.3.refs_3_), channel_id=1, source_target_pairs={{0,24},{2,26},{4,28},{6,30},{8,0},{10,2},{12,4},{14,6},{16,8},{18,... | collective-permute-start | bytes 2359304 | tf_op jit(solution)/shard_map/ppermute | solution.py:317
  225.9 35.9 %collective-permute-start.28 = (bf16[3,16,64,128]{3,2,1,0:T(8,128)(2,1)S(1)}, bf16[3,16,64,128]{3,2,1,0:T(8,128)(2,1)S(1)}, u32[]{:S(2)}, u32[]{:S(2)}) collective-permute-start(bf16[3,16,64,128]{3,2,1,0:T(8,128)(2,1)S(1)} %pad_maximum_fusion.3.refs_3_), channel_id=1, source_target_pairs={{0,8},{2,10},{4,12},{6,14},{8,16},{10,18},{12,20},{14,22},{16,24},... | collective-permute-start | bytes 2359304 | tf_op jit(solution)/shard_map/ppermute | solution.py:317
  225.9 22.1 %collective-permute-start.41 = (bf16[32,32,2,128]{3,2,1,0:T(2,128)(2,1)S(1)}, bf16[32,32,2,128]{3,2,1,0:T(2,128)(2,1)S(1)}, u32[]{:S(2)}, u32[]{:S(2)}) collective-permute-start(bf16[32,32,2,128]{3,2,1,0:T(2,128)(2,1)S(1)} %get-tuple-element.78), channel_id=1, source_target_pairs={{0,6},{2,4},{4,2},{6,0},{8,14},{10,12},{12,10},{14,8},{16,22},{18,... | collective-permute-start | bytes 1572872 | tf_op jit(solution)/shard_map/ppermute | solution.py:314
  227.3 45.7 %collective-permute-start.11 = (bf16[32,64,128]{2,1,0:T(8,128)(2,1)S(1)}, bf16[32,64,128]{2,1,0:T(8,128)(2,1)S(1)}, u32[]{:S(2)}, u32[]{:S(2)}) collective-permute-start(bf16[32,64,128]{2,1,0:T(8,128)(2,1)S(1)} %pad_maximum_fusion.4), channel_id=1, source_target_pairs={{0,8},{2,10},{4,12},{6,14},{8,16},{10,18},{12,20},{14,22},{16,24},... | collective-permute-start | bytes 1572872 | tf_op jit(solution)/shard_map/ppermute | solution.py:317
  237.0 41.5 %collective-permute-start.12 = (bf16[32,64,128]{2,1,0:T(8,128)(2,1)S(1)}, bf16[32,64,128]{2,1,0:T(8,128)(2,1)S(1)}, u32[]{:S(2)}, u32[]{:S(2)}) collective-permute-start(bf16[32,64,128]{2,1,0:T(8,128)(2,1)S(1)} %pad_maximum_fusion.5), channel_id=1, source_target_pairs={{0,24},{2,26},{4,28},{6,30},{8,0},{10,2},{12,4},{14,6},{16,8},{18,... | collective-permute-start | bytes 1572872 | tf_op jit(solution)/shard_map/ppermute | solution.py:317
  253.9 67.8 %collective-permute-start.42 = (bf16[32,256,128]{2,1,0:T(8,128)(2,1)S(1)}, bf16[32,256,128]{2,1,0:T(8,128)(2,1)S(1)}, u32[]{:S(2)}, u32[]{:S(2)}) collective-permute-start(bf16[32,256,128]{2,1,0:T(8,128)(2,1)S(1)} %pad_maximum_fusion.refs_1_), channel_id=1, source_target_pairs={{0,1},{1,0},{2,3},{3,2},{4,5},{5,4},{6,7},{7,6},{8,9},{9,8},{10,11... | collective-permute-start | bytes 6291464 | tf_op jit(solution)/shard_map/ppermute | solution.py:372
  254.0 73.5 %collective-permute-start.24 = (bf16[32,64,128]{2,1,0:T(8,128)(2,1)S(1)}, bf16[32,64,128]{2,1,0:T(8,128)(2,1)S(1)}, u32[]{:S(2)}, u32[]{:S(2)}) collective-permute-start(bf16[32,64,128]{2,1,0:T(8,128)(2,1)S(1)} %pad_maximum_fusion.6.refs_1_), channel_id=1, source_target_pairs={{0,1},{1,0},{2,3},{3,2},{4,5},{5,4},{6,7},{7,6},{8,9},{9,8},{10,11... | collective-permute-start | bytes 1572872 | tf_op jit(solution)/shard_map/ppermute | solution.py:372
  279.7 49.7 %collective-permute-start.13 = (bf16[32,64,128]{2,1,0:T(8,128)(2,1)S(1)}, bf16[32,64,128]{2,1,0:T(8,128)(2,1)S(1)}, u32[]{:S(2)}, u32[]{:S(2)}) collective-permute-start(bf16[32,64,128]{2,1,0:T(8,128)(2,1)S(1)} %add_convert_fusion.refs_0_), channel_id=1, source_target_pairs={{0,1},{1,0},{2,3},{3,2},{4,5},{5,4},{6,7},{7,6},{8,9},{9,8},{10,11... | collective-permute-start | bytes 1572872 | tf_op jit(solution)/shard_map/ppermute | solution.py:372
  286.1 39.0 %collective-permute-start.33 = (bf16[32,128,128]{2,1,0:T(8,128)(2,1)S(1)}, bf16[32,128,128]{2,1,0:T(8,128)(2,1)S(1)}, u32[]{:S(2)}, u32[]{:S(2)}) collective-permute-start(bf16[32,128,128]{2,1,0:T(8,128)(2,1)S(1)} %pad_maximum_fusion.2.refs_1_), channel_id=1, source_target_pairs={{0,1},{1,0},{2,3},{3,2},{4,5},{5,4},{6,7},{7,6},{8,9},{9,8},{10,11... | collective-permute-start | bytes 3145736 | tf_op jit(solution)/shard_map/ppermute | solution.py:372
  (27 other events, 288.0 us)

commit v3 on v2

--- a/solution.py
+++ b/solution.py
@@ -11,7 +11,7 @@
 
 H = 128
 UNITS = 8
-PARTS = (4, 2, 1, 1)
+PARTS = (5, 2, 1)
 VMEM_BYTES = 24 << 20
 
 
@@ -257,30 +257,19 @@
 
 
 def project_last(basis, pieces, total):
-    rows, out_rows, width = basis.shape
+    rows, out_rows, _ = basis.shape
     svd = pieces[0].shape[2]
     block = math.gcd(rows, 4)
 
     def kernel(a_ref, *refs):
         data_refs, t_ref, out, buf, sem = refs[: len(pieces)], *refs[len(pieces) :]
-        empty = jnp.zeros((width, svd), jnp.bfloat16)
-
-        @pl.loop(0, rows // block)
-        def step(n):
-            for m in range(0, block, 2):
-                at = n * block + m
-                left = jnp.concatenate([a_ref[at], a_ref[at + 1]], axis=1)
-                one = jnp.concatenate([ref[at] for ref in data_refs], axis=0)
-                two = jnp.concatenate([ref[at + 1] for ref in data_refs], axis=0)
-                right = jnp.concatenate(
-                    [jnp.concatenate([one, empty], axis=1), jnp.concatenate([empty, two], axis=1)], axis=0
-                )
-                value = jnp.dot(left, right, preferred_element_type=jnp.float32)
-                buf[at] = (value[:, :svd] + t_ref[at]).astype(buf.dtype)
-                buf[at + 1] = (value[:, svd:] + t_ref[at + 1]).astype(buf.dtype)
-            span = pl.ds(n * block, block)
+        for n in range(0, rows, block):
+            for m in range(n, n + block):
+                data = jnp.concatenate([ref[m] for ref in data_refs], axis=0)
+                value = jnp.dot(a_ref[m], data, preferred_element_type=jnp.float32)
+                buf[m] = (value + t_ref[m]).astype(buf.dtype)
+            span = pl.ds(n, block)
             pltpu.make_async_copy(buf.at[span], out.at[span], sem).start()
-
         pltpu.make_async_copy(buf, out, sem).wait()
 
     args = [basis, *pieces, total]

time: 333 us -> 290 us (0.87)
  waiting for transfers between devices: 186 us -> 144 us
  starting transfers between devices: 66.4 us -> 47.3 us
  other arithmetic: 13.5 us -> 26.2 us
  local copies, waits for them, and re-layouts: 5.33 us -> 9.93 us
    ppermute x26 -> x20, waiting for transfers between devices: 63.2 us -> 28.7 us  [swap(): return lax.ppermute(x, 'ma', [(i, i ^ bits) for i in range(count)])]
    ppermute x13 -> x11, starting transfers between devices: 34.7 us -> 19.2 us  [shift(): lax.ppermute(x, 'ma', [(i, (i + by * group) % count) for i in range(count)])]
    ppermute x13 -> x11, waiting for transfers between devices: 123 us -> 115 us  [shift(): lax.ppermute(x, 'ma', [(i, (i + by * group) % count) for i in range(count)])]
    unnamed x16 -> x72, local copies, waits for them, and re-layouts: 3.41 us -> 6.93 us
    ppermute x26 -> x20, starting transfers between devices: 31 us -> 27.5 us  [swap(): return lax.ppermute(x, 'ma', [(i, i ^ bits) for i in range(count)])]
    pallas_call x3 -> x2, Pallas kernels: 5.85 us -> 7.43 us  [mix(): pl.pallas_call(kernel, grid=(size // unit,), out_shape=[jax.ShapeDtypeStr...]
    pallas_call x3 -> x2, Pallas kernels: 7.61 us -> 6.35 us  [project(): pl.pallas_call(kernel, grid=(rows // step,), out_shape=out_shape, in_spec...]
  transfers between devices with their start and end apart: 43 -> 34, of which waited for: 13 -> 11; matrix products, arithmetic and copies ran while one was open for 5% -> 11% of each run, Pallas kernels for 16% -> 19%
where the time goes in v3:
time: 290 us; the launch traced here: 289 us
  waiting for transfers between devices  144 us (50%)
  Pallas kernels  55.3 us (19%)
  starting transfers between devices  47.3 us (16%)
  other arithmetic  26.2 us (9%)
  local copies, waits for them, and re-layouts  9.93 us (3%)
  matrix products  5.26 us (2%)
    ppermute x11, waiting for transfers between devices, shift(): lax.ppermute(x, 'ma', [(i, (i + by * group) % count) for i in range(count)])  115 us
    pallas_call x1, Pallas kernels, arrange_basis(): pl.pallas_call(kernel, grid=(rows,), out_shape=[jax.ShapeDtypeStruct((row...  32 us
    ppermute x20, waiting for transfers between devices, swap(): return lax.ppermute(x, 'ma', [(i, i ^ bits) for i in range(count)])  28.7 us
    ppermute x20, starting transfers between devices, swap(): return lax.ppermute(x, 'ma', [(i, i ^ bits) for i in range(count)])  27.5 us
    ppermute x11, starting transfers between devices, shift(): lax.ppermute(x, 'ma', [(i, (i + by * group) % count) for i in range(count)])  19.2 us
    sin x2, other arithmetic, waves(): return (jnp.cos(phases), jnp.sin(phases))  13.6 us
    pallas_call x2, Pallas kernels, mix(): pl.pallas_call(kernel, grid=(size // unit,), out_shape=[jax.ShapeDtypeStr...  7.43 us
    unnamed x72, local copies, waits for them, and re-layouts  6.93 us
  transfers between devices with their start and end apart: 34, of which 11 were waited for; matrix products, arithmetic and copies ran while one was open for 11% of the time, Pallas kernels for 19%

profile of v3, /device:TPU:0, one launch (start us, length us, event | category | flops | bytes accessed | tf_op | source)
XLA Modules:
  0.0 288.5 jit_solution(5010009252854090111)
XLA Ops:
  1.9 5.1 %collective-permute-start.2 = (s32[512]{0:T(512)}, s32[512]{0:T(512)}, u32[]{:S(2)}, u32[]{:S(2)}) collective-permute-start(s32[512]{0:T(512)} %dynamic_update_slice.5), channel_id=1, source_target_pairs={{0,24},{2,26},{4,28},{6,30},{8,0},{10,2},{12,4},{14,6},{16,8},{18,... | collective-permute-start | bytes 6152 | tf_op jit(solution)/shard_map/ppermute | solution.py:306
  7.0 4.6 %regroup.1 = (bf16[40,32,2,128]{3,2,1,0:T(2,128)(2,1)}, bf16[40,32,2,128]{3,2,1,0:T(2,128)(2,1)}, bf16[40,32,2,128]{3,2,1,0:T(2,128)(2,1)}, bf16[16,32,2,128]{3,...) custom-call(bf16[32,256,2,128]{3,2,1,0:T(2,128)(2,1)} %src.3), custom_call_target="tpu_custom_call" | custom-call | bytes 6553600 | tf_op jit(solution)/shard_map/regroup/pallas_call | solution.py:42
  20.9 9.8 %fusion.29 = (f32[768,512]{1,0:T(8,128)S(1)}, f32[768,512]{1,0:T(8,128)}) fusion(s32[768]{0:T(1024)} %get-tuple-element.93, s32[768]{0:T(1024)} %get-tuple-element.94, pred[768]{0:T(1024)(128)(4,1)} %fusion.52, s32[768]{0:T(1024)} %get-tuple-element.90, s32[768]{0:T(1024)S(1)} %get-tuple-element.92, pred[768]{0:T(1024)(128)(4,1)} %get-tuple-element.96, ...), kind=kLoop, calls=%fused_computation.87 | loop fusion | flops 19660800 | bytes 3173380 | tf_op jit(solution)/shard_map/sin | solution.py:85
  37.7 4.5 %collective-permute-done.3 = s32[512]{0:T(512)S(1)} collective-permute-done((s32[512]{0:T(512)S(1)}, s32[512]{0:T(512)S(1)}, u32[]{:S(2)}, u32[]{:S(2)}) %collective-permute-start.3) | collective-permute-done | bytes 2080 | tf_op jit(solution)/shard_map/ppermute | solution.py:303
  42.2 2.5 collective-permute-start.6
  48.4 3.3 %collective-permute-start.29 = (bf16[3,40,64,128]{3,2,1,0:T(8,128)(2,1)S(1)}, bf16[3,40,64,128]{3,2,1,0:T(8,128)(2,1)}, u32[]{:S(2)}, u32[]{:S(2)}) collective-permute-start(bf16[3,40,64,128]{3,2,1,0:T(8,128)(2,1)S(1)} %pad_maximum_fusion.1.refs_3_), channel_id=1, source_target_pairs={{0,24},{2,26},{4,28},{6,30},{8,0},{10,2},{12,4},{14,6},{16,8},{18,... | collective-permute-start | bytes 5898248 | tf_op jit(solution)/shard_map/ppermute | solution.py:306
  51.7 3.7 %fusion.47 = (f32[256,512]{1,0:T(8,128)}, f32[256,512]{1,0:T(8,128)}) fusion(s32[256]{0:T(256)S(1)} %copy-done.25, s32[256]{0:T(256)S(1)} %copy-done.26, pred[256]{0:T(512)(128)(4,1)S(1)} %compare_and_fusion, s32[256]{0:T(256)S(1)} %copy-done.23, s32[256]{0:T(256)S(1)} %copy-done.19, pred[256]{0:T(512)(128)(4,1)S(1)} %copy-done.28, s32[256]{0:T(256)S(1)} %copy-done.17, ...), kind=kLoop, calls=%fused_computation.110 | loop fusion | flops 6553600 | bytes 1057796 | tf_op jit(solution)/shard_map/sin | solution.py:85
  62.0 2.5 fusion.42
  65.3 3.7 %collective-permute-start.15 = (bf16[56,64,128]{2,1,0:T(8,128)(2,1)S(1)}, bf16[56,64,128]{2,1,0:T(8,128)(2,1)S(1)}, u32[]{:S(2)}, u32[]{:S(2)}) collective-permute-start(bf16[56,64,128]{2,1,0:T(8,128)(2,1)S(1)} %bitcast.43), channel_id=1, source_target_pairs={{0,24},{2,26},{4,28},{6,30},{8,0},{10,2},{12,4},{14,6},{16,8},{18,... | collective-permute-start | bytes 2752520 | tf_op jit(solution)/shard_map/ppermute | solution.py:306
  70.7 2.7 fusion.13.t_ref
  79.0 77.7 %collective-permute-done.15.refs_2_ = bf16[56,64,128]{2,1,0:T(8,128)(2,1)S(1)} collective-permute-done((bf16[56,64,128]{2,1,0:T(8,128)(2,1)S(1)}, bf16[56,64,128]{2,1,0:T(8,128)(2,1)S(1)}, u32[]{:S(2)}, u32[]{:S(2)}) %collective-permute-start.15) | collective-permute-done | bytes 917536 | tf_op jit(solution)/shard_map/ppermute | solution.py:306
  156.7 17.9 %collective-permute-done.14.refs_1_ = bf16[56,64,128]{2,1,0:T(8,128)(2,1)S(1)} collective-permute-done((bf16[56,64,128]{2,1,0:T(8,128)(2,1)S(1)}, bf16[56,64,128]{2,1,0:T(8,128)(2,1)S(1)}, u32[]{:S(2)}, u32[]{:S(2)}) %collective-permute-start.14) | collective-permute-done | bytes 917536 | tf_op jit(solution)/shard_map/ppermute | solution.py:306
  176.1 5.7 %mix.3 = (bf16[32,40,2,128]{3,2,1,0:T(2,128)(2,1)S(1)}, bf16[32,40,2,128]{3,2,1,0:T(2,128)(2,1)S(1)}, bf16[32,40,2,128]{3,2,1,0:T(2,128)(2,1)S(1)}, bf16[32,40,2,128]{3,2,1,0:T(2,128)(2,1)S(1)}) custom-call(bf16[256,768]{1,0:T(8,128)(2,1)S(1)} %fusion.13.t_ref, bf16[56,64,128]{2,1,0:T(8,128)(2,1)S(1)} %bitcast.45, ...), custom_call_target="tpu_custom_call" | custom-call | flops 2013265920 | bytes 10878976 | tf_op jit(solution)/shard_map/mix/pallas_call | solution.py:130
  189.0 10.7 %collective-permute-done.30 = bf16[32,40,2,128]{3,2,1,0:T(2,128)(2,1)S(1)} collective-permute-done((bf16[32,40,2,128]{3,2,1,0:T(2,128)(2,1)S(1)}, bf16[32,40,2,128]{3,2,1,0:T(2,128)(2,1)S(1)}, u32[]{:S(2)}, u32[]{:S(2)}) %collective-permute-start.30) | collective-permute-done | bytes 655392 | tf_op jit(solution)/shard_map/ppermute | solution.py:303
  201.3 11.7 %collective-permute-done.31 = bf16[32,40,2,128]{3,2,1,0:T(2,128)(2,1)S(1)} collective-permute-done((bf16[32,40,2,128]{3,2,1,0:T(2,128)(2,1)S(1)}, bf16[32,40,2,128]{3,2,1,0:T(2,128)(2,1)S(1)}, u32[]{:S(2)}, u32[]{:S(2)}) %collective-permute-start.31) | collective-permute-done | bytes 655392 | tf_op jit(solution)/shard_map/ppermute | solution.py:303
  215.3 7.7 %collective-permute-done.19.refs_4_ = bf16[3,16,64,128]{3,2,1,0:T(8,128)(2,1)S(1)} collective-permute-done((bf16[3,16,64,128]{3,2,1,0:T(8,128)(2,1)S(1)}, bf16[3,16,64,128]{3,2,1,0:T(8,128)(2,1)S(1)}, u32[]{:S(2)}, u32[]{:S(2)}) %collective-permute-start.19) | collective-permute-done | bytes 786464 | tf_op jit(solution)/shard_map/ppermute | solution.py:306
  224.7 4.8 %collective-permute-start.21 = (bf16[32,16,2,128]{3,2,1,0:T(2,128)(2,1)S(1)}, bf16[32,16,2,128]{3,2,1,0:T(2,128)(2,1)S(1)}, u32[]{:S(2)}, u32[]{:S(2)}) collective-permute-start(bf16[32,16,2,128]{3,2,1,0:T(2,128)(2,1)S(1)} %get-tuple-element.52), channel_id=1, source_target_pairs={{0,2},{2,0},{4,6},{6,4},{8,10},{10,8},{12,14},{14,12},{16,18},{18,... | collective-permute-start | bytes 786440 | tf_op jit(solution)/shard_map/ppermute | solution.py:303
  229.4 4.7 %collective-permute-done.11 = bf16[32,64,128]{2,1,0:T(8,128)(2,1)S(1)} collective-permute-done((bf16[32,64,128]{2,1,0:T(8,128)(2,1)S(1)}, bf16[32,64,128]{2,1,0:T(8,128)(2,1)S(1)}, u32[]{:S(2)}, u32[]{:S(2)}) %collective-permute-start.11) | collective-permute-done | bytes 524320 | tf_op jit(solution)/shard_map/ppermute | solution.py:306
  235.5 6.3 %collective-permute-done.12 = bf16[32,64,128]{2,1,0:T(8,128)(2,1)S(1)} collective-permute-done((bf16[32,64,128]{2,1,0:T(8,128)(2,1)S(1)}, bf16[32,64,128]{2,1,0:T(8,128)(2,1)S(1)}, u32[]{:S(2)}, u32[]{:S(2)}) %collective-permute-start.12) | collective-permute-done | bytes 524320 | tf_op jit(solution)/shard_map/ppermute | solution.py:306
  242.8 3.4 %copy-done.3 = bf16[32,128,2,512]{3,2,1,0:T(2,128)(2,1)S(1)} copy-done((bf16[32,128,2,512]{3,2,1,0:T(2,128)(2,1)S(1)}, bf16[32,128,2,512]{3,2,1,0:T(2,128)(2,1)}, u32[]{:S(2)}) %copy-start.3) | copy-done | bytes 8388632
  246.2 32.0 %arrange.1 = (bf16[32,256,640]{2,1,0:T(8,128)(2,1)S(1)}, bf16[32,256,256]{2,1,0:T(8,128)(2,1)S(1)}, bf16[32,256,128]{2,1,0:T(8,128)(2,1)S(1)}) custom-call(bf16[32,128,2,512]{3,2,1,0:T(2,128)(2,1)S(1)} %copy-done.3), custom_call_target="tpu_custom_call" | custom-call | flops 17179869184 | bytes 25165824 | tf_op jit(solution)/shard_map/arrange/pallas_call | solution.py:214
  278.2 4.0 %project.2.refs_3_ = f32[32,256,128]{2,1,0:T(8,128)S(1)} custom-call(bf16[32,256,640]{2,1,0:T(8,128)(2,1)S(1)} %get-tuple-element.55.refs_0_, bf16[32,320,128]{2,1,0:T(8,128)(2,1)S(1)} %pad_maximum_fusion.refs_1_, bf16[32,320,128]{2,1,0:T(8,128)(2,1)S(1)} %collective-permute-done.33.refs_2_), custom_call_target="tpu_custom_call" | custom-call | flops 1342177280 | bytes 19922944 | tf_op jit(solution)/shard_map/project/pallas_call | solution.py:247
  282.3 2.2 copy-done.2
  284.5 2.3 project.3.refs_2_
  (161 shorter events, 54.1 us)
Async XLA Ops:
  1.9 31.4 %collective-permute-start.2 = (s32[512]{0:T(512)}, s32[512]{0:T(512)}, u32[]{:S(2)}, u32[]{:S(2)}) collective-permute-start(s32[512]{0:T(512)} %dynamic_update_slice.5), channel_id=1, source_target_pairs={{0,24},{2,26},{4,28},{6,30},{8,0},{10,2},{12,4},{14,6},{16,8},{18,... | collective-permute-start | bytes 6152 | tf_op jit(solution)/shard_map/ppermute | solution.py:306
  7.0 23.8 %collective-permute-start = (s32[512]{0:T(512)}, s32[512]{0:T(512)}, u32[]{:S(2)}, u32[]{:S(2)}) collective-permute-start(s32[512]{0:T(512)} %dynamic_update_slice.5), channel_id=1, source_target_pairs={{0,8},{2,10},{4,12},{6,14},{8,16},{10,18},{12,20},{14,22},{16,24},... | collective-permute-start | bytes 6152 | tf_op jit(solution)/shard_map/ppermute | solution.py:306
  11.6 33.7 %collective-permute-start.25 = (bf16[40,64,128]{2,1,0:T(8,128)(2,1)}, bf16[40,64,128]{2,1,0:T(8,128)(2,1)S(1)}, u32[]{:S(2)}, u32[]{:S(2)}) collective-permute-start(bf16[40,64,128]{2,1,0:T(8,128)(2,1)} %bitcast.77), channel_id=1, source_target_pairs={{0,2},{2,0},{4,6},{6,4},{8,10},{10,8},{12,14},{14,12},{16,18},{18,... | collective-permute-start | bytes 1966088 | tf_op jit(solution)/shard_map/ppermute | solution.py:303
  13.2 32.1 %collective-permute-start.26 = (bf16[40,64,128]{2,1,0:T(8,128)(2,1)}, bf16[40,64,128]{2,1,0:T(8,128)(2,1)S(1)}, u32[]{:S(2)}, u32[]{:S(2)}) collective-permute-start(bf16[40,64,128]{2,1,0:T(8,128)(2,1)} %bitcast.76), channel_id=1, source_target_pairs={{0,4},{2,6},{4,0},{6,2},{8,12},{10,14},{12,8},{14,10},{16,20},{18,... | collective-permute-start | bytes 1966088 | tf_op jit(solution)/shard_map/ppermute | solution.py:303
  14.7 30.6 %collective-permute-start.27 = (bf16[40,64,128]{2,1,0:T(8,128)(2,1)}, bf16[40,64,128]{2,1,0:T(8,128)(2,1)S(1)}, u32[]{:S(2)}, u32[]{:S(2)}) collective-permute-start(bf16[40,64,128]{2,1,0:T(8,128)(2,1)} %bitcast.75), channel_id=1, source_target_pairs={{0,6},{2,4},{4,2},{6,0},{8,14},{10,12},{12,10},{14,8},{16,22},{18,... | collective-permute-start | bytes 1966088 | tf_op jit(solution)/shard_map/ppermute | solution.py:303
  33.3 26.5 %collective-permute-start.5 = (bf16[8,64,128]{2,1,0:T(8,128)(2,1)}, bf16[8,64,128]{2,1,0:T(8,128)(2,1)}, u32[]{:S(2)}, u32[]{:S(2)}) collective-permute-start(bf16[8,64,128]{2,1,0:T(8,128)(2,1)} %bitcast.1), channel_id=1, source_target_pairs={{0,2},{2,0},{4,6},{6,4},{8,10},{10,8},{12,14},{14,12},{16,18},{18,... | collective-permute-start | bytes 393224 | tf_op jit(solution)/shard_map/ppermute | solution.py:303
  42.2 18.3 %collective-permute-start.6 = (bf16[8,64,128]{2,1,0:T(8,128)(2,1)}, bf16[8,64,128]{2,1,0:T(8,128)(2,1)}, u32[]{:S(2)}, u32[]{:S(2)}) collective-permute-start(bf16[8,64,128]{2,1,0:T(8,128)(2,1)} %bitcast.3), channel_id=1, source_target_pairs={{0,4},{2,6},{4,0},{6,2},{8,12},{10,14},{12,8},{14,10},{16,20},{18,... | collective-permute-start | bytes 393224 | tf_op jit(solution)/shard_map/ppermute | solution.py:303
  48.4 127.8 %collective-permute-start.29 = (bf16[3,40,64,128]{3,2,1,0:T(8,128)(2,1)S(1)}, bf16[3,40,64,128]{3,2,1,0:T(8,128)(2,1)}, u32[]{:S(2)}, u32[]{:S(2)}) collective-permute-start(bf16[3,40,64,128]{3,2,1,0:T(8,128)(2,1)S(1)} %pad_maximum_fusion.1.refs_3_), channel_id=1, source_target_pairs={{0,24},{2,26},{4,28},{6,30},{8,0},{10,2},{12,4},{14,6},{16,8},{18,... | collective-permute-start | bytes 5898248 | tf_op jit(solution)/shard_map/ppermute | solution.py:306
  51.6 124.5 %collective-permute-start.28 = (bf16[3,40,64,128]{3,2,1,0:T(8,128)(2,1)S(1)}, bf16[3,40,64,128]{3,2,1,0:T(8,128)(2,1)}, u32[]{:S(2)}, u32[]{:S(2)}) collective-permute-start(bf16[3,40,64,128]{3,2,1,0:T(8,128)(2,1)S(1)} %pad_maximum_fusion.1.refs_3_), channel_id=1, source_target_pairs={{0,8},{2,10},{4,12},{6,14},{8,16},{10,18},{12,20},{14,22},{16,24},... | collective-permute-start | bytes 5898248 | tf_op jit(solution)/shard_map/ppermute | solution.py:306
  65.3 91.3 %collective-permute-start.15 = (bf16[56,64,128]{2,1,0:T(8,128)(2,1)S(1)}, bf16[56,64,128]{2,1,0:T(8,128)(2,1)S(1)}, u32[]{:S(2)}, u32[]{:S(2)}) collective-permute-start(bf16[56,64,128]{2,1,0:T(8,128)(2,1)S(1)} %bitcast.43), channel_id=1, source_target_pairs={{0,24},{2,26},{4,28},{6,30},{8,0},{10,2},{12,4},{14,6},{16,8},{18,... | collective-permute-start | bytes 2752520 | tf_op jit(solution)/shard_map/ppermute | solution.py:306
  69.0 105.6 %collective-permute-start.14 = (bf16[56,64,128]{2,1,0:T(8,128)(2,1)S(1)}, bf16[56,64,128]{2,1,0:T(8,128)(2,1)S(1)}, u32[]{:S(2)}, u32[]{:S(2)}) collective-permute-start(bf16[56,64,128]{2,1,0:T(8,128)(2,1)S(1)} %bitcast.44), channel_id=1, source_target_pairs={{0,8},{2,10},{4,12},{6,14},{8,16},{10,18},{12,20},{14,22},{16,24},... | collective-permute-start | bytes 2752520 | tf_op jit(solution)/shard_map/ppermute | solution.py:306
  76.5 107.4 %collective-permute-start.8 = (bf16[3,32,8,2,128]{4,3,2,1,0:T(2,128)(2,1)S(1)}, bf16[3,32,8,2,128]{4,3,2,1,0:T(2,128)(2,1)S(1)}, u32[]{:S(2)}, u32[]{:S(2)}) collective-permute-start(bf16[3,32,8,2,128]{4,3,2,1,0:T(2,128)(2,1)S(1)} %get-tuple-element.44), channel_id=1, source_target_pairs={{0,2},{2,0},{4,6},{6,4},{8,10},{10,8},{12,14},{14,12},{16,18},{18,... | collective-permute-start | bytes 1179656 | tf_op jit(solution)/shard_map/ppermute | solution.py:303
  156.7 29.0 %collective-permute-start.9 = (bf16[3,32,8,2,128]{4,3,2,1,0:T(2,128)(2,1)S(1)}, bf16[3,32,8,2,128]{4,3,2,1,0:T(2,128)(2,1)S(1)}, u32[]{:S(2)}, u32[]{:S(2)}) collective-permute-start(bf16[3,32,8,2,128]{4,3,2,1,0:T(2,128)(2,1)S(1)} %get-tuple-element.45), channel_id=1, source_target_pairs={{0,4},{2,6},{4,0},{6,2},{8,12},{10,14},{12,8},{14,10},{16,20},{18,... | collective-permute-start | bytes 1179656 | tf_op jit(solution)/shard_map/ppermute | solution.py:303
  181.9 17.8 %collective-permute-start.30 = (bf16[32,40,2,128]{3,2,1,0:T(2,128)(2,1)S(1)}, bf16[32,40,2,128]{3,2,1,0:T(2,128)(2,1)S(1)}, u32[]{:S(2)}, u32[]{:S(2)}) collective-permute-start(bf16[32,40,2,128]{3,2,1,0:T(2,128)(2,1)S(1)} %get-tuple-element.60), channel_id=1, source_target_pairs={{0,2},{2,0},{4,6},{6,4},{8,10},{10,8},{12,14},{14,12},{16,18},{18,... | collective-permute-start | bytes 1966088 | tf_op jit(solution)/shard_map/ppermute | solution.py:303
  182.4 30.7 %collective-permute-start.31 = (bf16[32,40,2,128]{3,2,1,0:T(2,128)(2,1)S(1)}, bf16[32,40,2,128]{3,2,1,0:T(2,128)(2,1)S(1)}, u32[]{:S(2)}, u32[]{:S(2)}) collective-permute-start(bf16[32,40,2,128]{3,2,1,0:T(2,128)(2,1)S(1)} %get-tuple-element.61), channel_id=1, source_target_pairs={{0,4},{2,6},{4,0},{6,2},{8,12},{10,14},{12,8},{14,10},{16,20},{18,... | collective-permute-start | bytes 1966088 | tf_op jit(solution)/shard_map/ppermute | solution.py:303
  183.9 29.1 %collective-permute-start.32 = (bf16[32,40,2,128]{3,2,1,0:T(2,128)(2,1)S(1)}, bf16[32,40,2,128]{3,2,1,0:T(2,128)(2,1)S(1)}, u32[]{:S(2)}, u32[]{:S(2)}) collective-permute-start(bf16[32,40,2,128]{3,2,1,0:T(2,128)(2,1)S(1)} %get-tuple-element.62), channel_id=1, source_target_pairs={{0,6},{2,4},{4,2},{6,0},{8,14},{10,12},{12,10},{14,8},{16,22},{18,... | collective-permute-start | bytes 1966088 | tf_op jit(solution)/shard_map/ppermute | solution.py:303
  185.7 29.6 %collective-permute-start.20 = (bf16[3,16,64,128]{3,2,1,0:T(8,128)(2,1)S(1)}, bf16[3,16,64,128]{3,2,1,0:T(8,128)(2,1)S(1)}, u32[]{:S(2)}, u32[]{:S(2)}) collective-permute-start(bf16[3,16,64,128]{3,2,1,0:T(8,128)(2,1)S(1)} %pad_maximum_fusion.3.refs_3_), channel_id=1, source_target_pairs={{0,24},{2,26},{4,28},{6,30},{8,0},{10,2},{12,4},{14,6},{16,8},{18,... | collective-permute-start | bytes 2359304 | tf_op jit(solution)/shard_map/ppermute | solution.py:306
  187.8 35.2 %collective-permute-start.19 = (bf16[3,16,64,128]{3,2,1,0:T(8,128)(2,1)S(1)}, bf16[3,16,64,128]{3,2,1,0:T(8,128)(2,1)S(1)}, u32[]{:S(2)}, u32[]{:S(2)}) collective-permute-start(bf16[3,16,64,128]{3,2,1,0:T(8,128)(2,1)S(1)} %pad_maximum_fusion.3.refs_3_), channel_id=1, source_target_pairs={{0,8},{2,10},{4,12},{6,14},{8,16},{10,18},{12,20},{14,22},{16,24},... | collective-permute-start | bytes 2359304 | tf_op jit(solution)/shard_map/ppermute | solution.py:306
  199.7 34.4 %collective-permute-start.11 = (bf16[32,64,128]{2,1,0:T(8,128)(2,1)S(1)}, bf16[32,64,128]{2,1,0:T(8,128)(2,1)S(1)}, u32[]{:S(2)}, u32[]{:S(2)}) collective-permute-start(bf16[32,64,128]{2,1,0:T(8,128)(2,1)S(1)} %pad_maximum_fusion.4), channel_id=1, source_target_pairs={{0,8},{2,10},{4,12},{6,14},{8,16},{10,18},{12,20},{14,22},{16,24},... | collective-permute-start | bytes 1572872 | tf_op jit(solution)/shard_map/ppermute | solution.py:306
  213.4 64.9 %collective-permute-start.33 = (bf16[32,320,128]{2,1,0:T(8,128)(2,1)S(1)}, bf16[32,320,128]{2,1,0:T(8,128)(2,1)S(1)}, u32[]{:S(2)}, u32[]{:S(2)}) collective-permute-start(bf16[32,320,128]{2,1,0:T(8,128)(2,1)S(1)} %pad_maximum_fusion.refs_1_), channel_id=1, source_target_pairs={{0,1},{1,0},{2,3},{3,2},{4,5},{5,4},{6,7},{7,6},{8,9},{9,8},{10,11... | collective-permute-start | bytes 7864328 | tf_op jit(solution)/shard_map/ppermute | solution.py:361
  213.5 28.3 %collective-permute-start.12 = (bf16[32,64,128]{2,1,0:T(8,128)(2,1)S(1)}, bf16[32,64,128]{2,1,0:T(8,128)(2,1)S(1)}, u32[]{:S(2)}, u32[]{:S(2)}) collective-permute-start(bf16[32,64,128]{2,1,0:T(8,128)(2,1)S(1)} %pad_maximum_fusion.5), channel_id=1, source_target_pairs={{0,24},{2,26},{4,28},{6,30},{8,0},{10,2},{12,4},{14,6},{16,8},{18,... | collective-permute-start | bytes 1572872 | tf_op jit(solution)/shard_map/ppermute | solution.py:306
  224.7 17.5 %collective-permute-start.21 = (bf16[32,16,2,128]{3,2,1,0:T(2,128)(2,1)S(1)}, bf16[32,16,2,128]{3,2,1,0:T(2,128)(2,1)S(1)}, u32[]{:S(2)}, u32[]{:S(2)}) collective-permute-start(bf16[32,16,2,128]{3,2,1,0:T(2,128)(2,1)S(1)} %get-tuple-element.52), channel_id=1, source_target_pairs={{0,2},{2,0},{4,6},{6,4},{8,10},{10,8},{12,14},{14,12},{16,18},{18,... | collective-permute-start | bytes 786440 | tf_op jit(solution)/shard_map/ppermute | solution.py:303
  242.1 44.8 %collective-permute-start.13 = (bf16[32,64,128]{2,1,0:T(8,128)(2,1)S(1)}, bf16[32,64,128]{2,1,0:T(8,128)(2,1)S(1)}, u32[]{:S(2)}, u32[]{:S(2)}) collective-permute-start(bf16[32,64,128]{2,1,0:T(8,128)(2,1)S(1)} %add_convert_fusion.refs_0_), channel_id=1, source_target_pairs={{0,1},{1,0},{2,3},{3,2},{4,5},{5,4},{6,7},{7,6},{8,9},{9,8},{10,11... | collective-permute-start | bytes 1572872 | tf_op jit(solution)/shard_map/ppermute | solution.py:361
  242.3 39.9 %collective-permute-start.24 = (bf16[32,128,128]{2,1,0:T(8,128)(2,1)S(1)}, bf16[32,128,128]{2,1,0:T(8,128)(2,1)S(1)}, u32[]{:S(2)}, u32[]{:S(2)}) collective-permute-start(bf16[32,128,128]{2,1,0:T(8,128)(2,1)S(1)} %pad_maximum_fusion.2.refs_1_), channel_id=1, source_target_pairs={{0,1},{1,0},{2,3},{3,2},{4,5},{5,4},{6,7},{7,6},{8,9},{9,8},{10,11... | collective-permute-start | bytes 3145736 | tf_op jit(solution)/shard_map/ppermute | solution.py:361
  (46 other events, 402.7 us)

commit v4 on v3

--- a/solution.py
+++ b/solution.py
@@ -11,7 +11,7 @@
 
 H = 128
 UNITS = 8
-PARTS = (5, 2, 1)
+PARTS = (4, 2, 1, 1)
 VMEM_BYTES = 24 << 20
 
 
@@ -312,10 +312,14 @@
 
     last = len(chunks) - 1
     begin, tail = chunks[last]
-    own = regroup_own(visibilities, width, begin, group)
+    early, part = chunks[last - 1]
+    first = lax.dynamic_slice_in_dim(visibilities, place * width + early, part, 1)
+    first = sides(first)
+    own = regroup_own(visibilities, width, early, group)
     firsts = sides(own)
     picks = [(p, offset, size) for offset, size in chunks for p in range(1, group)] + [(0, begin, tail)]
-    away = regroup(visibilities, picks, width, group)
+    away = regroup(visibilities, picks[: group - 1], width, group)
+    away += regroup(visibilities, picks[group - 1 :], width, group)
     others = []
     for n in range(len(chunks)):
         near = []
@@ -350,6 +354,9 @@
     result = None
     for n, (offset, size) in enumerate(chunks):
         if n < last:
+            if n == last - 1:
+                firsts = [jnp.swapaxes(x, 0, 1).reshape(size, 2 * rows, svd) for x in first]
+                offset = 0
             mixed = mix(matrix, firsts, others[n], offset, unit, size)
             back = returned(mixed)
             joined = jnp.concatenate(back, axis=1)

time: 290 us -> 317 us (1.093)
  waiting for transfers between devices: 144 us -> 177 us
  other arithmetic: 26.2 us -> 18.8 us
  starting transfers between devices: 47.3 us -> 51.7 us
    ppermute x20 -> x26, waiting for transfers between devices: 28.7 us -> 65.3 us  [swap(): return lax.ppermute(x, 'ma', [(i, i ^ bits) for i in range(count)])]
    ppermute x11 -> x15, waiting for transfers between devices: 115 us -> 111 us  [shift(): lax.ppermute(x, 'ma', [(i, (i + by * group) % count) for i in range(count)])]
    unnamed x72 -> x60, local copies, waits for them, and re-layouts: 6.93 us -> 3.49 us
    ppermute x11 -> x15, starting transfers between devices: 19.2 us -> 22.4 us  [shift(): lax.ppermute(x, 'ma', [(i, (i + by * group) % count) for i in range(count)])]
    pallas_call x1 -> x2, Pallas kernels: 4.63 us -> 6.98 us  [regroup(): pl.pallas_call(kernel, out_shape=[jax.ShapeDtypeStruct(shape, visibilitie...]
    pallas_call x2 -> x3, Pallas kernels: 7.43 us -> 5.85 us  [mix(): pl.pallas_call(kernel, grid=(size // unit,), out_shape=[jax.ShapeDtypeStr...]
    pallas_call x2 -> x3, Pallas kernels: 6.35 us -> 7.61 us  [project(): pl.pallas_call(kernel, grid=(rows // step,), out_shape=out_shape, in_spec...]
    ppermute x20 -> x26, starting transfers between devices: 27.5 us -> 28.5 us  [swap(): return lax.ppermute(x, 'ma', [(i, i ^ bits) for i in range(count)])]
  transfers between devices with their start and end apart: 34 -> 45, of which waited for: 11 -> 16; matrix products, arithmetic and copies ran while one was open for 11% -> 8% of each run, Pallas kernels for 19% -> 18%
where the time goes in v4:
time: 317 us; the launch traced here: 316 us
  waiting for transfers between devices  177 us (56%)
  Pallas kernels  57.3 us (18%)
  starting transfers between devices  51.7 us (16%)
  other arithmetic  18.8 us (6%)
  local copies, waits for them, and re-layouts  7.7 us (2%)
    ppermute x15, waiting for transfers between devices, shift(): lax.ppermute(x, 'ma', [(i, (i + by * group) % count) for i in range(count)])  111 us
    ppermute x26, waiting for transfers between devices, swap(): return lax.ppermute(x, 'ma', [(i, i ^ bits) for i in range(count)])  65.3 us
    pallas_call x1, Pallas kernels, arrange_basis(): pl.pallas_call(kernel, grid=(rows,), out_shape=[jax.ShapeDtypeStruct((row...  32.1 us
    ppermute x26, starting transfers between devices, swap(): return lax.ppermute(x, 'ma', [(i, i ^ bits) for i in range(count)])  28.5 us
    ppermute x15, starting transfers between devices, shift(): lax.ppermute(x, 'ma', [(i, (i + by * group) % count) for i in range(count)])  22.4 us
    sin x2, other arithmetic, waves(): return (jnp.cos(phases), jnp.sin(phases))  11.8 us
    pallas_call x3, Pallas kernels, project(): pl.pallas_call(kernel, grid=(rows // step,), out_shape=out_shape, in_spec...  7.61 us
    pallas_call x2, Pallas kernels, regroup(): pl.pallas_call(kernel, out_shape=[jax.ShapeDtypeStruct(shape, visibilitie...  6.98 us
  transfers between devices with their start and end apart: 45, of which 16 were waited for; matrix products, arithmetic and copies ran while one was open for 8% of the time, Pallas kernels for 18%

profile of v4, /device:TPU:0, one launch (start us, length us, event | category | flops | bytes accessed | tf_op | source)
XLA Modules:
  0.0 316.1 jit_solution(6322676393385066913)
XLA Ops:
  15.7 8.5 %fusion.29 = (f32[768,512]{1,0:T(8,128)S(1)}, f32[768,512]{1,0:T(8,128)}) fusion(s32[768]{0:T(1024)S(1)} %get-tuple-element.109, s32[768]{0:T(1024)S(1)} %get-tuple-element.110, pred[768]{0:T(1024)(128)(4,1)S(1)} %fusion.52, s32[768]{0:T(1024)S(1)} %get-tuple-element.106, s32[768]{0:T(1024)S(1)} %get-tuple-element.108, ...), kind=kLoop, calls=%fused_computation.87 | loop fusion | flops 19660800 | bytes 3173380 | tf_op jit(solution)/shard_map/sin | solution.py:85
  31.1 10.3 %collective-permute-done.3 = s32[512]{0:T(512)S(1)} collective-permute-done((s32[512]{0:T(512)S(1)}, s32[512]{0:T(512)S(1)}, u32[]{:S(2)}, u32[]{:S(2)}) %collective-permute-start.3) | collective-permute-done | bytes 2080 | tf_op jit(solution)/shard_map/ppermute | solution.py:303
  47.8 4.5 %regroup.2 = (bf16[16,32,2,128]{3,2,1,0:T(2,128)(2,1)}, bf16[16,32,2,128]{3,2,1,0:T(2,128)(2,1)}, bf16[16,32,2,128]{3,2,1,0:T(2,128)(2,1)}, bf16[8,32,2,128]{3,2...) custom-call(bf16[32,256,2,128]{3,2,1,0:T(2,128)(2,1)} %src.5), custom_call_target="tpu_custom_call" | custom-call | bytes 3407872 | tf_op jit(solution)/shard_map/regroup/pallas_call | solution.py:42
  56.6 11.7 %collective-permute-done.16 = bf16[8,64,128]{2,1,0:T(8,128)(2,1)S(1)} collective-permute-done((bf16[8,64,128]{2,1,0:T(8,128)(2,1)}, bf16[8,64,128]{2,1,0:T(8,128)(2,1)S(1)}, u32[]{:S(2)}, u32[]{:S(2)}) %collective-permute-start.16) | collective-permute-done | bytes 131104 | tf_op jit(solution)/shard_map/ppermute | solution.py:303
  71.4 4.4 %collective-permute-done.18 = bf16[8,64,128]{2,1,0:T(8,128)(2,1)S(1)} collective-permute-done((bf16[8,64,128]{2,1,0:T(8,128)(2,1)}, bf16[8,64,128]{2,1,0:T(8,128)(2,1)S(1)}, u32[]{:S(2)}, u32[]{:S(2)}) %collective-permute-start.18) | collective-permute-done | bytes 131104 | tf_op jit(solution)/shard_map/ppermute | solution.py:303
  81.1 4.7 %collective-permute-start.29 = (bf16[16,64,128]{2,1,0:T(8,128)(2,1)S(1)}, bf16[16,64,128]{2,1,0:T(8,128)(2,1)S(1)}, u32[]{:S(2)}, u32[]{:S(2)}) collective-permute-start(bf16[16,64,128]{2,1,0:T(8,128)(2,1)S(1)} %bitcast.108), channel_id=1, source_target_pairs={{0,6},{2,4},{4,2},{6,0},{8,14},{10,12},{12,10},{14,8},{16,22},{18,... | collective-permute-start | bytes 786440 | tf_op jit(solution)/shard_map/ppermute | solution.py:303
  85.8 5.9 %collective-permute-done.6 = bf16[8,64,128]{2,1,0:T(8,128)(2,1)S(1)} collective-permute-done((bf16[8,64,128]{2,1,0:T(8,128)(2,1)S(1)}, bf16[8,64,128]{2,1,0:T(8,128)(2,1)S(1)}, u32[]{:S(2)}, u32[]{:S(2)}) %collective-permute-start.6) | collective-permute-done | bytes 131104 | tf_op jit(solution)/shard_map/ppermute | solution.py:303
  91.7 3.8 %collective-permute-start.20 = (bf16[3,8,64,128]{3,2,1,0:T(8,128)(2,1)S(1)}, bf16[3,8,64,128]{3,2,1,0:T(8,128)(2,1)S(1)}, u32[]{:S(2)}, u32[]{:S(2)}) collective-permute-start(bf16[3,8,64,128]{3,2,1,0:T(8,128)(2,1)S(1)} %pad_maximum_fusion.8.refs_3_), channel_id=1, source_target_pairs={{0,24},{2,26},{4,28},{6,30},{8,0},{10,2},{12,4},{14,6},{16,8},{18,... | collective-permute-start | bytes 1179656 | tf_op jit(solution)/shard_map/ppermute | solution.py:306
  95.5 3.8 %collective-permute-start.40 = (bf16[3,32,64,128]{3,2,1,0:T(8,128)(2,1)S(1)}, bf16[3,32,64,128]{3,2,1,0:T(8,128)(2,1)S(1)}, u32[]{:S(2)}, u32[]{:S(2)}) collective-permute-start(bf16[3,32,64,128]{3,2,1,0:T(8,128)(2,1)S(1)} %pad_maximum_fusion.1.refs_3_), channel_id=1, source_target_pairs={{0,24},{2,26},{4,28},{6,30},{8,0},{10,2},{12,4},{14,6},{16,8},{18,... | collective-permute-start | bytes 4718600 | tf_op jit(solution)/shard_map/ppermute | solution.py:306
  101.2 4.3 %collective-permute-done.19.refs_4_ = bf16[3,8,64,128]{3,2,1,0:T(8,128)(2,1)S(1)} collective-permute-done((bf16[3,8,64,128]{3,2,1,0:T(8,128)(2,1)S(1)}, bf16[3,8,64,128]{3,2,1,0:T(8,128)(2,1)S(1)}, u32[]{:S(2)}, u32[]{:S(2)}) %collective-permute-start.19) | collective-permute-done | bytes 393248 | tf_op jit(solution)/shard_map/ppermute | solution.py:306
  106.7 24.4 %collective-permute-done.20.refs_5_ = bf16[3,8,64,128]{3,2,1,0:T(8,128)(2,1)S(1)} collective-permute-done((bf16[3,8,64,128]{3,2,1,0:T(8,128)(2,1)S(1)}, bf16[3,8,64,128]{3,2,1,0:T(8,128)(2,1)S(1)}, u32[]{:S(2)}, u32[]{:S(2)}) %collective-permute-start.20) | collective-permute-done | bytes 393248 | tf_op jit(solution)/shard_map/ppermute | solution.py:306
  132.9 6.1 %collective-permute-done.8 = bf16[3,32,8,2,128]{4,3,2,1,0:T(2,128)(2,1)S(1)} collective-permute-done((bf16[3,32,8,2,128]{4,3,2,1,0:T(2,128)(2,1)S(1)}, bf16[3,32,8,2,128]{4,3,2,1,0:T(2,128)(2,1)S(1)}, u32[]{:S(2)}, u32[]{:S(2)}) %collective-permute-start.8) | collective-permute-done | bytes 393248 | tf_op jit(solution)/shard_map/ppermute | solution.py:303
  140.2 54.1 %collective-permute-done.25.refs_1_ = bf16[48,64,128]{2,1,0:T(8,128)(2,1)S(1)} collective-permute-done((bf16[48,64,128]{2,1,0:T(8,128)(2,1)S(1)}, bf16[48,64,128]{2,1,0:T(8,128)(2,1)S(1)}, u32[]{:S(2)}, u32[]{:S(2)}) %collective-permute-start.25) | collective-permute-done | bytes 786464 | tf_op jit(solution)/shard_map/ppermute | solution.py:306
  195.3 6.6 %collective-permute-done.26.refs_2_ = bf16[48,64,128]{2,1,0:T(8,128)(2,1)S(1)} collective-permute-done((bf16[48,64,128]{2,1,0:T(8,128)(2,1)S(1)}, bf16[48,64,128]{2,1,0:T(8,128)(2,1)S(1)}, u32[]{:S(2)}, u32[]{:S(2)}) %collective-permute-start.26) | collective-permute-done | bytes 786464 | tf_op jit(solution)/shard_map/ppermute | solution.py:306
  203.1 3.5 %mix.5 = (bf16[32,32,2,128]{3,2,1,0:T(2,128)(2,1)S(1)}, bf16[32,32,2,128]{3,2,1,0:T(2,128)(2,1)S(1)}, bf16[32,32,2,128]{3,2,1,0:T(2,128)(2,1)S(1)}, bf16[32,32,2,128]{3,2,1,0:T(2,128)(2,1)S(1)}) custom-call(bf16[256,768]{1,0:T(8,128)(2,1)S(1)} %fusion.13.t_ref, bf16[48,64,128]{2,1,0:T(8,128)(2,1)S(1)} %bitcast.62, ...), custom_call_target="tpu_custom_call" | custom-call | flops 1610612736 | bytes 8781824 | tf_op jit(solution)/shard_map/mix/pallas_call | solution.py:130
  209.8 3.8 %collective-permute-start.31 = (bf16[3,16,64,128]{3,2,1,0:T(8,128)(2,1)S(1)}, bf16[3,16,64,128]{3,2,1,0:T(8,128)(2,1)S(1)}, u32[]{:S(2)}, u32[]{:S(2)}) collective-permute-start(bf16[3,16,64,128]{3,2,1,0:T(8,128)(2,1)S(1)} %pad_maximum_fusion.3.refs_3_), channel_id=1, source_target_pairs={{0,24},{2,26},{4,28},{6,30},{8,0},{10,2},{12,4},{14,6},{16,8},{18,... | collective-permute-start | bytes 2359304 | tf_op jit(solution)/shard_map/ppermute | solution.py:306
  214.6 6.8 %collective-permute-done.41 = bf16[32,32,2,128]{3,2,1,0:T(2,128)(2,1)S(1)} collective-permute-done((bf16[32,32,2,128]{3,2,1,0:T(2,128)(2,1)S(1)}, bf16[32,32,2,128]{3,2,1,0:T(2,128)(2,1)S(1)}, u32[]{:S(2)}, u32[]{:S(2)}) %collective-permute-start.41) | collective-permute-done | bytes 524320 | tf_op jit(solution)/shard_map/ppermute | solution.py:303
  221.5 9.2 %collective-permute-done.42 = bf16[32,32,2,128]{3,2,1,0:T(2,128)(2,1)S(1)} collective-permute-done((bf16[32,32,2,128]{3,2,1,0:T(2,128)(2,1)S(1)}, bf16[32,32,2,128]{3,2,1,0:T(2,128)(2,1)S(1)}, u32[]{:S(2)}, u32[]{:S(2)}) %collective-permute-start.42) | collective-permute-done | bytes 524320 | tf_op jit(solution)/shard_map/ppermute | solution.py:303
  232.4 4.2 %collective-permute-done.23 = bf16[32,8,2,128]{3,2,1,0:T(2,128)(2,1)S(1)} collective-permute-done((bf16[32,8,2,128]{3,2,1,0:T(2,128)(2,1)S(1)}, bf16[32,8,2,128]{3,2,1,0:T(2,128)(2,1)S(1)}, u32[]{:S(2)}, u32[]{:S(2)}) %collective-permute-start.23) | collective-permute-done | bytes 131104 | tf_op jit(solution)/shard_map/ppermute | solution.py:303
  237.2 10.6 %collective-permute-done.31.refs_5_ = bf16[3,16,64,128]{3,2,1,0:T(8,128)(2,1)S(1)} collective-permute-done((bf16[3,16,64,128]{3,2,1,0:T(8,128)(2,1)S(1)}, bf16[3,16,64,128]{3,2,1,0:T(8,128)(2,1)S(1)}, u32[]{:S(2)}, u32[]{:S(2)}) %collective-permute-start.31) | collective-permute-done | bytes 786464 | tf_op jit(solution)/shard_map/ppermute | solution.py:306
  251.2 7.9 %collective-permute-done.11 = bf16[32,64,128]{2,1,0:T(8,128)(2,1)S(1)} collective-permute-done((bf16[32,64,128]{2,1,0:T(8,128)(2,1)S(1)}, bf16[32,64,128]{2,1,0:T(8,128)(2,1)S(1)}, u32[]{:S(2)}, u32[]{:S(2)}) %collective-permute-start.11) | collective-permute-done | bytes 524320 | tf_op jit(solution)/shard_map/ppermute | solution.py:306
  259.4 3.4 %collective-permute-done.12 = bf16[32,64,128]{2,1,0:T(8,128)(2,1)S(1)} collective-permute-done((bf16[32,64,128]{2,1,0:T(8,128)(2,1)S(1)}, bf16[32,64,128]{2,1,0:T(8,128)(2,1)S(1)}, u32[]{:S(2)}, u32[]{:S(2)}) %collective-permute-start.12) | collective-permute-done | bytes 524320 | tf_op jit(solution)/shard_map/ppermute | solution.py:306
  264.5 6.5 %collective-permute-done.33 = bf16[32,16,2,128]{3,2,1,0:T(2,128)(2,1)S(1)} collective-permute-done((bf16[32,16,2,128]{3,2,1,0:T(2,128)(2,1)S(1)}, bf16[32,16,2,128]{3,2,1,0:T(2,128)(2,1)S(1)}, u32[]{:S(2)}, u32[]{:S(2)}) %collective-permute-start.33) | collective-permute-done | bytes 262176 | tf_op jit(solution)/shard_map/ppermute | solution.py:303
  274.7 32.1 %arrange.1 = (bf16[32,256,512]{2,1,0:T(8,128)(2,1)S(1)}, bf16[32,256,256]{2,1,0:T(8,128)(2,1)S(1)}, bf16[32,256,128]{2,1,0:T(8,128)(2,1)S(1)}, bf16[32,256,128]{2,1,0:T(8,128)(2,1)S(1)}) custom-call(bf16[32,128,2,512]{3,2,1,0:T(2,128)(2,1)S(1)} %copy-done.1), custom_call_target="tpu_custom_call" | custom-call | flops 17179869184 | bytes 25165824 | tf_op jit(solution)/shard_map/arrange/pallas_call | solution.py:214
  (181 shorter events, 74.0 us)
Async XLA Ops:
  0.8 26.4 %collective-permute-start = (s32[512]{0:T(512)S(1)}, s32[512]{0:T(512)S(1)}, u32[]{:S(2)}, u32[]{:S(2)}) collective-permute-start(s32[512]{0:T(512)S(1)} %dynamic_update_slice.5), channel_id=1, source_target_pairs={{0,8},{2,10},{4,12},{6,14},{8,16},{10,18},{12,20},{14,22},{16,24},... | collective-permute-start | bytes 6152 | tf_op jit(solution)/shard_map/ppermute | solution.py:306
  3.9 25.1 %collective-permute-start.1 = (s32[512]{0:T(512)S(1)}, s32[512]{0:T(512)S(1)}, u32[]{:S(2)}, u32[]{:S(2)}) collective-permute-start(s32[512]{0:T(512)S(1)} %dynamic_update_slice.5), channel_id=1, source_target_pairs={{0,16},{2,18},{4,20},{6,22},{8,24},{10,26},{12,28},{14,30},{16,0},... | collective-permute-start | bytes 6152 | tf_op jit(solution)/shard_map/ppermute | solution.py:306
  6.5 24.0 %collective-permute-start.2 = (s32[512]{0:T(512)S(1)}, s32[512]{0:T(512)S(1)}, u32[]{:S(2)}, u32[]{:S(2)}) collective-permute-start(s32[512]{0:T(512)S(1)} %dynamic_update_slice.5), channel_id=1, source_target_pairs={{0,24},{2,26},{4,28},{6,30},{8,0},{10,2},{12,4},{14,6},{16,8},{18,... | collective-permute-start | bytes 6152 | tf_op jit(solution)/shard_map/ppermute | solution.py:306
  8.8 46.0 %collective-permute-start.14 = (bf16[32,8,2,128]{3,2,1,0:T(2,128)(2,1)S(1)}, bf16[32,8,2,128]{3,2,1,0:T(2,128)(2,1)S(1)}, u32[]{:S(2)}, u32[]{:S(2)}) collective-permute-start(bf16[32,8,2,128]{3,2,1,0:T(2,128)(2,1)S(1)} %constant_dynamic-slice_fusion), channel_id=1, source_target_pairs={{0,8},{2,10},{4,12},{6,14},{8,16},{10,18},{12,20},{14,22},{16,24},... | collective-permute-start | bytes 393224 | tf_op jit(solution)/shard_map/ppermute | solution.py:306
  9.6 46.5 %collective-permute-start.15 = (bf16[32,8,2,128]{3,2,1,0:T(2,128)(2,1)S(1)}, bf16[32,8,2,128]{3,2,1,0:T(2,128)(2,1)S(1)}, u32[]{:S(2)}, u32[]{:S(2)}) collective-permute-start(bf16[32,8,2,128]{3,2,1,0:T(2,128)(2,1)S(1)} %constant_dynamic-slice_fusion), channel_id=1, source_target_pairs={{0,24},{2,26},{4,28},{6,30},{8,0},{10,2},{12,4},{14,6},{16,8},{18,... | collective-permute-start | bytes 393224 | tf_op jit(solution)/shard_map/ppermute | solution.py:306
  27.3 48.6 %collective-permute-start.36 = (bf16[32,64,128]{2,1,0:T(8,128)(2,1)}, bf16[32,64,128]{2,1,0:T(8,128)(2,1)S(1)}, u32[]{:S(2)}, u32[]{:S(2)}) collective-permute-start(bf16[32,64,128]{2,1,0:T(8,128)(2,1)} %bitcast.107), channel_id=1, source_target_pairs={{0,2},{2,0},{4,6},{6,4},{8,10},{10,8},{12,14},{14,12},{16,18},{18,... | collective-permute-start | bytes 1572872 | tf_op jit(solution)/shard_map/ppermute | solution.py:303
  29.0 48.5 %collective-permute-start.37 = (bf16[32,64,128]{2,1,0:T(8,128)(2,1)}, bf16[32,64,128]{2,1,0:T(8,128)(2,1)}, u32[]{:S(2)}, u32[]{:S(2)}) collective-permute-start(bf16[32,64,128]{2,1,0:T(8,128)(2,1)} %bitcast.106), channel_id=1, source_target_pairs={{0,4},{2,6},{4,0},{6,2},{8,12},{10,14},{12,8},{14,10},{16,20},{18,... | collective-permute-start | bytes 1572872 | tf_op jit(solution)/shard_map/ppermute | solution.py:303
  52.3 27.1 %collective-permute-start.38 = (bf16[32,64,128]{2,1,0:T(8,128)(2,1)}, bf16[32,64,128]{2,1,0:T(8,128)(2,1)S(1)}, u32[]{:S(2)}, u32[]{:S(2)}) collective-permute-start(bf16[32,64,128]{2,1,0:T(8,128)(2,1)} %bitcast.105), channel_id=1, source_target_pairs={{0,6},{2,4},{4,2},{6,0},{8,14},{10,12},{12,10},{14,8},{16,22},{18,... | collective-permute-start | bytes 1572872 | tf_op jit(solution)/shard_map/ppermute | solution.py:303
  70.3 25.2 %collective-permute-start.27 = (bf16[16,64,128]{2,1,0:T(8,128)(2,1)S(1)}, bf16[16,64,128]{2,1,0:T(8,128)(2,1)S(1)}, u32[]{:S(2)}, u32[]{:S(2)}) collective-permute-start(bf16[16,64,128]{2,1,0:T(8,128)(2,1)S(1)} %bitcast.110), channel_id=1, source_target_pairs={{0,2},{2,0},{4,6},{6,4},{8,10},{10,8},{12,14},{14,12},{16,18},{18,... | collective-permute-start | bytes 786440 | tf_op jit(solution)/shard_map/ppermute | solution.py:303
  91.7 39.5 %collective-permute-start.20 = (bf16[3,8,64,128]{3,2,1,0:T(8,128)(2,1)S(1)}, bf16[3,8,64,128]{3,2,1,0:T(8,128)(2,1)S(1)}, u32[]{:S(2)}, u32[]{:S(2)}) collective-permute-start(bf16[3,8,64,128]{3,2,1,0:T(8,128)(2,1)S(1)} %pad_maximum_fusion.8.refs_3_), channel_id=1, source_target_pairs={{0,24},{2,26},{4,28},{6,30},{8,0},{10,2},{12,4},{14,6},{16,8},{18,... | collective-permute-start | bytes 1179656 | tf_op jit(solution)/shard_map/ppermute | solution.py:306
  95.5 107.5 %collective-permute-start.39 = (bf16[3,32,64,128]{3,2,1,0:T(8,128)(2,1)S(1)}, bf16[3,32,64,128]{3,2,1,0:T(8,128)(2,1)S(1)}, u32[]{:S(2)}, u32[]{:S(2)}) collective-permute-start(bf16[3,32,64,128]{3,2,1,0:T(8,128)(2,1)S(1)} %pad_maximum_fusion.1.refs_3_), channel_id=1, source_target_pairs={{0,8},{2,10},{4,12},{6,14},{8,16},{10,18},{12,20},{14,22},{16,24},... | collective-permute-start | bytes 4718600 | tf_op jit(solution)/shard_map/ppermute | solution.py:306
  95.5 107.6 %collective-permute-start.40 = (bf16[3,32,64,128]{3,2,1,0:T(8,128)(2,1)S(1)}, bf16[3,32,64,128]{3,2,1,0:T(8,128)(2,1)S(1)}, u32[]{:S(2)}, u32[]{:S(2)}) collective-permute-start(bf16[3,32,64,128]{3,2,1,0:T(8,128)(2,1)S(1)} %pad_maximum_fusion.1.refs_3_), channel_id=1, source_target_pairs={{0,24},{2,26},{4,28},{6,30},{8,0},{10,2},{12,4},{14,6},{16,8},{18,... | collective-permute-start | bytes 4718600 | tf_op jit(solution)/shard_map/ppermute | solution.py:306
  101.1 93.1 %collective-permute-start.25 = (bf16[48,64,128]{2,1,0:T(8,128)(2,1)S(1)}, bf16[48,64,128]{2,1,0:T(8,128)(2,1)S(1)}, u32[]{:S(2)}, u32[]{:S(2)}) collective-permute-start(bf16[48,64,128]{2,1,0:T(8,128)(2,1)S(1)} %bitcast.60), channel_id=1, source_target_pairs={{0,8},{2,10},{4,12},{6,14},{8,16},{10,18},{12,20},{14,22},{16,24},... | collective-permute-start | bytes 2359304 | tf_op jit(solution)/shard_map/ppermute | solution.py:306
  105.5 96.4 %collective-permute-start.26 = (bf16[48,64,128]{2,1,0:T(8,128)(2,1)S(1)}, bf16[48,64,128]{2,1,0:T(8,128)(2,1)S(1)}, u32[]{:S(2)}, u32[]{:S(2)}) collective-permute-start(bf16[48,64,128]{2,1,0:T(8,128)(2,1)S(1)} %bitcast.61), channel_id=1, source_target_pairs={{0,24},{2,26},{4,28},{6,30},{8,0},{10,2},{12,4},{14,6},{16,8},{18,... | collective-permute-start | bytes 2359304 | tf_op jit(solution)/shard_map/ppermute | solution.py:306
  138.9 68.5 %collective-permute-start.9 = (bf16[3,32,8,2,128]{4,3,2,1,0:T(2,128)(2,1)S(1)}, bf16[3,32,8,2,128]{4,3,2,1,0:T(2,128)(2,1)S(1)}, u32[]{:S(2)}, u32[]{:S(2)}) collective-permute-start(bf16[3,32,8,2,128]{4,3,2,1,0:T(2,128)(2,1)S(1)} %get-tuple-element.53), channel_id=1, source_target_pairs={{0,4},{2,6},{4,0},{6,2},{8,12},{10,14},{12,8},{14,10},{16,20},{18,... | collective-permute-start | bytes 1179656 | tf_op jit(solution)/shard_map/ppermute | solution.py:303
  207.5 23.2 %collective-permute-start.42 = (bf16[32,32,2,128]{3,2,1,0:T(2,128)(2,1)S(1)}, bf16[32,32,2,128]{3,2,1,0:T(2,128)(2,1)S(1)}, u32[]{:S(2)}, u32[]{:S(2)}) collective-permute-start(bf16[32,32,2,128]{3,2,1,0:T(2,128)(2,1)S(1)} %get-tuple-element.77), channel_id=1, source_target_pairs={{0,4},{2,6},{4,0},{6,2},{8,12},{10,14},{12,8},{14,10},{16,20},{18,... | collective-permute-start | bytes 1572872 | tf_op jit(solution)/shard_map/ppermute | solution.py:303
  209.8 26.9 %collective-permute-start.30 = (bf16[3,16,64,128]{3,2,1,0:T(8,128)(2,1)S(1)}, bf16[3,16,64,128]{3,2,1,0:T(8,128)(2,1)S(1)}, u32[]{:S(2)}, u32[]{:S(2)}) collective-permute-start(bf16[3,16,64,128]{3,2,1,0:T(8,128)(2,1)S(1)} %pad_maximum_fusion.3.refs_3_), channel_id=1, source_target_pairs={{0,8},{2,10},{4,12},{6,14},{8,16},{10,18},{12,20},{14,22},{16,24},... | collective-permute-start | bytes 2359304 | tf_op jit(solution)/shard_map/ppermute | solution.py:306
  209.8 38.0 %collective-permute-start.31 = (bf16[3,16,64,128]{3,2,1,0:T(8,128)(2,1)S(1)}, bf16[3,16,64,128]{3,2,1,0:T(8,128)(2,1)S(1)}, u32[]{:S(2)}, u32[]{:S(2)}) collective-permute-start(bf16[3,16,64,128]{3,2,1,0:T(8,128)(2,1)S(1)} %pad_maximum_fusion.3.refs_3_), channel_id=1, source_target_pairs={{0,24},{2,26},{4,28},{6,30},{8,0},{10,2},{12,4},{14,6},{16,8},{18,... | collective-permute-start | bytes 2359304 | tf_op jit(solution)/shard_map/ppermute | solution.py:306
  221.4 37.7 %collective-permute-start.11 = (bf16[32,64,128]{2,1,0:T(8,128)(2,1)S(1)}, bf16[32,64,128]{2,1,0:T(8,128)(2,1)S(1)}, u32[]{:S(2)}, u32[]{:S(2)}) collective-permute-start(bf16[32,64,128]{2,1,0:T(8,128)(2,1)S(1)} %pad_maximum_fusion.4), channel_id=1, source_target_pairs={{0,8},{2,10},{4,12},{6,14},{8,16},{10,18},{12,20},{14,22},{16,24},... | collective-permute-start | bytes 1572872 | tf_op jit(solution)/shard_map/ppermute | solution.py:306
  230.7 32.1 %collective-permute-start.12 = (bf16[32,64,128]{2,1,0:T(8,128)(2,1)S(1)}, bf16[32,64,128]{2,1,0:T(8,128)(2,1)S(1)}, u32[]{:S(2)}, u32[]{:S(2)}) collective-permute-start(bf16[32,64,128]{2,1,0:T(8,128)(2,1)S(1)} %pad_maximum_fusion.5), channel_id=1, source_target_pairs={{0,24},{2,26},{4,28},{6,30},{8,0},{10,2},{12,4},{14,6},{16,8},{18,... | collective-permute-start | bytes 1572872 | tf_op jit(solution)/shard_map/ppermute | solution.py:306
  236.6 70.2 %collective-permute-start.44 = (bf16[32,256,128]{2,1,0:T(8,128)(2,1)S(1)}, bf16[32,256,128]{2,1,0:T(8,128)(2,1)S(1)}, u32[]{:S(2)}, u32[]{:S(2)}) collective-permute-start(bf16[32,256,128]{2,1,0:T(8,128)(2,1)S(1)} %pad_maximum_fusion.refs_1_), channel_id=1, source_target_pairs={{0,1},{1,0},{2,3},{3,2},{4,5},{5,4},{6,7},{7,6},{8,9},{9,8},{10,11... | collective-permute-start | bytes 6291464 | tf_op jit(solution)/shard_map/ppermute | solution.py:368
  236.7 75.9 %collective-permute-start.24 = (bf16[32,64,128]{2,1,0:T(8,128)(2,1)S(1)}, bf16[32,64,128]{2,1,0:T(8,128)(2,1)S(1)}, u32[]{:S(2)}, u32[]{:S(2)}) collective-permute-start(bf16[32,64,128]{2,1,0:T(8,128)(2,1)S(1)} %pad_maximum_fusion.6.refs_1_), channel_id=1, source_target_pairs={{0,1},{1,0},{2,3},{3,2},{4,5},{5,4},{6,7},{7,6},{8,9},{9,8},{10,11... | collective-permute-start | bytes 1572872 | tf_op jit(solution)/shard_map/ppermute | solution.py:368
  264.5 50.0 %collective-permute-start.13 = (bf16[32,64,128]{2,1,0:T(8,128)(2,1)S(1)}, bf16[32,64,128]{2,1,0:T(8,128)(2,1)S(1)}, u32[]{:S(2)}, u32[]{:S(2)}) collective-permute-start(bf16[32,64,128]{2,1,0:T(8,128)(2,1)S(1)} %add_convert_fusion.refs_0_), channel_id=1, source_target_pairs={{0,1},{1,0},{2,3},{3,2},{4,5},{5,4},{6,7},{7,6},{8,9},{9,8},{10,11... | collective-permute-start | bytes 1572872 | tf_op jit(solution)/shard_map/ppermute | solution.py:368
  271.2 39.0 %collective-permute-start.35 = (bf16[32,128,128]{2,1,0:T(8,128)(2,1)S(1)}, bf16[32,128,128]{2,1,0:T(8,128)(2,1)S(1)}, u32[]{:S(2)}, u32[]{:S(2)}) collective-permute-start(bf16[32,128,128]{2,1,0:T(8,128)(2,1)S(1)} %pad_maximum_fusion.2.refs_1_), channel_id=1, source_target_pairs={{0,1},{1,0},{2,3},{3,2},{4,5},{5,4},{6,7},{7,6},{8,9},{9,8},{10,11... | collective-permute-start | bytes 3145736 | tf_op jit(solution)/shard_map/ppermute | solution.py:368
  (51 other events, 733.3 us)

commit v5 on v4

--- a/solution.py
+++ b/solution.py
@@ -100,7 +100,8 @@
     row = (at // 2) % rows
     block = lax.bitwise_xor((at // (2 * rows)) % group, place)
     side = at // (2 * rows * group)
-    return block * rows + row + jnp.where(side == 1, -H, jnp.where(side == 2, H, 0))
+    reach = H - 2 * H * (lax.axis_index("ch") % 2)
+    return block * rows + row + jnp.where(side == 1, -reach, jnp.where(side == 2, reach, 0))
 
 
 def mix(matrix, firsts, others, offset, unit, size):
@@ -305,9 +306,17 @@
     def shift(x, by):
         return lax.ppermute(x, "ma", [(i, (i + by * group) % count) for i in range(count)])
 
+    def cross(x, by):
+        pairs = []
+        for i in range(count):
+            for core in range(copies):
+                step = by * group * (1 - 2 * (core % 2))
+                pairs.append((i * copies + core, (i + step) % count * copies + core))
+        return lax.ppermute(x, ("ma", "ch"), pairs)
+
     def sides(x):
-        up = shift(x, 1)
-        down = shift(x, -1)
+        up = cross(x, 1)
+        down = cross(x, -1)
         return x, up, down
 
     last = len(chunks) - 1
@@ -348,8 +357,8 @@
     shares = mix_apart(matrix, away[-1], others[last])
     shares = returned(shares)
     kept, rise, fall = [jnp.concatenate([share[side] for share in shares], axis=1) for side in range(3)]
-    rise = shift(rise, 1)
-    fall = shift(fall, -1)
+    rise = cross(rise, 1)
+    fall = cross(fall, -1)
 
     result = None
     for n, (offset, size) in enumerate(chunks):

time: 317 us -> 309 us (0.975)
  waiting for transfers between devices: 177 us -> 147 us
  starting transfers between devices: 51.7 us -> 73.2 us
    ppermute x15 -> x3, waiting for transfers between devices: 111 us -> 0.01 us  [shift(): lax.ppermute(x, 'ma', [(i, (i + by * group) % count) for i in range(count)])]
    ppermute x0 -> x12, waiting for transfers between devices: none -> 92.9 us  [cross(): return lax.ppermute(x, ('ma', 'ch'), pairs)]
    ppermute x0 -> x12, starting transfers between devices: none -> 39.9 us  [cross(): return lax.ppermute(x, ('ma', 'ch'), pairs)]
    ppermute x15 -> x3, starting transfers between devices: 22.4 us -> 6.99 us  [shift(): lax.ppermute(x, 'ma', [(i, (i + by * group) % count) for i in range(count)])]
    ppermute x26, waiting for transfers between devices: 65.3 us -> 53.9 us  [swap(): return lax.ppermute(x, 'ma', [(i, i ^ bits) for i in range(count)])]
  transfers between devices with their start and end apart: 45 -> 45, of which waited for: 16 -> 17; matrix products, arithmetic and copies ran while one was open for 8% -> 8% of each run, Pallas kernels for 18% -> 18%
where the time goes in v5:
time: 309 us; the launch traced here: 308 us
  waiting for transfers between devices  147 us (48%)
  starting transfers between devices  73.2 us (24%)
  Pallas kernels  57.3 us (19%)
  other arithmetic  18.8 us (6%)
  local copies, waits for them, and re-layouts  7.7 us (2%)
  matrix products  3.11 us (1%)
    ppermute x12, waiting for transfers between devices, cross(): return lax.ppermute(x, ('ma', 'ch'), pairs)  92.9 us
    ppermute x26, waiting for transfers between devices, swap(): return lax.ppermute(x, 'ma', [(i, i ^ bits) for i in range(count)])  53.9 us
    ppermute x12, starting transfers between devices, cross(): return lax.ppermute(x, ('ma', 'ch'), pairs)  39.9 us
    pallas_call x1, Pallas kernels, arrange_basis(): pl.pallas_call(kernel, grid=(rows,), out_shape=[jax.ShapeDtypeStruct((row...  32.1 us
    ppermute x26, starting transfers between devices, swap(): return lax.ppermute(x, 'ma', [(i, i ^ bits) for i in range(count)])  25.6 us
    sin x2, other arithmetic, waves(): return (jnp.cos(phases), jnp.sin(phases))  11.8 us
    pallas_call x3, Pallas kernels, project(): pl.pallas_call(kernel, grid=(rows // step,), out_shape=out_shape, in_spec...  7.61 us
    ppermute x3, starting transfers between devices, shift(): lax.ppermute(x, 'ma', [(i, (i + by * group) % count) for i in range(count)])  6.99 us
  transfers between devices with their start and end apart: 45, of which 17 were waited for; matrix products, arithmetic and copies ran while one was open for 8% of the time, Pallas kernels for 18%

profile of v5, /device:TPU:0, one launch (start us, length us, event | category | flops | bytes accessed | tf_op | source)
XLA Modules:
  0.0 308.0 jit_solution(869641228080189702)
XLA Ops:
  15.7 8.6 %fusion.29 = (f32[768,512]{1,0:T(8,128)S(1)}, f32[768,512]{1,0:T(8,128)}) fusion(s32[768]{0:T(1024)S(1)} %get-tuple-element.109, s32[768]{0:T(1024)S(1)} %get-tuple-element.110, pred[768]{0:T(1024)(128)(4,1)S(1)} %fusion.52, s32[]{:T(128)S(6)} %sub.93, s32[]{:T(128)S(6)} %neg.2, s32[768]{0:T(1024)S(1)} %get-tuple-element.106, ...), kind=kLoop, calls=%fused_computation.87 | loop fusion | flops 19660800 | bytes 3173388 | tf_op jit(solution)/shard_map/sin | solution.py:85
  31.1 8.5 %collective-permute-done.3 = s32[512]{0:T(512)S(1)} collective-permute-done((s32[512]{0:T(512)S(1)}, s32[512]{0:T(512)S(1)}, u32[]{:S(2)}, u32[]{:S(2)}) %collective-permute-start.3) | collective-permute-done | bytes 2080 | tf_op jit(solution)/shard_map/ppermute | solution.py:304
  46.0 4.5 %regroup.2 = (bf16[16,32,2,128]{3,2,1,0:T(2,128)(2,1)}, bf16[16,32,2,128]{3,2,1,0:T(2,128)(2,1)}, bf16[16,32,2,128]{3,2,1,0:T(2,128)(2,1)}, bf16[8,32,2,128]{3,2...) custom-call(bf16[32,256,2,128]{3,2,1,0:T(2,128)(2,1)} %src.5), custom_call_target="tpu_custom_call" | custom-call | bytes 3407872 | tf_op jit(solution)/shard_map/regroup/pallas_call | solution.py:42
  54.8 10.3 %collective-permute-done.16 = bf16[8,64,128]{2,1,0:T(8,128)(2,1)S(1)} collective-permute-done((bf16[8,64,128]{2,1,0:T(8,128)(2,1)}, bf16[8,64,128]{2,1,0:T(8,128)(2,1)S(1)}, u32[]{:S(2)}, u32[]{:S(2)}) %collective-permute-start.16) | collective-permute-done | bytes 131104 | tf_op jit(solution)/shard_map/ppermute | solution.py:304
  68.7 3.9 %collective-permute-done.18 = bf16[8,64,128]{2,1,0:T(8,128)(2,1)S(1)} collective-permute-done((bf16[8,64,128]{2,1,0:T(8,128)(2,1)}, bf16[8,64,128]{2,1,0:T(8,128)(2,1)S(1)}, u32[]{:S(2)}, u32[]{:S(2)}) %collective-permute-start.18) | collective-permute-done | bytes 131104 | tf_op jit(solution)/shard_map/ppermute | solution.py:304
  78.9 3.6 %collective-permute-start.29 = (bf16[16,64,128]{2,1,0:T(8,128)(2,1)S(1)}, bf16[16,64,128]{2,1,0:T(8,128)(2,1)S(1)}, u32[]{:S(2)}, u32[]{:S(2)}) collective-permute-start(bf16[16,64,128]{2,1,0:T(8,128)(2,1)S(1)} %bitcast.108), channel_id=1, source_target_pairs={{0,6},{2,4},{4,2},{6,0},{8,14},{10,12},{12,10},{14,8},{16,22},{18,... | collective-permute-start | bytes 786440 | tf_op jit(solution)/shard_map/ppermute | solution.py:304
  82.5 5.2 %collective-permute-done.6 = bf16[8,64,128]{2,1,0:T(8,128)(2,1)S(1)} collective-permute-done((bf16[8,64,128]{2,1,0:T(8,128)(2,1)S(1)}, bf16[8,64,128]{2,1,0:T(8,128)(2,1)S(1)}, u32[]{:S(2)}, u32[]{:S(2)}) %collective-permute-start.6) | collective-permute-done | bytes 131104 | tf_op jit(solution)/shard_map/ppermute | solution.py:304
  92.6 3.4 %collective-permute-start.40 = (bf16[3,32,64,128]{3,2,1,0:T(8,128)(2,1)S(1)}, bf16[3,32,64,128]{3,2,1,0:T(8,128)(2,1)S(1)}, u32[]{:S(2)}, u32[]{:S(2)}) collective-permute-start(bf16[3,32,64,128]{3,2,1,0:T(8,128)(2,1)S(1)} %pad_maximum_fusion.1.refs_3_), channel_id=1, source_target_pairs={{0,24},{1,9},{2,26},{3,11},{4,28},{5,13},{6,30},{7,15},{8,0},{9,17... | collective-permute-start | bytes 4718600 | tf_op jit(solution)/shard_map/ppermute | solution.py:315
  97.9 4.2 %collective-permute-done.19.refs_4_ = bf16[3,8,64,128]{3,2,1,0:T(8,128)(2,1)S(1)} collective-permute-done((bf16[3,8,64,128]{3,2,1,0:T(8,128)(2,1)S(1)}, bf16[3,8,64,128]{3,2,1,0:T(8,128)(2,1)S(1)}, u32[]{:S(2)}, u32[]{:S(2)}) %collective-permute-start.19) | collective-permute-done | bytes 393248 | tf_op jit(solution)/shard_map/ppermute | solution.py:315
  102.1 19.2 %collective-permute-start.26 = (bf16[48,64,128]{2,1,0:T(8,128)(2,1)S(1)}, bf16[48,64,128]{2,1,0:T(8,128)(2,1)S(1)}, u32[]{:S(2)}, u32[]{:S(2)}) collective-permute-start(bf16[48,64,128]{2,1,0:T(8,128)(2,1)S(1)} %bitcast.61), channel_id=1, source_target_pairs={{0,24},{1,9},{2,26},{3,11},{4,28},{5,13},{6,30},{7,15},{8,0},{9,17... | collective-permute-start | bytes 2359304 | tf_op jit(solution)/shard_map/ppermute | solution.py:315
  125.8 4.6 %collective-permute-done.8 = bf16[3,32,8,2,128]{4,3,2,1,0:T(2,128)(2,1)S(1)} collective-permute-done((bf16[3,32,8,2,128]{4,3,2,1,0:T(2,128)(2,1)S(1)}, bf16[3,32,8,2,128]{4,3,2,1,0:T(2,128)(2,1)S(1)}, u32[]{:S(2)}, u32[]{:S(2)}) %collective-permute-start.8) | collective-permute-done | bytes 393248 | tf_op jit(solution)/shard_map/ppermute | solution.py:304
  130.6 60.5 %collective-permute-done.25.refs_1_ = bf16[48,64,128]{2,1,0:T(8,128)(2,1)S(1)} collective-permute-done((bf16[48,64,128]{2,1,0:T(8,128)(2,1)S(1)}, bf16[48,64,128]{2,1,0:T(8,128)(2,1)S(1)}, u32[]{:S(2)}, u32[]{:S(2)}) %collective-permute-start.25) | collective-permute-done | bytes 786464 | tf_op jit(solution)/shard_map/ppermute | solution.py:315
  192.2 9.2 %collective-permute-done.26.refs_2_ = bf16[48,64,128]{2,1,0:T(8,128)(2,1)S(1)} collective-permute-done((bf16[48,64,128]{2,1,0:T(8,128)(2,1)S(1)}, bf16[48,64,128]{2,1,0:T(8,128)(2,1)S(1)}, u32[]{:S(2)}, u32[]{:S(2)}) %collective-permute-start.26) | collective-permute-done | bytes 786464 | tf_op jit(solution)/shard_map/ppermute | solution.py:315
  201.5 3.5 %mix.5 = (bf16[32,32,2,128]{3,2,1,0:T(2,128)(2,1)S(1)}, bf16[32,32,2,128]{3,2,1,0:T(2,128)(2,1)S(1)}, bf16[32,32,2,128]{3,2,1,0:T(2,128)(2,1)S(1)}, bf16[32,32,2,128]{3,2,1,0:T(2,128)(2,1)S(1)}) custom-call(bf16[256,768]{1,0:T(8,128)(2,1)S(1)} %fusion.13.t_ref, bf16[48,64,128]{2,1,0:T(8,128)(2,1)S(1)} %bitcast.62, ...), custom_call_target="tpu_custom_call" | custom-call | flops 1610612736 | bytes 8781824 | tf_op jit(solution)/shard_map/mix/pallas_call | solution.py:131
  209.4 4.4 %collective-permute-start.31 = (bf16[3,16,64,128]{3,2,1,0:T(8,128)(2,1)S(1)}, bf16[3,16,64,128]{3,2,1,0:T(8,128)(2,1)S(1)}, u32[]{:S(2)}, u32[]{:S(2)}) collective-permute-start(bf16[3,16,64,128]{3,2,1,0:T(8,128)(2,1)S(1)} %pad_maximum_fusion.3.refs_3_), channel_id=1, source_target_pairs={{0,24},{1,9},{2,26},{3,11},{4,28},{5,13},{6,30},{7,15},{8,0},{9,17... | collective-permute-start | bytes 2359304 | tf_op jit(solution)/shard_map/ppermute | solution.py:315
  218.5 6.8 %collective-permute-done.42 = bf16[32,32,2,128]{3,2,1,0:T(2,128)(2,1)S(1)} collective-permute-done((bf16[32,32,2,128]{3,2,1,0:T(2,128)(2,1)S(1)}, bf16[32,32,2,128]{3,2,1,0:T(2,128)(2,1)S(1)}, u32[]{:S(2)}, u32[]{:S(2)}) %collective-permute-start.42) | collective-permute-done | bytes 524320 | tf_op jit(solution)/shard_map/ppermute | solution.py:304
  229.3 4.3 %collective-permute-done.23 = bf16[32,8,2,128]{3,2,1,0:T(2,128)(2,1)S(1)} collective-permute-done((bf16[32,8,2,128]{3,2,1,0:T(2,128)(2,1)S(1)}, bf16[32,8,2,128]{3,2,1,0:T(2,128)(2,1)S(1)}, u32[]{:S(2)}, u32[]{:S(2)}) %collective-permute-start.23) | collective-permute-done | bytes 131104 | tf_op jit(solution)/shard_map/ppermute | solution.py:304
  234.3 10.2 %collective-permute-done.31.refs_5_ = bf16[3,16,64,128]{3,2,1,0:T(8,128)(2,1)S(1)} collective-permute-done((bf16[3,16,64,128]{3,2,1,0:T(8,128)(2,1)S(1)}, bf16[3,16,64,128]{3,2,1,0:T(8,128)(2,1)S(1)}, u32[]{:S(2)}, u32[]{:S(2)}) %collective-permute-start.31) | collective-permute-done | bytes 786464 | tf_op jit(solution)/shard_map/ppermute | solution.py:315
  246.7 3.5 %collective-permute-done.11 = bf16[32,64,128]{2,1,0:T(8,128)(2,1)S(1)} collective-permute-done((bf16[32,64,128]{2,1,0:T(8,128)(2,1)S(1)}, bf16[32,64,128]{2,1,0:T(8,128)(2,1)S(1)}, u32[]{:S(2)}, u32[]{:S(2)}) %collective-permute-start.11) | collective-permute-done | bytes 524320 | tf_op jit(solution)/shard_map/ppermute | solution.py:315
  250.4 5.3 %collective-permute-done.12 = bf16[32,64,128]{2,1,0:T(8,128)(2,1)S(1)} collective-permute-done((bf16[32,64,128]{2,1,0:T(8,128)(2,1)S(1)}, bf16[32,64,128]{2,1,0:T(8,128)(2,1)S(1)}, u32[]{:S(2)}, u32[]{:S(2)}) %collective-permute-start.12) | collective-permute-done | bytes 524320 | tf_op jit(solution)/shard_map/ppermute | solution.py:315
  256.6 6.4 %collective-permute-done.34 = bf16[32,16,2,128]{3,2,1,0:T(2,128)(2,1)S(1)} collective-permute-done((bf16[32,16,2,128]{3,2,1,0:T(2,128)(2,1)S(1)}, bf16[32,16,2,128]{3,2,1,0:T(2,128)(2,1)S(1)}, u32[]{:S(2)}, u32[]{:S(2)}) %collective-permute-start.34) | collective-permute-done | bytes 262176 | tf_op jit(solution)/shard_map/ppermute | solution.py:304
  263.2 3.4 %copy-done.1 = bf16[32,128,2,512]{3,2,1,0:T(2,128)(2,1)S(1)} copy-done((bf16[32,128,2,512]{3,2,1,0:T(2,128)(2,1)S(1)}, bf16[32,128,2,512]{3,2,1,0:T(2,128)(2,1)}, u32[]{:S(2)}) %copy-start.1) | copy-done | bytes 8388632
  266.6 32.1 %arrange.1 = (bf16[32,256,512]{2,1,0:T(8,128)(2,1)S(1)}, bf16[32,256,256]{2,1,0:T(8,128)(2,1)S(1)}, bf16[32,256,128]{2,1,0:T(8,128)(2,1)S(1)}, bf16[32,256,128]{2,1,0:T(8,128)(2,1)S(1)}) custom-call(bf16[32,128,2,512]{3,2,1,0:T(2,128)(2,1)S(1)} %copy-done.1), custom_call_target="tpu_custom_call" | custom-call | flops 17179869184 | bytes 25165824 | tf_op jit(solution)/shard_map/arrange/pallas_call | solution.py:215
  298.6 3.4 %project.3.refs_3_ = f32[32,256,128]{2,1,0:T(8,128)S(1)} custom-call(bf16[32,256,512]{2,1,0:T(8,128)(2,1)S(1)} %get-tuple-element.71.refs_0_, bf16[32,256,128]{2,1,0:T(8,128)(2,1)S(1)} %pad_maximum_fusion.refs_1_, bf16[32,256,128]{2,1,0:T(8,128)(2,1)S(1)} %collective-permute-done.44.refs_2_), custom_call_target="tpu_custom_call" | custom-call | flops 1073741824 | bytes 16777216 | tf_op jit(solution)/shard_map/project/pallas_call | solution.py:248
  (181 shorter events, 78.1 us)
Async XLA Ops:
  0.8 26.4 %collective-permute-start = (s32[512]{0:T(512)S(1)}, s32[512]{0:T(512)S(1)}, u32[]{:S(2)}, u32[]{:S(2)}) collective-permute-start(s32[512]{0:T(512)S(1)} %dynamic_update_slice.5), channel_id=1, source_target_pairs={{0,8},{2,10},{4,12},{6,14},{8,16},{10,18},{12,20},{14,22},{16,24},... | collective-permute-start | bytes 6152 | tf_op jit(solution)/shard_map/ppermute | solution.py:307
  3.9 25.1 %collective-permute-start.1 = (s32[512]{0:T(512)S(1)}, s32[512]{0:T(512)S(1)}, u32[]{:S(2)}, u32[]{:S(2)}) collective-permute-start(s32[512]{0:T(512)S(1)} %dynamic_update_slice.5), channel_id=1, source_target_pairs={{0,16},{2,18},{4,20},{6,22},{8,24},{10,26},{12,28},{14,30},{16,0},... | collective-permute-start | bytes 6152 | tf_op jit(solution)/shard_map/ppermute | solution.py:307
  6.5 24.1 %collective-permute-start.2 = (s32[512]{0:T(512)S(1)}, s32[512]{0:T(512)S(1)}, u32[]{:S(2)}, u32[]{:S(2)}) collective-permute-start(s32[512]{0:T(512)S(1)} %dynamic_update_slice.5), channel_id=1, source_target_pairs={{0,24},{2,26},{4,28},{6,30},{8,0},{10,2},{12,4},{14,6},{16,8},{18,... | collective-permute-start | bytes 6152 | tf_op jit(solution)/shard_map/ppermute | solution.py:307
  8.8 44.2 %collective-permute-start.14 = (bf16[32,8,2,128]{3,2,1,0:T(2,128)(2,1)S(1)}, bf16[32,8,2,128]{3,2,1,0:T(2,128)(2,1)S(1)}, u32[]{:S(2)}, u32[]{:S(2)}) collective-permute-start(bf16[32,8,2,128]{3,2,1,0:T(2,128)(2,1)S(1)} %constant_dynamic-slice_fusion), channel_id=1, source_target_pairs={{0,8},{1,25},{2,10},{3,27},{4,12},{5,29},{6,14},{7,31},{8,16},{9,1... | collective-permute-start | bytes 393224 | tf_op jit(solution)/shard_map/ppermute | solution.py:315
  9.6 44.7 %collective-permute-start.15 = (bf16[32,8,2,128]{3,2,1,0:T(2,128)(2,1)S(1)}, bf16[32,8,2,128]{3,2,1,0:T(2,128)(2,1)S(1)}, u32[]{:S(2)}, u32[]{:S(2)}) collective-permute-start(bf16[32,8,2,128]{3,2,1,0:T(2,128)(2,1)S(1)} %constant_dynamic-slice_fusion), channel_id=1, source_target_pairs={{0,24},{1,9},{2,26},{3,11},{4,28},{5,13},{6,30},{7,15},{8,0},{9,17... | collective-permute-start | bytes 393224 | tf_op jit(solution)/shard_map/ppermute | solution.py:315
  27.3 45.4 %collective-permute-start.36 = (bf16[32,64,128]{2,1,0:T(8,128)(2,1)}, bf16[32,64,128]{2,1,0:T(8,128)(2,1)S(1)}, u32[]{:S(2)}, u32[]{:S(2)}) collective-permute-start(bf16[32,64,128]{2,1,0:T(8,128)(2,1)} %bitcast.107), channel_id=1, source_target_pairs={{0,2},{2,0},{4,6},{6,4},{8,10},{10,8},{12,14},{14,12},{16,18},{18,... | collective-permute-start | bytes 1572872 | tf_op jit(solution)/shard_map/ppermute | solution.py:304
  29.0 45.8 %collective-permute-start.37 = (bf16[32,64,128]{2,1,0:T(8,128)(2,1)}, bf16[32,64,128]{2,1,0:T(8,128)(2,1)}, u32[]{:S(2)}, u32[]{:S(2)}) collective-permute-start(bf16[32,64,128]{2,1,0:T(8,128)(2,1)} %bitcast.106), channel_id=1, source_target_pairs={{0,4},{2,6},{4,0},{6,2},{8,12},{10,14},{12,8},{14,10},{16,20},{18,... | collective-permute-start | bytes 1572872 | tf_op jit(solution)/shard_map/ppermute | solution.py:304
  50.6 25.7 %collective-permute-start.38 = (bf16[32,64,128]{2,1,0:T(8,128)(2,1)}, bf16[32,64,128]{2,1,0:T(8,128)(2,1)S(1)}, u32[]{:S(2)}, u32[]{:S(2)}) collective-permute-start(bf16[32,64,128]{2,1,0:T(8,128)(2,1)} %bitcast.105), channel_id=1, source_target_pairs={{0,6},{2,4},{4,2},{6,0},{8,14},{10,12},{12,10},{14,8},{16,22},{18,... | collective-permute-start | bytes 1572872 | tf_op jit(solution)/shard_map/ppermute | solution.py:304
  68.1 24.1 %collective-permute-start.27 = (bf16[16,64,128]{2,1,0:T(8,128)(2,1)S(1)}, bf16[16,64,128]{2,1,0:T(8,128)(2,1)S(1)}, u32[]{:S(2)}, u32[]{:S(2)}) collective-permute-start(bf16[16,64,128]{2,1,0:T(8,128)(2,1)S(1)} %bitcast.110), channel_id=1, source_target_pairs={{0,2},{2,0},{4,6},{6,4},{8,10},{10,8},{12,14},{14,12},{16,18},{18,... | collective-permute-start | bytes 786440 | tf_op jit(solution)/shard_map/ppermute | solution.py:304
  72.6 20.0 %collective-permute-start.28 = (bf16[16,64,128]{2,1,0:T(8,128)(2,1)S(1)}, bf16[16,64,128]{2,1,0:T(8,128)(2,1)S(1)}, u32[]{:S(2)}, u32[]{:S(2)}) collective-permute-start(bf16[16,64,128]{2,1,0:T(8,128)(2,1)S(1)} %bitcast.109), channel_id=1, source_target_pairs={{0,4},{2,6},{4,0},{6,2},{8,12},{10,14},{12,8},{14,10},{16,20},{18,... | collective-permute-start | bytes 786440 | tf_op jit(solution)/shard_map/ppermute | solution.py:304
  90.6 31.9 %collective-permute-start.20 = (bf16[3,8,64,128]{3,2,1,0:T(8,128)(2,1)S(1)}, bf16[3,8,64,128]{3,2,1,0:T(8,128)(2,1)S(1)}, u32[]{:S(2)}, u32[]{:S(2)}) collective-permute-start(bf16[3,8,64,128]{3,2,1,0:T(8,128)(2,1)S(1)} %pad_maximum_fusion.8.refs_3_), channel_id=1, source_target_pairs={{0,24},{1,9},{2,26},{3,11},{4,28},{5,13},{6,30},{7,15},{8,0},{9,17... | collective-permute-start | bytes 1179656 | tf_op jit(solution)/shard_map/ppermute | solution.py:315
  92.2 109.3 %collective-permute-start.39 = (bf16[3,32,64,128]{3,2,1,0:T(8,128)(2,1)S(1)}, bf16[3,32,64,128]{3,2,1,0:T(8,128)(2,1)S(1)}, u32[]{:S(2)}, u32[]{:S(2)}) collective-permute-start(bf16[3,32,64,128]{3,2,1,0:T(8,128)(2,1)S(1)} %pad_maximum_fusion.1.refs_3_), channel_id=1, source_target_pairs={{0,8},{1,25},{2,10},{3,27},{4,12},{5,29},{6,14},{7,31},{8,16},{9,1... | collective-permute-start | bytes 4718600 | tf_op jit(solution)/shard_map/ppermute | solution.py:315
  92.6 108.8 %collective-permute-start.40 = (bf16[3,32,64,128]{3,2,1,0:T(8,128)(2,1)S(1)}, bf16[3,32,64,128]{3,2,1,0:T(8,128)(2,1)S(1)}, u32[]{:S(2)}, u32[]{:S(2)}) collective-permute-start(bf16[3,32,64,128]{3,2,1,0:T(8,128)(2,1)S(1)} %pad_maximum_fusion.1.refs_3_), channel_id=1, source_target_pairs={{0,24},{1,9},{2,26},{3,11},{4,28},{5,13},{6,30},{7,15},{8,0},{9,17... | collective-permute-start | bytes 4718600 | tf_op jit(solution)/shard_map/ppermute | solution.py:315
  97.8 93.4 %collective-permute-start.25 = (bf16[48,64,128]{2,1,0:T(8,128)(2,1)S(1)}, bf16[48,64,128]{2,1,0:T(8,128)(2,1)S(1)}, u32[]{:S(2)}, u32[]{:S(2)}) collective-permute-start(bf16[48,64,128]{2,1,0:T(8,128)(2,1)S(1)} %bitcast.60), channel_id=1, source_target_pairs={{0,8},{1,25},{2,10},{3,27},{4,12},{5,29},{6,14},{7,31},{8,16},{9,1... | collective-permute-start | bytes 2359304 | tf_op jit(solution)/shard_map/ppermute | solution.py:315
  102.1 99.3 %collective-permute-start.26 = (bf16[48,64,128]{2,1,0:T(8,128)(2,1)S(1)}, bf16[48,64,128]{2,1,0:T(8,128)(2,1)S(1)}, u32[]{:S(2)}, u32[]{:S(2)}) collective-permute-start(bf16[48,64,128]{2,1,0:T(8,128)(2,1)S(1)} %bitcast.61), channel_id=1, source_target_pairs={{0,24},{1,9},{2,26},{3,11},{4,28},{5,13},{6,30},{7,15},{8,0},{9,17... | collective-permute-start | bytes 2359304 | tf_op jit(solution)/shard_map/ppermute | solution.py:315
  130.4 76.7 %collective-permute-start.9 = (bf16[3,32,8,2,128]{4,3,2,1,0:T(2,128)(2,1)S(1)}, bf16[3,32,8,2,128]{4,3,2,1,0:T(2,128)(2,1)S(1)}, u32[]{:S(2)}, u32[]{:S(2)}) collective-permute-start(bf16[3,32,8,2,128]{4,3,2,1,0:T(2,128)(2,1)S(1)} %get-tuple-element.53), channel_id=1, source_target_pairs={{0,4},{2,6},{4,0},{6,2},{8,12},{10,14},{12,8},{14,10},{16,20},{18,... | collective-permute-start | bytes 1179656 | tf_op jit(solution)/shard_map/ppermute | solution.py:304
  209.3 24.4 %collective-permute-start.30 = (bf16[3,16,64,128]{3,2,1,0:T(8,128)(2,1)S(1)}, bf16[3,16,64,128]{3,2,1,0:T(8,128)(2,1)S(1)}, u32[]{:S(2)}, u32[]{:S(2)}) collective-permute-start(bf16[3,16,64,128]{3,2,1,0:T(8,128)(2,1)S(1)} %pad_maximum_fusion.3.refs_3_), channel_id=1, source_target_pairs={{0,8},{1,25},{2,10},{3,27},{4,12},{5,29},{6,14},{7,31},{8,16},{9,1... | collective-permute-start | bytes 2359304 | tf_op jit(solution)/shard_map/ppermute | solution.py:315
  209.4 35.1 %collective-permute-start.31 = (bf16[3,16,64,128]{3,2,1,0:T(8,128)(2,1)S(1)}, bf16[3,16,64,128]{3,2,1,0:T(8,128)(2,1)S(1)}, u32[]{:S(2)}, u32[]{:S(2)}) collective-permute-start(bf16[3,16,64,128]{3,2,1,0:T(8,128)(2,1)S(1)} %pad_maximum_fusion.3.refs_3_), channel_id=1, source_target_pairs={{0,24},{1,9},{2,26},{3,11},{4,28},{5,13},{6,30},{7,15},{8,0},{9,17... | collective-permute-start | bytes 2359304 | tf_op jit(solution)/shard_map/ppermute | solution.py:315
  216.8 33.4 %collective-permute-start.11 = (bf16[32,64,128]{2,1,0:T(8,128)(2,1)S(1)}, bf16[32,64,128]{2,1,0:T(8,128)(2,1)S(1)}, u32[]{:S(2)}, u32[]{:S(2)}) collective-permute-start(bf16[32,64,128]{2,1,0:T(8,128)(2,1)S(1)} %pad_maximum_fusion.4), channel_id=1, source_target_pairs={{0,8},{1,25},{2,10},{3,27},{4,12},{5,29},{6,14},{7,31},{8,16},{9,1... | collective-permute-start | bytes 1572872 | tf_op jit(solution)/shard_map/ppermute | solution.py:315
  225.4 30.3 %collective-permute-start.12 = (bf16[32,64,128]{2,1,0:T(8,128)(2,1)S(1)}, bf16[32,64,128]{2,1,0:T(8,128)(2,1)S(1)}, u32[]{:S(2)}, u32[]{:S(2)}) collective-permute-start(bf16[32,64,128]{2,1,0:T(8,128)(2,1)S(1)} %pad_maximum_fusion.5), channel_id=1, source_target_pairs={{0,24},{1,9},{2,26},{3,11},{4,28},{5,13},{6,30},{7,15},{8,0},{9,17... | collective-permute-start | bytes 1572872 | tf_op jit(solution)/shard_map/ppermute | solution.py:315
  233.6 65.0 %collective-permute-start.44 = (bf16[32,256,128]{2,1,0:T(8,128)(2,1)S(1)}, bf16[32,256,128]{2,1,0:T(8,128)(2,1)S(1)}, u32[]{:S(2)}, u32[]{:S(2)}) collective-permute-start(bf16[32,256,128]{2,1,0:T(8,128)(2,1)S(1)} %pad_maximum_fusion.refs_1_), channel_id=1, source_target_pairs={{0,1},{1,0},{2,3},{3,2},{4,5},{5,4},{6,7},{7,6},{8,9},{9,8},{10,11... | collective-permute-start | bytes 6291464 | tf_op jit(solution)/shard_map/ppermute | solution.py:377
  233.7 70.8 %collective-permute-start.24 = (bf16[32,64,128]{2,1,0:T(8,128)(2,1)S(1)}, bf16[32,64,128]{2,1,0:T(8,128)(2,1)S(1)}, u32[]{:S(2)}, u32[]{:S(2)}) collective-permute-start(bf16[32,64,128]{2,1,0:T(8,128)(2,1)S(1)} %pad_maximum_fusion.6.refs_1_), channel_id=1, source_target_pairs={{0,1},{1,0},{2,3},{3,2},{4,5},{5,4},{6,7},{7,6},{8,9},{9,8},{10,11... | collective-permute-start | bytes 1572872 | tf_op jit(solution)/shard_map/ppermute | solution.py:377
  256.3 50.0 %collective-permute-start.13 = (bf16[32,64,128]{2,1,0:T(8,128)(2,1)S(1)}, bf16[32,64,128]{2,1,0:T(8,128)(2,1)S(1)}, u32[]{:S(2)}, u32[]{:S(2)}) collective-permute-start(bf16[32,64,128]{2,1,0:T(8,128)(2,1)S(1)} %add_convert_fusion.refs_0_), channel_id=1, source_target_pairs={{0,1},{1,0},{2,3},{3,2},{4,5},{5,4},{6,7},{7,6},{8,9},{9,8},{10,11... | collective-permute-start | bytes 1572872 | tf_op jit(solution)/shard_map/ppermute | solution.py:377
  263.1 39.0 %collective-permute-start.35 = (bf16[32,128,128]{2,1,0:T(8,128)(2,1)S(1)}, bf16[32,128,128]{2,1,0:T(8,128)(2,1)S(1)}, u32[]{:S(2)}, u32[]{:S(2)}) collective-permute-start(bf16[32,128,128]{2,1,0:T(8,128)(2,1)S(1)} %pad_maximum_fusion.2.refs_1_), channel_id=1, source_target_pairs={{0,1},{1,0},{2,3},{3,2},{4,5},{5,4},{6,7},{7,6},{8,9},{9,8},{10,11... | collective-permute-start | bytes 3145736 | tf_op jit(solution)/shard_map/ppermute | solution.py:377
  (51 other events, 730.0 us)

commit v6 on v4

--- a/solution.py
+++ b/solution.py
@@ -12,7 +12,7 @@
 H = 128
 UNITS = 8
 PARTS = (4, 2, 1, 1)
-VMEM_BYTES = 24 << 20
+VMEM_BYTES = 12 << 20
 
 
 def regroup(visibilities, picks, width, group):
@@ -173,24 +173,23 @@
     )(matrix, first, others)
 
 
-def arrange_basis(kl_basis, chunks, width, group, copies):
+def arrange_basis(kl_basis, blocks, width, group, copies):
     rows, modes, two, chans = kl_basis.shape
-    pieces = copies * group
-    widths = [2 * pieces * size for _, size in chunks]
+    widths = [2 * copies * len(partners) * size for _, size, partners in blocks]
 
     def kernel(kl_ref, *refs):
-        outs, picked = refs[: len(chunks)], refs[len(chunks) :]
+        outs, picked = refs[: len(blocks)], refs[len(blocks) :]
 
         @pl.when(pl.program_id(0) == 0)
         def _():
             place = lax.rem(lax.axis_index("ma"), group)
             core = lax.axis_index("ch")
-            for n, (offset, size) in enumerate(chunks):
+            for n, (offset, size, partners) in enumerate(blocks):
                 at = lax.broadcasted_iota(jnp.int32, (1, widths[n]), 1)
                 begin = jnp.zeros_like(at)
-                for piece in range(pieces):
-                    source = lax.rem(core + piece // group, copies)
-                    quarter = lax.bitwise_xor(place, piece % group)
+                for piece in range(copies * len(partners)):
+                    source = lax.rem(core + piece // len(partners), copies)
+                    quarter = lax.bitwise_xor(place, partners[piece % len(partners)])
                     first = source * group * width + quarter * width + offset - piece * size
                     begin = jnp.where(at >= 2 * piece * size, first, begin)
                 hit = begin + (at >> 1) == lax.broadcasted_iota(jnp.int32, (chans, widths[n]), 0)
@@ -259,7 +258,9 @@
 def project_last(basis, pieces, total):
     rows, out_rows, _ = basis.shape
     svd = pieces[0].shape[2]
-    block = math.gcd(rows, 4)
+    if pieces[0].shape[1] % 16 != 0:
+        pieces = [jnp.concatenate(pieces, axis=1)]
+    block = math.gcd(rows, 2)
 
     def kernel(a_ref, *refs):
         data_refs, t_ref, out, buf, sem = refs[: len(pieces)], *refs[len(pieces) :]
@@ -337,7 +338,9 @@
         flags = flags + swap(flags, bits)
         bits //= 2
     matrix = mixing_matrix(flags, place, rows, group, total)
-    bases = arrange_basis(kl_basis, chunks, width, group, copies)
+    half = group // 2
+    blocks = [(offset, size, range(group)) for offset, size in chunks]
+    bases = arrange_basis(kl_basis, blocks + [(begin, tail, range(half, group))], width, group, copies)
 
     def returned(pieces):
         back = [pieces[0]]
@@ -345,11 +348,19 @@
             back.append(swap(pieces[p], p))
         return [piece.reshape(piece.shape[:-3] + (2 * piece.shape[-3], svd)) for piece in back]
 
+    def spread(x):
+        pieces = [x]
+        for o in range(1, copies):
+            pieces.append(lax.ppermute(x, "ch", [(i, (i - o) % copies) for i in range(copies)]))
+        return pieces
+
     shares = mix_apart(matrix, away[-1], others[last])
     shares = returned(shares)
-    kept, rise, fall = [jnp.concatenate([share[side] for share in shares], axis=1) for side in range(3)]
+    kept, rise = [jnp.concatenate([share[side] for share in shares], axis=1) for side in range(2)]
+    fall, late = [jnp.concatenate([share[2] for share in part], axis=1) for part in (shares[:half], shares[half:])]
     rise = shift(rise, 1)
     fall = shift(fall, -1)
+    late = shift(late, -1)
 
     result = None
     for n, (offset, size) in enumerate(chunks):
@@ -361,12 +372,14 @@
             back = returned(mixed)
             joined = jnp.concatenate(back, axis=1)
         else:
-            wide = [share.astype(jnp.float32) for share in (kept, rise, fall)]
-            joined = (wide[0] + wide[1] + wide[2]).astype(jnp.bfloat16)
-        pieces = [joined]
-        for o in range(1, copies):
-            pieces.append(lax.ppermute(joined, "ch", [(i, (i - o) % copies) for i in range(copies)]))
-        result = (project_last if n == last else project)(bases[n], pieces, result)
+            wide = kept.astype(jnp.float32) + rise.astype(jnp.float32)
+            cut = fall.shape[1]
+            wide = jnp.concatenate([wide[:, :cut] + fall.astype(jnp.float32), wide[:, cut:]], axis=1)
+            joined = wide.astype(jnp.bfloat16)
+        pieces = spread(joined)
+        result = project(bases[n], pieces, result)
+    pieces = spread(late)
+    result = project_last(bases[-1], pieces, result)
     return result.reshape(rows, modes, 2, svd)
 
 

time: 317 us -> 305 us (0.962)
  waiting for transfers between devices: 177 us -> 155 us
  starting transfers between devices: 51.7 us -> 65.6 us
  other arithmetic: 18.8 us -> 12.3 us
  Pallas kernels: 57.3 us -> 63.7 us
  local copies, waits for them, and re-layouts: 7.7 us -> 4.3 us
    ppermute x26, waiting for transfers between devices: 65.3 us -> 41.7 us  [swap(): return lax.ppermute(x, 'ma', [(i, i ^ bits) for i in range(count)])]
    ppermute x15 -> x16, starting transfers between devices: 22.4 us -> 33 us  [shift(): lax.ppermute(x, 'ma', [(i, (i + by * group) % count) for i in range(count)])]
    pallas_call x1, Pallas kernels: 32.1 us -> 36.5 us  [arrange_basis(): pl.pallas_call(kernel, grid=(rows,), out_shape=[jax.ShapeDtypeStruct((row...]
    unnamed x60 -> x28, local copies, waits for them, and re-layouts: 3.49 us -> 0.06 us
    ppermute x15 -> x16, waiting for transfers between devices: 111 us -> 113 us  [shift(): lax.ppermute(x, 'ma', [(i, (i + by * group) % count) for i in range(count)])]
    pallas_call x3 -> x4, Pallas kernels: 7.61 us -> 9.51 us  [project(): pl.pallas_call(kernel, grid=(rows // step,), out_shape=out_shape, in_spec...]
  transfers between devices with their start and end apart: 45 -> 47, of which waited for: 16 -> 16; matrix products, arithmetic and copies ran while one was open for 8% -> 6% of each run, Pallas kernels for 18% -> 20%
where the time goes in v6:
time: 305 us
  waiting for transfers between devices  155 us (51%)
  starting transfers between devices  65.6 us (22%)
  Pallas kernels  63.7 us (21%)
  other arithmetic  12.3 us (4%)
  local copies, waits for them, and re-layouts  4.3 us (1%)
  matrix products  3.18 us (1%)
    ppermute x16, waiting for transfers between devices, shift(): lax.ppermute(x, 'ma', [(i, (i + by * group) % count) for i in range(count)])  113 us
    ppermute x26, waiting for transfers between devices, swap(): return lax.ppermute(x, 'ma', [(i, i ^ bits) for i in range(count)])  41.7 us
    pallas_call x1, Pallas kernels, arrange_basis(): pl.pallas_call(kernel, grid=(rows,), out_shape=[jax.ShapeDtypeStruct((row...  36.5 us
    ppermute x16, starting transfers between devices, shift(): lax.ppermute(x, 'ma', [(i, (i + by * group) % count) for i in range(count)])  33 us
    ppermute x26, starting transfers between devices, swap(): return lax.ppermute(x, 'ma', [(i, i ^ bits) for i in range(count)])  31.4 us
    sin x2, other arithmetic, waves(): return (jnp.cos(phases), jnp.sin(phases))  11 us
    pallas_call x4, Pallas kernels, project(): pl.pallas_call(kernel, grid=(rows // step,), out_shape=out_shape, in_spec...  9.51 us
    pallas_call x2, Pallas kernels, regroup(): pl.pallas_call(kernel, out_shape=[jax.ShapeDtypeStruct(shape, visibilitie...  7.07 us
  transfers between devices with their start and end apart: 47, of which 16 were waited for; matrix products, arithmetic and copies ran while one was open for 6% of the time, Pallas kernels for 20%

profile of v6, /device:TPU:0, one launch (start us, length us, event | category | flops | bytes accessed | tf_op | source)
XLA Modules:
  0.0 305.0 jit_solution(3053764229187818841)
XLA Ops:
  0.8 3.1 %collective-permute-start = (s32[512]{0:T(512)S(1)}, s32[512]{0:T(512)S(1)}, u32[]{:S(2)}, u32[]{:S(2)}) collective-permute-start(s32[512]{0:T(512)S(1)} %dynamic_update_slice.5), channel_id=1, source_target_pairs={{0,8},{2,10},{4,12},{6,14},{8,16},{10,18},{12,20},{14,22},{16,24},... | collective-permute-start | bytes 6152 | tf_op jit(solution)/shard_map/ppermute | solution.py:307
  3.9 2.6 collective-permute-start.1
  9.6 3.1 %collective-permute-start.17 = (bf16[32,8,2,128]{3,2,1,0:T(2,128)(2,1)S(1)}, bf16[32,8,2,128]{3,2,1,0:T(2,128)(2,1)S(1)}, u32[]{:S(2)}, u32[]{:S(2)}) collective-permute-start(bf16[32,8,2,128]{3,2,1,0:T(2,128)(2,1)S(1)} %constant_dynamic-slice_fusion), channel_id=1, source_target_pairs={{0,24},{2,26},{4,28},{6,30},{8,0},{10,2},{12,4},{14,6},{16,8},{18,... | collective-permute-start | bytes 393224 | tf_op jit(solution)/shard_map/ppermute | solution.py:307
  12.8 8.6 %fusion.29 = (f32[768,512]{1,0:T(8,128)S(1)}, f32[768,512]{1,0:T(8,128)}) fusion(s32[768]{0:T(1024)S(1)} %get-tuple-element.111, s32[768]{0:T(1024)S(1)} %get-tuple-element.112, pred[768]{0:T(1024)(128)(4,1)S(1)} %fusion.53, s32[768]{0:T(1024)S(1)} %get-tuple-element.108, s32[768]{0:T(1024)S(1)} %get-tuple-element.110, ...), kind=kLoop, calls=%fused_computation.87 | loop fusion | flops 19660800 | bytes 3173380 | tf_op jit(solution)/shard_map/sin | solution.py:85
  21.4 4.5 %regroup.2 = (bf16[16,32,2,128]{3,2,1,0:T(2,128)(2,1)}, bf16[16,32,2,128]{3,2,1,0:T(2,128)(2,1)}, bf16[16,32,2,128]{3,2,1,0:T(2,128)(2,1)}, bf16[8,32,2,128]{3,2...) custom-call(bf16[32,256,2,128]{3,2,1,0:T(2,128)(2,1)} %src.5), custom_call_target="tpu_custom_call" | custom-call | bytes 3407872 | tf_op jit(solution)/shard_map/regroup/pallas_call | solution.py:42
  29.8 3.2 %collective-permute-done.3 = s32[512]{0:T(512)S(1)} collective-permute-done((s32[512]{0:T(512)S(1)}, s32[512]{0:T(512)S(1)}, u32[]{:S(2)}, u32[]{:S(2)}) %collective-permute-start.3) | collective-permute-done | bytes 2080 | tf_op jit(solution)/shard_map/ppermute | solution.py:304
  35.9 2.5 regroup.3
  54.2 21.9 %collective-permute-done.6 = bf16[8,64,128]{2,1,0:T(8,128)(2,1)S(1)} collective-permute-done((bf16[8,64,128]{2,1,0:T(8,128)(2,1)S(1)}, bf16[8,64,128]{2,1,0:T(8,128)(2,1)S(1)}, u32[]{:S(2)}, u32[]{:S(2)}) %collective-permute-start.6) | collective-permute-done | bytes 131104 | tf_op jit(solution)/shard_map/ppermute | solution.py:304
  78.0 3.9 %collective-permute-start.22 = (bf16[3,8,64,128]{3,2,1,0:T(8,128)(2,1)S(1)}, bf16[3,8,64,128]{3,2,1,0:T(8,128)(2,1)S(1)}, u32[]{:S(2)}, u32[]{:S(2)}) collective-permute-start(bf16[3,8,64,128]{3,2,1,0:T(8,128)(2,1)S(1)} %pad_maximum_fusion.8.refs_3_), channel_id=1, source_target_pairs={{0,24},{2,26},{4,28},{6,30},{8,0},{10,2},{12,4},{14,6},{16,8},{18,... | collective-permute-start | bytes 1179656 | tf_op jit(solution)/shard_map/ppermute | solution.py:307
  84.4 3.8 %collective-permute-start.42 = (bf16[3,32,64,128]{3,2,1,0:T(8,128)(2,1)S(1)}, bf16[3,32,64,128]{3,2,1,0:T(8,128)(2,1)S(1)}, u32[]{:S(2)}, u32[]{:S(2)}) collective-permute-start(bf16[3,32,64,128]{3,2,1,0:T(8,128)(2,1)S(1)} %pad_maximum_fusion.1.refs_3_), channel_id=1, source_target_pairs={{0,24},{2,26},{4,28},{6,30},{8,0},{10,2},{12,4},{14,6},{16,8},{18,... | collective-permute-start | bytes 4718600 | tf_op jit(solution)/shard_map/ppermute | solution.py:307
  92.5 30.7 %collective-permute-done.22.refs_5_ = bf16[3,8,64,128]{3,2,1,0:T(8,128)(2,1)S(1)} collective-permute-done((bf16[3,8,64,128]{3,2,1,0:T(8,128)(2,1)S(1)}, bf16[3,8,64,128]{3,2,1,0:T(8,128)(2,1)S(1)}, u32[]{:S(2)}, u32[]{:S(2)}) %collective-permute-start.22) | collective-permute-done | bytes 393248 | tf_op jit(solution)/shard_map/ppermute | solution.py:307
  123.3 2.8 collective-permute-start.31
  127.3 3.3 %collective-permute-done.31 = bf16[16,64,128]{2,1,0:T(8,128)(2,1)S(1)} collective-permute-done((bf16[16,64,128]{2,1,0:T(8,128)(2,1)S(1)}, bf16[16,64,128]{2,1,0:T(8,128)(2,1)S(1)}, u32[]{:S(2)}, u32[]{:S(2)}) %collective-permute-start.31) | collective-permute-done | bytes 262176 | tf_op jit(solution)/shard_map/ppermute | solution.py:304
  130.6 3.8 %collective-permute-start.28 = (bf16[48,64,128]{2,1,0:T(8,128)(2,1)S(1)}, bf16[48,64,128]{2,1,0:T(8,128)(2,1)S(1)}, u32[]{:S(2)}, u32[]{:S(2)}) collective-permute-start(bf16[48,64,128]{2,1,0:T(8,128)(2,1)S(1)} %bitcast.61), channel_id=1, source_target_pairs={{0,24},{2,26},{4,28},{6,30},{8,0},{10,2},{12,4},{14,6},{16,8},{18,... | collective-permute-start | bytes 2359304 | tf_op jit(solution)/shard_map/ppermute | solution.py:307
  136.8 3.7 %collective-permute-done.23 = bf16[32,8,2,128]{3,2,1,0:T(2,128)(2,1)S(1)} collective-permute-done((bf16[32,8,2,128]{3,2,1,0:T(2,128)(2,1)S(1)}, bf16[32,8,2,128]{3,2,1,0:T(2,128)(2,1)S(1)}, u32[]{:S(2)}, u32[]{:S(2)}) %collective-permute-start.23) | collective-permute-done | bytes 131104 | tf_op jit(solution)/shard_map/ppermute | solution.py:304
  140.6 42.7 %collective-permute-done.27.refs_1_ = bf16[48,64,128]{2,1,0:T(8,128)(2,1)S(1)} collective-permute-done((bf16[48,64,128]{2,1,0:T(8,128)(2,1)S(1)}, bf16[48,64,128]{2,1,0:T(8,128)(2,1)S(1)}, u32[]{:S(2)}, u32[]{:S(2)}) %collective-permute-start.27) | collective-permute-done | bytes 786464 | tf_op jit(solution)/shard_map/ppermute | solution.py:307
  183.3 7.7 %collective-permute-start.32 = (bf16[3,16,64,128]{3,2,1,0:T(8,128)(2,1)S(1)}, bf16[3,16,64,128]{3,2,1,0:T(8,128)(2,1)S(1)}, u32[]{:S(2)}, u32[]{:S(2)}) collective-permute-start(bf16[3,16,64,128]{3,2,1,0:T(8,128)(2,1)S(1)} %pad_maximum_fusion.3.refs_3_), channel_id=1, source_target_pairs={{0,8},{2,10},{4,12},{6,14},{8,16},{10,18},{12,20},{14,22},{16,24},... | collective-permute-start | bytes 2359304 | tf_op jit(solution)/shard_map/ppermute | solution.py:307
  191.0 24.9 %collective-permute-done.28.refs_2_ = bf16[48,64,128]{2,1,0:T(8,128)(2,1)S(1)} collective-permute-done((bf16[48,64,128]{2,1,0:T(8,128)(2,1)S(1)}, bf16[48,64,128]{2,1,0:T(8,128)(2,1)S(1)}, u32[]{:S(2)}, u32[]{:S(2)}) %collective-permute-start.28) | collective-permute-done | bytes 786464 | tf_op jit(solution)/shard_map/ppermute | solution.py:307
  219.3 3.5 %mix.5 = (bf16[32,32,2,128]{3,2,1,0:T(2,128)(2,1)S(1)}, bf16[32,32,2,128]{3,2,1,0:T(2,128)(2,1)S(1)}, bf16[32,32,2,128]{3,2,1,0:T(2,128)(2,1)S(1)}, bf16[32,32,2,128]{3,2,1,0:T(2,128)(2,1)S(1)}) custom-call(bf16[256,768]{1,0:T(8,128)(2,1)S(1)} %fusion.13.t_ref, bf16[48,64,128]{2,1,0:T(8,128)(2,1)S(1)} %bitcast.62, ...), custom_call_target="tpu_custom_call" | custom-call | flops 1610612736 | bytes 8781824 | tf_op jit(solution)/shard_map/mix/pallas_call | solution.py:130
  228.3 12.5 %collective-permute-done.33.refs_5_ = bf16[3,16,64,128]{3,2,1,0:T(8,128)(2,1)S(1)} collective-permute-done((bf16[3,16,64,128]{3,2,1,0:T(8,128)(2,1)S(1)}, bf16[3,16,64,128]{3,2,1,0:T(8,128)(2,1)S(1)}, u32[]{:S(2)}, u32[]{:S(2)}) %collective-permute-start.33) | collective-permute-done | bytes 786464 | tf_op jit(solution)/shard_map/ppermute | solution.py:307
  240.8 2.9 collective-permute-start.10
  251.9 4.7 %collective-permute-done.35 = bf16[32,16,2,128]{3,2,1,0:T(2,128)(2,1)S(1)} collective-permute-done((bf16[32,16,2,128]{3,2,1,0:T(2,128)(2,1)S(1)}, bf16[32,16,2,128]{3,2,1,0:T(2,128)(2,1)S(1)}, u32[]{:S(2)}, u32[]{:S(2)}) %collective-permute-start.35) | collective-permute-done | bytes 262176 | tf_op jit(solution)/shard_map/ppermute | solution.py:304
  257.3 36.5 %arrange.1 = (bf16[32,256,512]{2,1,0:T(8,128)(2,1)S(1)}, bf16[32,256,256]{2,1,0:T(8,128)(2,1)S(1)}, bf16[32,256,128]{2,1,0:T(8,128)(2,1)S(1)}, bf16[32,256,128]{2,1,0:T(8,128)(2,1)S(1)}, bf16[32,256,64]{2,1,0:T(8,128)(2,1)S(1)}) custom-call(bf16[32,128,2,512]{3,2,1,0:T(2,128)(2,1)S(1)} %bitcast.71), custom_call_target="tpu_custom_call" | custom-call | flops 18253611008 | bytes 26214400 | tf_op jit(solution)/shard_map/arrange/pallas_call | solution.py:213
  293.8 3.5 %project.4.refs_3_ = f32[32,256,128]{2,1,0:T(8,128)S(1)} custom-call(bf16[32,256,512]{2,1,0:T(8,128)(2,1)S(1)} %get-tuple-element.73.refs_0_, bf16[32,256,128]{2,1,0:T(8,128)(2,1)S(1)} %pad_maximum_fusion.refs_1_, bf16[32,256,128]{2,1,0:T(8,128)(2,1)S(1)} %collective-permute-done.46.refs_2_), custom_call_target="tpu_custom_call" | custom-call | flops 1073741824 | bytes 16777216 | tf_op jit(solution)/shard_map/project/pallas_call | solution.py:246
  (159 shorter events, 63.8 us)
Async XLA Ops:
  0.8 25.1 %collective-permute-start = (s32[512]{0:T(512)S(1)}, s32[512]{0:T(512)S(1)}, u32[]{:S(2)}, u32[]{:S(2)}) collective-permute-start(s32[512]{0:T(512)S(1)} %dynamic_update_slice.5), channel_id=1, source_target_pairs={{0,8},{2,10},{4,12},{6,14},{8,16},{10,18},{12,20},{14,22},{16,24},... | collective-permute-start | bytes 6152 | tf_op jit(solution)/shard_map/ppermute | solution.py:307
  8.8 34.3 %collective-permute-start.16 = (bf16[32,8,2,128]{3,2,1,0:T(2,128)(2,1)S(1)}, bf16[32,8,2,128]{3,2,1,0:T(2,128)(2,1)S(1)}, u32[]{:S(2)}, u32[]{:S(2)}) collective-permute-start(bf16[32,8,2,128]{3,2,1,0:T(2,128)(2,1)S(1)} %constant_dynamic-slice_fusion), channel_id=1, source_target_pairs={{0,8},{2,10},{4,12},{6,14},{8,16},{10,18},{12,20},{14,22},{16,24},... | collective-permute-start | bytes 393224 | tf_op jit(solution)/shard_map/ppermute | solution.py:307
  9.6 35.7 %collective-permute-start.17 = (bf16[32,8,2,128]{3,2,1,0:T(2,128)(2,1)S(1)}, bf16[32,8,2,128]{3,2,1,0:T(2,128)(2,1)S(1)}, u32[]{:S(2)}, u32[]{:S(2)}) collective-permute-start(bf16[32,8,2,128]{3,2,1,0:T(2,128)(2,1)S(1)} %constant_dynamic-slice_fusion), channel_id=1, source_target_pairs={{0,24},{2,26},{4,28},{6,30},{8,0},{10,2},{12,4},{14,6},{16,8},{18,... | collective-permute-start | bytes 393224 | tf_op jit(solution)/shard_map/ppermute | solution.py:307
  45.2 31.5 %collective-permute-start.38 = (bf16[32,64,128]{2,1,0:T(8,128)(2,1)}, bf16[32,64,128]{2,1,0:T(8,128)(2,1)S(1)}, u32[]{:S(2)}, u32[]{:S(2)}) collective-permute-start(bf16[32,64,128]{2,1,0:T(8,128)(2,1)} %bitcast.110), channel_id=1, source_target_pairs={{0,2},{2,0},{4,6},{6,4},{8,10},{10,8},{12,14},{14,12},{16,18},{18,... | collective-permute-start | bytes 1572872 | tf_op jit(solution)/shard_map/ppermute | solution.py:304
  46.8 31.2 %collective-permute-start.39 = (bf16[32,64,128]{2,1,0:T(8,128)(2,1)S(1)}, bf16[32,64,128]{2,1,0:T(8,128)(2,1)S(1)}, u32[]{:S(2)}, u32[]{:S(2)}) collective-permute-start(bf16[32,64,128]{2,1,0:T(8,128)(2,1)S(1)} %bitcast.109), channel_id=1, source_target_pairs={{0,4},{2,6},{4,0},{6,2},{8,12},{10,14},{12,8},{14,10},{16,20},{18,... | collective-permute-start | bytes 1572872 | tf_op jit(solution)/shard_map/ppermute | solution.py:304
  47.3 34.6 %collective-permute-start.40 = (bf16[32,64,128]{2,1,0:T(8,128)(2,1)S(1)}, bf16[32,64,128]{2,1,0:T(8,128)(2,1)S(1)}, u32[]{:S(2)}, u32[]{:S(2)}) collective-permute-start(bf16[32,64,128]{2,1,0:T(8,128)(2,1)S(1)} %bitcast.108), channel_id=1, source_target_pairs={{0,6},{2,4},{4,2},{6,0},{8,14},{10,12},{12,10},{14,8},{16,22},{18,... | collective-permute-start | bytes 1572872 | tf_op jit(solution)/shard_map/ppermute | solution.py:304
  48.8 27.2 %collective-permute-start.6 = (bf16[8,64,128]{2,1,0:T(8,128)(2,1)S(1)}, bf16[8,64,128]{2,1,0:T(8,128)(2,1)S(1)}, u32[]{:S(2)}, u32[]{:S(2)}) collective-permute-start(bf16[8,64,128]{2,1,0:T(8,128)(2,1)S(1)} %bitcast.115), channel_id=1, source_target_pairs={{0,4},{2,6},{4,0},{6,2},{8,12},{10,14},{12,8},{14,10},{16,20},{18,... | collective-permute-start | bytes 393224 | tf_op jit(solution)/shard_map/ppermute | solution.py:304
  51.0 25.1 %collective-permute-start.7 = (bf16[8,64,128]{2,1,0:T(8,128)(2,1)S(1)}, bf16[8,64,128]{2,1,0:T(8,128)(2,1)S(1)}, u32[]{:S(2)}, u32[]{:S(2)}) collective-permute-start(bf16[8,64,128]{2,1,0:T(8,128)(2,1)S(1)} %bitcast.114), channel_id=1, source_target_pairs={{0,6},{2,4},{4,2},{6,0},{8,14},{10,12},{12,10},{14,8},{16,22},{18,... | collective-permute-start | bytes 393224 | tf_op jit(solution)/shard_map/ppermute | solution.py:304
  78.0 45.2 %collective-permute-start.22 = (bf16[3,8,64,128]{3,2,1,0:T(8,128)(2,1)S(1)}, bf16[3,8,64,128]{3,2,1,0:T(8,128)(2,1)S(1)}, u32[]{:S(2)}, u32[]{:S(2)}) collective-permute-start(bf16[3,8,64,128]{3,2,1,0:T(8,128)(2,1)S(1)} %pad_maximum_fusion.8.refs_3_), channel_id=1, source_target_pairs={{0,24},{2,26},{4,28},{6,30},{8,0},{10,2},{12,4},{14,6},{16,8},{18,... | collective-permute-start | bytes 1179656 | tf_op jit(solution)/shard_map/ppermute | solution.py:307
  81.9 44.9 %collective-permute-start.12 = (bf16[3,32,8,2,128]{4,3,2,1,0:T(2,128)(2,1)S(1)}, bf16[3,32,8,2,128]{4,3,2,1,0:T(2,128)(2,1)S(1)}, u32[]{:S(2)}, u32[]{:S(2)}) collective-permute-start(bf16[3,32,8,2,128]{4,3,2,1,0:T(2,128)(2,1)S(1)} %get-tuple-element.56), channel_id=1, source_target_pairs={{0,2},{2,0},{4,6},{6,4},{8,10},{10,8},{12,14},{14,12},{16,18},{18,... | collective-permute-start | bytes 1179656 | tf_op jit(solution)/shard_map/ppermute | solution.py:304
  84.4 131.6 %collective-permute-start.41 = (bf16[3,32,64,128]{3,2,1,0:T(8,128)(2,1)S(1)}, bf16[3,32,64,128]{3,2,1,0:T(8,128)(2,1)S(1)}, u32[]{:S(2)}, u32[]{:S(2)}) collective-permute-start(bf16[3,32,64,128]{3,2,1,0:T(8,128)(2,1)S(1)} %pad_maximum_fusion.1.refs_3_), channel_id=1, source_target_pairs={{0,8},{2,10},{4,12},{6,14},{8,16},{10,18},{12,20},{14,22},{16,24},... | collective-permute-start | bytes 4718600 | tf_op jit(solution)/shard_map/ppermute | solution.py:307
  84.4 133.2 %collective-permute-start.42 = (bf16[3,32,64,128]{3,2,1,0:T(8,128)(2,1)S(1)}, bf16[3,32,64,128]{3,2,1,0:T(8,128)(2,1)S(1)}, u32[]{:S(2)}, u32[]{:S(2)}) collective-permute-start(bf16[3,32,64,128]{3,2,1,0:T(8,128)(2,1)S(1)} %pad_maximum_fusion.1.refs_3_), channel_id=1, source_target_pairs={{0,24},{2,26},{4,28},{6,30},{8,0},{10,2},{12,4},{14,6},{16,8},{18,... | collective-permute-start | bytes 4718600 | tf_op jit(solution)/shard_map/ppermute | solution.py:307
  90.6 39.9 %collective-permute-start.8 = (bf16[3,32,8,2,128]{4,3,2,1,0:T(2,128)(2,1)S(1)}, bf16[3,32,8,2,128]{4,3,2,1,0:T(2,128)(2,1)S(1)}, u32[]{:S(2)}, u32[]{:S(2)}) collective-permute-start(bf16[3,32,8,2,128]{4,3,2,1,0:T(2,128)(2,1)S(1)} %get-tuple-element.52), channel_id=1, source_target_pairs={{0,4},{2,6},{4,0},{6,2},{8,12},{10,14},{12,8},{14,10},{16,20},{18,... | collective-permute-start | bytes 1179656 | tf_op jit(solution)/shard_map/ppermute | solution.py:304
  130.5 52.8 %collective-permute-start.27 = (bf16[48,64,128]{2,1,0:T(8,128)(2,1)S(1)}, bf16[48,64,128]{2,1,0:T(8,128)(2,1)S(1)}, u32[]{:S(2)}, u32[]{:S(2)}) collective-permute-start(bf16[48,64,128]{2,1,0:T(8,128)(2,1)S(1)} %bitcast.60), channel_id=1, source_target_pairs={{0,8},{2,10},{4,12},{6,14},{8,16},{10,18},{12,20},{14,22},{16,24},... | collective-permute-start | bytes 2359304 | tf_op jit(solution)/shard_map/ppermute | solution.py:307
  130.6 85.4 %collective-permute-start.28 = (bf16[48,64,128]{2,1,0:T(8,128)(2,1)S(1)}, bf16[48,64,128]{2,1,0:T(8,128)(2,1)S(1)}, u32[]{:S(2)}, u32[]{:S(2)}) collective-permute-start(bf16[48,64,128]{2,1,0:T(8,128)(2,1)S(1)} %bitcast.61), channel_id=1, source_target_pairs={{0,24},{2,26},{4,28},{6,30},{8,0},{10,2},{12,4},{14,6},{16,8},{18,... | collective-permute-start | bytes 2359304 | tf_op jit(solution)/shard_map/ppermute | solution.py:307
  140.5 85.4 %collective-permute-start.13 = (bf16[32,64,128]{2,1,0:T(8,128)(2,1)S(1)}, bf16[32,64,128]{2,1,0:T(8,128)(2,1)S(1)}, u32[]{:S(2)}, u32[]{:S(2)}) collective-permute-start(bf16[32,64,128]{2,1,0:T(8,128)(2,1)S(1)} %pad_maximum_fusion.4), channel_id=1, source_target_pairs={{0,8},{2,10},{4,12},{6,14},{8,16},{10,18},{12,20},{14,22},{16,24},... | collective-permute-start | bytes 1572872 | tf_op jit(solution)/shard_map/ppermute | solution.py:307
  183.3 45.0 %collective-permute-start.32 = (bf16[3,16,64,128]{3,2,1,0:T(8,128)(2,1)S(1)}, bf16[3,16,64,128]{3,2,1,0:T(8,128)(2,1)S(1)}, u32[]{:S(2)}, u32[]{:S(2)}) collective-permute-start(bf16[3,16,64,128]{3,2,1,0:T(8,128)(2,1)S(1)} %pad_maximum_fusion.3.refs_3_), channel_id=1, source_target_pairs={{0,8},{2,10},{4,12},{6,14},{8,16},{10,18},{12,20},{14,22},{16,24},... | collective-permute-start | bytes 2359304 | tf_op jit(solution)/shard_map/ppermute | solution.py:307
  216.0 24.8 %collective-permute-start.33 = (bf16[3,16,64,128]{3,2,1,0:T(8,128)(2,1)S(1)}, bf16[3,16,64,128]{3,2,1,0:T(8,128)(2,1)S(1)}, u32[]{:S(2)}, u32[]{:S(2)}) collective-permute-start(bf16[3,16,64,128]{3,2,1,0:T(8,128)(2,1)S(1)} %pad_maximum_fusion.3.refs_3_), channel_id=1, source_target_pairs={{0,24},{2,26},{4,28},{6,30},{8,0},{10,2},{12,4},{14,6},{16,8},{18,... | collective-permute-start | bytes 2359304 | tf_op jit(solution)/shard_map/ppermute | solution.py:307
  223.5 24.0 %collective-permute-start.44 = (bf16[32,32,2,128]{3,2,1,0:T(2,128)(2,1)S(1)}, bf16[32,32,2,128]{3,2,1,0:T(2,128)(2,1)S(1)}, u32[]{:S(2)}, u32[]{:S(2)}) collective-permute-start(bf16[32,32,2,128]{3,2,1,0:T(2,128)(2,1)S(1)} %get-tuple-element.79), channel_id=1, source_target_pairs={{0,4},{2,6},{4,0},{6,2},{8,12},{10,14},{12,8},{14,10},{16,20},{18,... | collective-permute-start | bytes 1572872 | tf_op jit(solution)/shard_map/ppermute | solution.py:304
  249.2 44.6 %collective-permute-start.46 = (bf16[32,256,128]{2,1,0:T(8,128)(2,1)S(1)}, bf16[32,256,128]{2,1,0:T(8,128)(2,1)S(1)}, u32[]{:S(2)}, u32[]{:S(2)}) collective-permute-start(bf16[32,256,128]{2,1,0:T(8,128)(2,1)S(1)} %pad_maximum_fusion.refs_1_), channel_id=1, source_target_pairs={{0,1},{1,0},{2,3},{3,2},{4,5},{5,4},{6,7},{7,6},{8,9},{9,8},{10,11... | collective-permute-start | bytes 6291464 | tf_op jit(solution)/shard_map/ppermute | solution.py:354
  249.4 50.3 %collective-permute-start.26 = (bf16[32,64,128]{2,1,0:T(8,128)(2,1)S(1)}, bf16[32,64,128]{2,1,0:T(8,128)(2,1)S(1)}, u32[]{:S(2)}, u32[]{:S(2)}) collective-permute-start(bf16[32,64,128]{2,1,0:T(8,128)(2,1)S(1)} %pad_maximum_fusion.6.refs_1_), channel_id=1, source_target_pairs={{0,1},{1,0},{2,3},{3,2},{4,5},{5,4},{6,7},{7,6},{8,9},{9,8},{10,11... | collective-permute-start | bytes 1572872 | tf_op jit(solution)/shard_map/ppermute | solution.py:354
  251.9 51.5 %collective-permute-start.11 = (bf16[32,32,128]{2,1,0:T(8,128)(2,1)S(1)}, bf16[32,32,128]{2,1,0:T(8,128)(2,1)S(1)}, u32[]{:S(2)}, u32[]{:S(2)}) collective-permute-start(bf16[32,32,128]{2,1,0:T(8,128)(2,1)S(1)} %collective-permute-done.10.refs_0_), channel_id=1, source_target_pairs={{0,1},{1,0},{2,3},{3,2},{4,5},{5,4},{6,7},{7,6},{8,9},{9,8},{10,11... | collective-permute-start | bytes 786440 | tf_op jit(solution)/shard_map/ppermute | solution.py:354
  256.6 45.0 %collective-permute-start.15 = (bf16[32,64,128]{2,1,0:T(8,128)(2,1)S(1)}, bf16[32,64,128]{2,1,0:T(8,128)(2,1)S(1)}, u32[]{:S(2)}, u32[]{:S(2)}) collective-permute-start(bf16[32,64,128]{2,1,0:T(8,128)(2,1)S(1)} %pad_maximum_fusion.5.refs_1_), channel_id=1, source_target_pairs={{0,1},{1,0},{2,3},{3,2},{4,5},{5,4},{6,7},{7,6},{8,9},{9,8},{10,11... | collective-permute-start | bytes 1572872 | tf_op jit(solution)/shard_map/ppermute | solution.py:354
  256.7 40.5 %collective-permute-start.37 = (bf16[32,128,128]{2,1,0:T(8,128)(2,1)S(1)}, bf16[32,128,128]{2,1,0:T(8,128)(2,1)S(1)}, u32[]{:S(2)}, u32[]{:S(2)}) collective-permute-start(bf16[32,128,128]{2,1,0:T(8,128)(2,1)S(1)} %pad_maximum_fusion.2.refs_1_), channel_id=1, source_target_pairs={{0,1},{1,0},{2,3},{3,2},{4,5},{5,4},{6,7},{7,6},{8,9},{9,8},{10,11... | collective-permute-start | bytes 3145736 | tf_op jit(solution)/shard_map/ppermute | solution.py:354
  (37 other events, 520.6 us)
